TPU v7x, 32 devices: a whole 2x2x4 slice. The times are simulated.
32 devices in a mesh: seq: 4 (over y, x), ctx: 4 (over z), fsdp: 2 (over core).
Axes of the slice: x: 2, y: 2, z: 4, core: 2. Of those that a mesh axis runs over, the one named last changes fastest.
Arguments:
- inputs: bfloat16 [8, 512, 2048], P(('seq', 'fsdp'), 'ctx'), may hold values from -6 to 6
- block_index: int32 [8, 4, 2], P(('seq', 'fsdp'), 'ctx'), may hold values from 0 to 7, as said below
- attention_gain: float32 [2048], replicated, may hold values from 0.1 to 1.9
- query_norm_gain: float32 [128], replicated, may hold values from 0.1 to 1.9
- key_gain: float32 [128], replicated, may hold values from 0.1 to 1.9
- feedforward_gain: float32 [2048], replicated, may hold values from 0.1 to 1.9
- attention_in: bfloat16 [2048, 4096], P(('seq', 'fsdp')), may hold values from -0.125 to 0.125
- attention_out: bfloat16 [2048, 2048], P(('seq', 'fsdp')), may hold values from -0.75 to 0.75
- gate_up: bfloat16 [2048, 12288], P(('seq', 'fsdp')), may hold values from -0.125 to 0.125
- down_weight: bfloat16 [2048, 6144], P(('seq', 'fsdp')), may hold values from -0.078125 to 0.078125
- grad_output: bfloat16 [8, 512, 2048], P(('seq', 'fsdp'), 'ctx'), may hold values from -6 to 6
Outputs:
- output: bfloat16 [8, 512, 2048], P(('seq', 'fsdp'), 'ctx')
- input_grad: bfloat16 [8, 512, 2048], P(('seq', 'fsdp'), 'ctx')
- attention_gain_grad: float32 [2048], replicated
- query_gain_grad: float32 [128], replicated
- key_gain_grad: float32 [128], replicated
- feedforward_gain_grad: float32 [2048], replicated
- attention_in_grad: float32 [2048, 4096], P(('seq', 'ctx', 'fsdp'))
- attention_out_grad: float32 [2048, 2048], P(('seq', 'ctx', 'fsdp'))
- gate_up_grad: float32 [2048, 12288], P(('seq', 'ctx', 'fsdp'))
- down_grad: float32 [2048, 6144], P(('seq', 'ctx', 'fsdp'))
Inputs may be any that keep to these rules, and one draw needn't show every extreme that they name: For each sequence s, block_index[s, c, 0] over c takes each of 0 to 3 once, and block_index[s, c, 1] = 7 - block_index[s, c, 0].
All inputs are finite; a program needn't handle non-finite values.
Results may differ from a plain program's by a relative error of at most 0.018.
Values may be sent and summed in bfloat16 or wider, within the bound.
No kernel may reach another device: no remote copies, remote signals or barrier semaphores. Data moves between devices by JAX's collectives and lax.ppermute only.
A program may use at most 832 MiB of HBM per device.

v0:
```python
import jax
import jax.numpy as jnp
from jax import lax
from jax.sharding import PartitionSpec as P

D = 2048
QUERY_HEADS = 16
KEY_VALUE_HEADS = 8
HEAD_SIZE = 128
FF = 6144


EPS = 1e-06
ROPE_BASE = 1000000.0
MASK_FLOOR = -1e30


def rms_scale(values):
    return lax.rsqrt(jnp.mean(values * values, axis=-1, keepdims=True) + EPS)


def rms_back(grad_normed, normed_hat, scale, gain):
    grad_hat = grad_normed * gain
    inner = jnp.mean(grad_hat * normed_hat, axis=-1, keepdims=True)
    return scale * (grad_hat - normed_hat * inner)


def rope_tables(token_positions):
    half = HEAD_SIZE // 2
    rates = jnp.power(
        jnp.float32(ROPE_BASE), jnp.arange(half, dtype=jnp.float32) * (-2.0 / HEAD_SIZE)
    )
    angles = token_positions.astype(jnp.float32)[:, None] * rates[None, :]
    angles = jnp.concatenate([angles, angles], axis=1)
    return (jnp.cos(angles), jnp.sin(angles))


def apply_rotation(values, cosine_table, sine_table):
    half = values.shape[-1] // 2
    turned = jnp.concatenate([-values[..., half:], values[..., :half]], axis=-1)
    return values * cosine_table[:, None, :] + turned * sine_table[:, None, :]


def rotate_back(grads, cosine_table, sine_table):
    half = grads.shape[-1] // 2
    scaled = grads * sine_table[:, None, :]
    turned = jnp.concatenate([scaled[..., half:], -scaled[..., :half]], axis=-1)
    return grads * cosine_table[:, None, :] + turned


def add_rows(left, piece):
    return jnp.dot(left, piece, preferred_element_type=jnp.float32)


def right_columns(left, piece):
    return lax.dot_general(
        left, piece, (((1,), (1,)), ((), ())), preferred_element_type=jnp.float32
    )


def transposed(left, right):
    return lax.dot_general(
        left, right, (((0,), (0,)), ((), ())), preferred_element_type=jnp.float32
    )


def local(
    inputs,
    block_index,
    attention_gain,
    query_norm_gain,
    key_gain,
    feedforward_gain,
    attention_in,
    attention_out,
    gate_up,
    down_weight,
    grad_output,
):
    rows = inputs[0].astype(jnp.float32)
    row_tally = rows.shape[0]
    half_rows = row_tally // 2
    head_group = QUERY_HEADS // KEY_VALUE_HEADS
    query_width = QUERY_HEADS * HEAD_SIZE
    key_width = KEY_VALUE_HEADS * HEAD_SIZE
    scale = HEAD_SIZE ** (-0.5)
    steps_along = jnp.arange(half_rows, dtype=jnp.int32)
    token_positions = (block_index[0, 0][:, None] * half_rows + steps_along[None, :]).reshape(-1)
    first_scale = rms_scale(rows)
    first_hat = rows * first_scale
    first_normed = (first_hat * attention_gain).astype(jnp.bfloat16)
    projected_rows = add_rows(
        first_normed, lax.all_gather(attention_in, ("seq", "fsdp"), axis=0, tiled=True)
    )
    query = projected_rows[:, :query_width].reshape(row_tally, QUERY_HEADS, HEAD_SIZE)
    key_rows_all = projected_rows[:, query_width : query_width + key_width].reshape(
        row_tally, KEY_VALUE_HEADS, HEAD_SIZE
    )
    value_rows = (
        projected_rows[:, query_width + key_width :]
        .astype(jnp.bfloat16)
        .reshape(1, row_tally, key_width)
    )
    query_scale = rms_scale(query)
    query_normalized = query * query_scale
    key_scale = rms_scale(key_rows_all)
    key_hat = key_rows_all * key_scale
    cosine_table, sine_table = rope_tables(token_positions)
    rotary_query = (
        apply_rotation(query_normalized * query_norm_gain, cosine_table, sine_table)
        .astype(jnp.bfloat16)
        .reshape(row_tally, KEY_VALUE_HEADS, head_group, HEAD_SIZE)
    )
    key_rows = (
        apply_rotation(key_hat * key_gain, cosine_table, sine_table)
        .astype(jnp.bfloat16)
        .reshape(1, row_tally, key_width)
    )

    def split_piece(piece):
        key_portion, value_portion, index_part = piece
        shard_list = index_part.shape[1]
        blocks_key = key_portion.reshape(shard_list, row_tally, KEY_VALUE_HEADS, HEAD_SIZE)
        blocks_value = value_portion.reshape(shard_list, row_tally, KEY_VALUE_HEADS, HEAD_SIZE)
        key_positions = (
            index_part[0][:, :, None] * half_rows + steps_along[None, None, :]
        ).reshape(shard_list, row_tally)
        return (blocks_key, blocks_value, key_positions)

    def block_scores(key_block, key_positions):
        scores = (
            jnp.einsum(
                "qhgd,khd->hgqk", rotary_query, key_block, preferred_element_type=jnp.float32
            )
            * scale
        )
        allowed = key_positions[None, :] <= token_positions[:, None]
        return (jnp.where(allowed, scores, MASK_FLOOR), allowed)

    def across_keys(fold_step, state):
        return fold_step(
            state,
            (
                lax.all_gather(key_rows, "ctx", axis=1, tiled=True),
                lax.all_gather(value_rows, "ctx", axis=1, tiled=True),
                lax.all_gather(block_index, "ctx", axis=1, tiled=True),
            ),
            jnp.int32(0),
        )

    def softmax_sums(carry, piece, start):
        blocks_key, blocks_value, key_positions = split_piece(piece)

        def softmax_step(state, block):
            peak, total = state
            scores, allowed = block_scores(block[0], block[1])
            fresh = jnp.maximum(peak, jnp.max(scores, axis=-1))
            total = total * jnp.exp(peak - fresh) + jnp.sum(
                jnp.where(allowed, jnp.exp(scores - fresh[..., None]), 0.0), axis=-1
            )
            return ((fresh, total), None)

        carry, unused = lax.scan(softmax_step, carry, (blocks_key, key_positions))
        return carry

    initial_maximum = jnp.full((KEY_VALUE_HEADS, head_group, row_tally), MASK_FLOOR, jnp.float32)
    peak, total = across_keys(
        softmax_sums,
        (initial_maximum, jnp.zeros((KEY_VALUE_HEADS, head_group, row_tally), jnp.float32)),
    )
    total_logarithm = peak + jnp.log(total)

    def weighted_total(carry, piece, start):
        blocks_key, blocks_value, key_positions = split_piece(piece)

        def weighted_step(state, block):
            scores, allowed = block_scores(block[0], block[2])
            weights = jnp.where(allowed, jnp.exp(scores - total_logarithm[..., None]), 0.0).astype(
                jnp.bfloat16
            )
            return (
                state
                + jnp.einsum(
                    "hgqk,khd->qhgd", weights, block[1], preferred_element_type=jnp.float32
                ),
                None,
            )

        carry, unused = lax.scan(weighted_step, carry, (blocks_key, blocks_value, key_positions))
        return carry

    summed_rows = across_keys(
        weighted_total, jnp.zeros((row_tally, KEY_VALUE_HEADS, head_group, HEAD_SIZE), jnp.float32)
    )
    attended_rows = summed_rows.astype(jnp.bfloat16).reshape(row_tally, query_width)
    middle = rows + right_columns(
        attended_rows, lax.all_gather(attention_out, ("seq", "fsdp"), axis=0, tiled=True)
    )
    second_scale = rms_scale(middle)
    second_hat = middle * second_scale
    second_normed = (second_hat * feedforward_gain).astype(jnp.bfloat16)
    gate_values = add_rows(
        second_normed, lax.all_gather(gate_up, ("seq", "fsdp"), axis=0, tiled=True)
    )
    gate = gate_values[:, :FF]
    upward = gate_values[:, FF:]
    hidden = (jax.nn.silu(gate) * upward).astype(jnp.bfloat16)
    result = middle + right_columns(
        hidden, lax.all_gather(down_weight, ("seq", "fsdp"), axis=0, tiled=True)
    )
    output = result.astype(jnp.bfloat16).reshape(1, row_tally, D)
    grad_rows = grad_output[0]
    grad_hidden = add_rows(
        grad_rows, lax.all_gather(down_weight, ("seq", "fsdp"), axis=0, tiled=True)
    )
    sigmoid_gate = jax.nn.sigmoid(gate)
    grad_gate = grad_hidden * upward * sigmoid_gate * (1.0 + gate * (1.0 - sigmoid_gate))
    grad_upward = grad_hidden * jax.nn.silu(gate)
    grad_gate_up = jnp.concatenate([grad_gate, grad_upward], axis=1).astype(jnp.bfloat16)
    grad_second = right_columns(
        grad_gate_up, lax.all_gather(gate_up, ("seq", "fsdp"), axis=0, tiled=True)
    )
    feedforward_part = jnp.sum(grad_second * second_hat, axis=0)
    grad_middle = grad_rows.astype(jnp.float32) + rms_back(
        grad_second, second_hat, second_scale, feedforward_gain
    )
    grad_middle_short = grad_middle.astype(jnp.bfloat16)
    width_in = attention_in.shape[1]
    width_out = attention_out.shape[1]
    attended_gradient = add_rows(
        grad_middle_short, lax.all_gather(attention_out, ("seq", "fsdp"), axis=0, tiled=True)
    ).astype(jnp.bfloat16)
    head_gradients = attended_gradient.reshape(row_tally, KEY_VALUE_HEADS, head_group, HEAD_SIZE)
    heads_attended = attended_rows.reshape(row_tally, KEY_VALUE_HEADS, head_group, HEAD_SIZE)
    delta_rows = jnp.transpose(
        jnp.sum(head_gradients.astype(jnp.float32) * heads_attended.astype(jnp.float32), axis=-1),
        (1, 2, 0),
    )

    def attention_back(carry, piece, start):
        blocks_key, blocks_value, key_positions = split_piece(piece)
        shard_list = blocks_key.shape[0]

        def attention_step(state, block):
            query_acc, key_acc, value_acc = state
            key_block, value_block, key_pos, shard = block
            scores, allowed = block_scores(key_block, key_pos)
            probs = jnp.where(allowed, jnp.exp(scores - total_logarithm[..., None]), 0.0)
            weights = probs.astype(jnp.bfloat16)
            grad_probs = jnp.einsum(
                "qhgd,khd->hgqk", head_gradients, value_block, preferred_element_type=jnp.float32
            )
            grad_scores = (probs * (grad_probs - delta_rows[..., None])).astype(jnp.bfloat16)
            query_acc = query_acc + jnp.einsum(
                "hgqk,khd->qhgd", grad_scores, key_block, preferred_element_type=jnp.float32
            )
            offset = shard * row_tally
            key_term = jnp.einsum(
                "hgqk,qhgd->khd", grad_scores, rotary_query, preferred_element_type=jnp.float32
            )
            value_term = jnp.einsum(
                "hgqk,qhgd->khd", weights, head_gradients, preferred_element_type=jnp.float32
            )
            key_acc = lax.dynamic_update_slice_in_dim(
                key_acc,
                lax.dynamic_slice_in_dim(key_acc, offset, row_tally, 0) + key_term,
                offset,
                0,
            )
            value_acc = lax.dynamic_update_slice_in_dim(
                value_acc,
                lax.dynamic_slice_in_dim(value_acc, offset, row_tally, 0) + value_term,
                offset,
                0,
            )
            return ((query_acc, key_acc, value_acc), None)

        carry, unused = lax.scan(
            attention_step,
            carry,
            (blocks_key, blocks_value, key_positions, jnp.arange(shard_list, dtype=jnp.int32)),
        )
        return carry

    rows_sequence = row_tally * lax.axis_size("ctx")
    back_start = (
        jnp.zeros((row_tally, KEY_VALUE_HEADS, head_group, HEAD_SIZE), jnp.float32),
        jnp.zeros((rows_sequence, KEY_VALUE_HEADS, HEAD_SIZE), jnp.float32),
        jnp.zeros((rows_sequence, KEY_VALUE_HEADS, HEAD_SIZE), jnp.float32),
    )
    query_acc, key_acc, value_acc = across_keys(attention_back, back_start)
    key_sum, value_sum = (
        lax.psum_scatter(
            key_acc.astype(jnp.bfloat16), "ctx", scatter_dimension=0, tiled=True
        ).astype(jnp.float32),
        lax.psum_scatter(
            value_acc.astype(jnp.bfloat16), "ctx", scatter_dimension=0, tiled=True
        ).astype(jnp.float32),
    )
    unrotated_query = rotate_back(
        query_acc.reshape(row_tally, QUERY_HEADS, HEAD_SIZE) * scale, cosine_table, sine_table
    )
    unrotated_key = rotate_back(key_sum * scale, cosine_table, sine_table)
    query_part = jnp.sum(unrotated_query * query_normalized, axis=(0, 1))
    key_portion = jnp.sum(unrotated_key * key_hat, axis=(0, 1))
    grad_query = rms_back(unrotated_query, query_normalized, query_scale, query_norm_gain)
    grad_key = rms_back(unrotated_key, key_hat, key_scale, key_gain)
    grad_projected = jnp.concatenate(
        [
            grad_query.reshape(row_tally, query_width),
            grad_key.reshape(row_tally, key_width),
            value_sum.reshape(row_tally, key_width),
        ],
        axis=1,
    ).astype(jnp.bfloat16)
    grad_first = right_columns(
        grad_projected, lax.all_gather(attention_in, ("seq", "fsdp"), axis=0, tiled=True)
    )
    attention_part = jnp.sum(grad_first * first_hat, axis=0)
    input_grad = (
        grad_middle + rms_back(grad_first, first_hat, first_scale, attention_gain)
    ).astype(jnp.bfloat16)
    input_grad = input_grad.reshape(1, row_tally, D)
    combined = lax.psum_scatter(
        jnp.concatenate(
            [
                jnp.concatenate(
                    [
                        transposed(first_normed, grad_projected),
                        transposed(grad_middle_short, attended_rows),
                    ],
                    axis=1,
                ),
                jnp.concatenate(
                    [transposed(second_normed, grad_gate_up), transposed(grad_rows, hidden)], axis=1
                ),
            ],
            axis=1,
        ),
        ("seq", "ctx", "fsdp"),
        scatter_dimension=0,
        tiled=True,
    )
    attention_sum = combined[:, : width_in + width_out]
    feedforward_sum = combined[:, width_in + width_out :]
    gain_sums = lax.psum(
        (attention_part, query_part, key_portion, feedforward_part), ("seq", "ctx", "fsdp")
    )
    return (
        output,
        input_grad,
        gain_sums[0],
        gain_sums[1],
        gain_sums[2],
        gain_sums[3],
        attention_sum[:, :width_in],
        attention_sum[:, width_in:],
        feedforward_sum[:, : 2 * FF],
        feedforward_sum[:, 2 * FF :],
    )


def solution(mesh):
    in_specs = (
        P(("seq", "fsdp"), "ctx", None),
        P(("seq", "fsdp"), "ctx", None),
        P(),
        P(),
        P(),
        P(),
        P(("seq", "fsdp"), None),
        P(("seq", "fsdp"), None),
        P(("seq", "fsdp"), None),
        P(("seq", "fsdp"), None),
        P(("seq", "fsdp"), "ctx", None),
    )
    out_specs = (
        P(("seq", "fsdp"), "ctx", None),
        P(("seq", "fsdp"), "ctx", None),
        P(),
        P(),
        P(),
        P(),
        P(("seq", "ctx", "fsdp"), None),
        P(("seq", "ctx", "fsdp"), None),
        P(("seq", "ctx", "fsdp"), None),
        P(("seq", "ctx", "fsdp"), None),
    )
    return jax.shard_map(local, mesh=mesh, in_specs=in_specs, out_specs=out_specs, check_vma=False)
```

profile of v0, /device:TPU:0, one launch (start us, length us, event | category | flops | bytes accessed | tf_op | source)
XLA Modules:
  0.0 2544.8 jit_solution(16096200539208161568)
XLA Ops:
  10.2 92.1 %all-gather.9.cloned.1.call-done = bf16[2048,4096]{1,0:T(8,128)(2,1)} async-done(((bf16[256,4096]{1,0:T(8,128)(2,1)}), bf16[2048,4096]{1,0:T(8,128)(2,1)}) %all-gather.9.cloned.1.call-update) | async-done | bytes 16777232 | tf_op jit(solution)/shard_map/all_gather | solution.py:93
  102.4 8.2 fusion.97
  116.1 11.1 all_gather.32
  141.1 28.0 %all-gather.19.cloned.1.call-done = bf16[512,1024]{1,0:T(8,128)(2,1)} async-done(((bf16[128,1024]{1,0:T(8,128)(2,1)}), bf16[512,1024]{1,0:T(8,128)(2,1)}) %all-gather.19.cloned.1.call-update) | async-done | bytes 1048592 | tf_op jit(solution)/shard_map/all_gather | solution.py:144
  171.9 7.8 while.39
  179.8 13.3 while.40
  195.5 29.1 %all-gather.11.cloned.1.call-done = bf16[2048,2048]{1,0:T(8,128)(2,1)} async-done(((bf16[256,2048]{1,0:T(8,128)(2,1)}), bf16[2048,2048]{1,0:T(8,128)(2,1)}) %all-gather.11.cloned.1.call-update) | async-done | bytes 8388624 | tf_op jit(solution)/shard_map/all_gather | solution.py:197
  224.6 6.5 multiply_reduce_fusion.5
  231.2 227.3 %all-gather.13.cloned.1.call-done = bf16[2048,12288]{1,0:T(8,128)(2,1)} async-done(((bf16[256,12288]{1,0:T(8,128)(2,1)}), bf16[2048,12288]{1,0:T(8,128)(2,1)}) %all-gather.13.cloned.1.call-update) | async-done | bytes 50331664 | tf_op jit(solution)/shard_map/all_gather | solution.py:203
  458.4 23.5 fusion.105
  481.9 103.5 %all-gather.15.cloned.1.call-done = bf16[2048,6144]{1,0:T(8,128)(2,1)} async-done(((bf16[256,6144]{1,0:T(8,128)(2,1)}), bf16[2048,6144]{1,0:T(8,128)(2,1)}) %all-gather.15.cloned.1.call-update) | async-done | bytes 25165840 | tf_op jit(solution)/shard_map/all_gather | solution.py:209
  585.4 14.9 multiply_convert_fusion.1
  600.3 24.7 multiply_reduce_fusion
  641.1 39.6 %while.41 = (s32[]{:T(128)}, f32[128,8,2,128]{0,3,2,1:T(8,128)S(1)}, f32[512,8,128]{2,0,1:T(8,128)}, f32[512,8,128]{2,0,1:T(8,128)}, bf16[4,128,8,128]{3,1,2,0:T...) while((s32[]{:T(128)}, ...), condition=%wide.region_13.14_spmd.clone, body=%wide.region_12.13_spmd.clone.sunk | while | flops 338444416 | bytes 12373769 | solution.py:278
  688.9 36.4 %fusion.60 = f32[2048,12288]{1,0:T(8,128)} fusion(bf16[128,6144]{1,0:T(8,128)(2,1)} %get-tuple-element.479, bf16[128,6144]{1,0:T(8,128)(2,1)} %get-tuple-element.478, f32[128,2048]{1,0:T(8,128)S(1)} %get-tuple-element.496, f32[2048]{0:T(1024)S(1)} %copy-done.22, f32[128]{0:T(128)S(1)} %add_rsqrt_fusion.2), kind=kOutput, calls=%fused_computation.87 | convolution fusion | flops 6449528832 | bytes 104866304 | tf_op jit(solution)/shard_map/dot_general | solution.py:62
  734.5 21.2 convolution_bitcast_fusion.5
  761.4 8.1 fusion.93
  773.3 13.8 reduce-scatter.6.cloned.1.call-done
  788.1 13.5 fusion.89
  801.6 131.9 %pad_maximum_fusion = f32[2048,24576]{1,0:T(8,128)} fusion(f32[2048,6144]{1,0:T(8,128)} %convolution_bitcast_fusion.5, f32[2048,12288]{1,0:T(8,128)} %fusion.60, f32[2048,2048]{1,0:T(8,128)} %fusion.93, f32[2048,4096]{1,0:T(8,128)} %fusion.89), kind=kLoop, calls=%fused_computation.74 | loop fusion | flops 150994944 | bytes 402653184 | tf_op jit(solution)/shard_map/concatenate | solution.py:325
  935.2 17.2 fusion.59
  952.5 15.4 fusion.72
  967.9 37.8 %all-reduce = (f32[2048]{0:T(1024)}, f32[128]{0:T(128)}, f32[128]{0:T(128)}, f32[2048]{0:T(1024)}) all-reduce(f32[2048]{0:T(1024)S(1)} %get-tuple-element.411, f32[128]{0:T(128)S(1)} %copy-done.40, f32[128]{0:T(128)S(1)} %copy-done.41, f32[2048]{0:T(1024)S(1)} %copy-done.33), channel_id=1, replica_groups=mesh['seq'=4,'ctx'=4,'fsdp'=2] {'seq','ctx','fsdp'}, use_global_device_ids=true, to_apply=%region_20.21 | all-reduce | flops 4352 | bytes 34816 | tf_op jit(solution)/shard_map/psum | solution.py:346
  1006.9 1520.4 %reduce-scatter.8.cloned.1.call-done = f32[64,24576]{1,0:T(8,128)} async-done(((f32[2048,24576]{1,0:T(8,128)}), f32[64,24576]{1,0:T(8,128)}) %reduce-scatter.8.cloned.1.call-update) | async-done | bytes 6291472 | tf_op jit(solution)/shard_map/reduce_scatter | solution.py:324
  (305 shorter events, 141.6 us)
Async XLA Ops:
  7.2 95.2 %copy-start.7 = (bf16[1,128,2048]{2,1,0:T(8,128)(2,1)S(1)}, bf16[1,128,2048]{2,1,0:T(8,128)(2,1)}, u32[]{:S(2)}) copy-start(bf16[1,128,2048]{2,1,0:T(8,128)(2,1)} %param.17) | copy-start | bytes 1572868
  7.2 95.2 %all-gather.9.cloned.1.call-start = ((), (), s32[]{:S(2)}) async-start(), calls=%async_computation.3 | async-start | bytes 18874368 | tf_op jit(solution)/shard_map/all_gather | solution.py:93
  7.9 131.7 %all-gather.17.cloned.1.call-start = ((), (), s32[]{:S(2)}) async-start(), calls=%async_computation.10 | async-start | bytes 1310720 | tf_op jit(solution)/shard_map/all_gather | solution.py:145
  10.1 100.5 %copy-start.34 = (f32[128]{0:T(128)}, f32[128]{0:T(128)S(1)}, u32[]{:S(2)}) copy-start(f32[128]{0:T(128)S(1)} %add_rsqrt_fusion.3) | copy-start | bytes 1540
  10.2 101.3 %copy-start.38 = (f32[128]{0:T(128)S(1)}, f32[128]{0:T(128)}, u32[]{:S(2)}) copy-start(f32[128]{0:T(128)} %param.21) | copy-start | bytes 1540
  110.6 17.9 copy-start.10
  111.5 57.7 %all-gather.19.cloned.1.call-start = ((), (), s32[]{:S(2)}) async-start(), calls=%async_computation.11 | async-start | bytes 1310720 | tf_op jit(solution)/shard_map/all_gather | solution.py:144
  114.3 110.3 %all-gather.11.cloned.1.call-start = ((), (), s32[]{:S(2)}) async-start(), calls=%async_computation.4 | async-start | bytes 9437184 | tf_op jit(solution)/shard_map/all_gather | solution.py:197
  114.9 343.5 %all-gather.13.cloned.1.call-start = ((), (), s32[]{:S(2)}) async-start(), calls=%async_computation.5 | async-start | bytes 56623104 | tf_op jit(solution)/shard_map/all_gather | solution.py:203
  115.5 469.9 %all-gather.15.cloned.1.call-start = ((), (), s32[]{:S(2)}) async-start(), calls=%async_computation.6 | async-start | bytes 28311552 | tf_op jit(solution)/shard_map/all_gather | solution.py:209
  116.1 653.5 %reduce-scatter.4.cloned.1.call-start = ((), (), s32[]{:S(2)}) async-start(), calls=%async_computation.7 | async-start | bytes 1310720 | tf_op jit(solution)/shard_map/reduce_scatter | solution.py:293
  193.0 31.6 %copy-start.13 = (bf16[4,128,8,128]{3,2,1,0:T(8,128)(2,1)}, bf16[4,128,8,128]{3,2,1,0:T(8,128)(2,1)S(1)}, u32[]{:S(2)}) copy-start(bf16[4,128,8,128]{3,2,1,0:T(8,128)(2,1)S(1)} %get-tuple-element.797) | copy-start | bytes 3145732
  224.6 233.9 %copy-start.22 = (f32[2048]{0:T(1024)S(1)}, f32[2048]{0:T(1024)}, u32[]{:S(2)}) copy-start(f32[2048]{0:T(1024)} %param.22) | copy-start | bytes 24580
  231.1 457.7 %copy-start = (f32[128,2048]{1,0:T(8,128)}, f32[128,2048]{1,0:T(8,128)S(1)}, u32[]{:S(2)}) copy-start(f32[128,2048]{1,0:T(8,128)S(1)} %get-tuple-element.496) | copy-start | bytes 3145732
  458.4 127.0 %copy-start.18 = (bf16[1,128,2048]{2,1,0:T(8,128)(2,1)S(1)}, bf16[1,128,2048]{2,1,0:T(8,128)(2,1)}, u32[]{:S(2)}) copy-start(bf16[1,128,2048]{2,1,0:T(8,128)(2,1)} %param.27) | copy-start | bytes 1572868
  730.9 56.1 %reduce-scatter.6.cloned.1.call-start = ((), (), s32[]{:S(2)}) async-start(), calls=%async_computation.8 | async-start | bytes 1310720 | tf_op jit(solution)/shard_map/reduce_scatter | solution.py:296
  734.5 21.3 copy-start.27
  755.7 1771.5 %reduce-scatter.8.cloned.1.call-start = ((), (), s32[]{:S(2)}) async-start(), calls=%async_computation.9 | async-start | bytes 207618048 | tf_op jit(solution)/shard_map/reduce_scatter | solution.py:324
  770.6 17.4 copy-start.8
  770.6 17.4 copy-start.20
  770.6 17.4 copy-start.28
  770.6 17.4 copy-start.35
  773.3 28.4 %copy-start.23 = (bf16[128,1024]{1,0:T(8,128)(2,1)}, bf16[128,1024]{1,0:T(8,128)(2,1)S(1)}, u32[]{:S(2)}) copy-start(bf16[128,1024]{1,0:T(8,128)(2,1)S(1)} %copy_bitcast_fusion.3) | copy-start | bytes 786436
  952.5 53.3 %copy-start.6 = (f32[128,2048]{1,0:T(8,128)S(1)}, f32[128,2048]{1,0:T(8,128)}, u32[]{:S(2)}) copy-start(f32[128,2048]{1,0:T(8,128)} %copy-done.4) | copy-start | bytes 3145732
  (28 other events, 212.1 us)
Sparse Core Ops, SparseCore 0:
  9.9 92.4 all-gather.8
  111.6 27.9 all-gather.16
  141.8 27.3 all-gather.18
  170.9 53.6 all-gather.10
  226.3 232.0 all-gather.12
  460.2 125.1 all-gather.14
  731.0 27.2 reduce-scatter.3
  761.2 25.7 reduce-scatter.5
  933.7 1593.5 reduce-scatter.7
where the time goes:
time: 2550 us; the launch traced here: 2540 us
  waiting for transfers between devices  2020 us (79%)
  matrix products  240 us (9%)
  other arithmetic  165 us (6%)
  local copies, waits for them, and re-layouts  49.3 us (2%)
  blocking collectives  48.9 us (2%)
    reduce_scatter x1, waiting for transfers between devices, local(): lax.psum_scatter(jnp.concatenate([jnp.concatenate([transposed(first_norme...  1520 us
    all_gather x1, waiting for transfers between devices, local(): lax.all_gather(gate_up, ('seq', 'fsdp'), axis=0, tiled=True)  227 us
    concatenate x1, other arithmetic, local(): jnp.concatenate([jnp.concatenate([transposed(first_normed, grad_projected...  132 us
    all_gather x1, waiting for transfers between devices, local(): lax.all_gather(down_weight, ('seq', 'fsdp'), axis=0, tiled=True)  104 us
    all_gather x1, waiting for transfers between devices, local(): lax.all_gather(attention_in, ('seq', 'fsdp'), axis=0, tiled=True)  92.1 us
    dot_general x4, matrix products, transposed(): lax.dot_general(left, right, (((0,), (0,)), ((), ())), preferred_element_...  79.3 us
    dot_general x4, matrix products, right_columns(): lax.dot_general(left, piece, (((1,), (1,)), ((), ())), preferred_element_...  63.8 us
    dot_general x4, matrix products, add_rows(): return jnp.dot(left, piece, preferred_element_type=jnp.float32)  51.2 us
  transfers between devices with their start and end apart: 9, of which 8 were waited for; matrix products, arithmetic and copies ran while one was open for 6% of the time, Pallas kernels for 0%

commit v1 on v0

v1 whole, which is shorter than its diff:
```python
import jax
import jax.numpy as jnp
from jax import lax
from jax.sharding import PartitionSpec as P

D = 2048
QUERY_HEADS = 16
KEY_VALUE_HEADS = 8
HEAD_SIZE = 128
FF = 6144

EPS = 1e-06
ROPE_BASE = 1000000.0
MASK_FLOOR = -1e30
PLANE = ("seq", "fsdp")
F32 = jnp.float32
BF16 = jnp.bfloat16


def rms_scale(values):
    return lax.rsqrt(jnp.mean(values * values, axis=-1, keepdims=True) + EPS)


def rms_back(grad_normed, normed_hat, scale, gain):
    grad_hat = grad_normed * gain
    inner = jnp.mean(grad_hat * normed_hat, axis=-1, keepdims=True)
    return scale * (grad_hat - normed_hat * inner)


def rope_tables(token_positions):
    half = HEAD_SIZE // 2
    rates = jnp.power(F32(ROPE_BASE), jnp.arange(half, dtype=F32) * (-2.0 / HEAD_SIZE))
    angles = token_positions.astype(F32)[:, None] * rates[None, :]
    angles = jnp.concatenate([angles, angles], axis=1)
    return (jnp.cos(angles), jnp.sin(angles))


def apply_rotation(values, cosine_table, sine_table):
    half = values.shape[-1] // 2
    turned = jnp.concatenate([-values[..., half:], values[..., :half]], axis=-1)
    return values * cosine_table[:, None, :] + turned * sine_table[:, None, :]


def rotate_back(grads, cosine_table, sine_table):
    half = grads.shape[-1] // 2
    scaled = grads * sine_table[:, None, :]
    turned = jnp.concatenate([scaled[..., half:], -scaled[..., :half]], axis=-1)
    return grads * cosine_table[:, None, :] + turned


def rows_by(left, right):
    return jnp.dot(left, right, preferred_element_type=F32)


def rows_by_t(left, right):
    return lax.dot_general(left, right, (((1,), (1,)), ((), ())), preferred_element_type=F32)


def t_by_rows(left, right):
    return lax.dot_general(left, right, (((0,), (0,)), ((), ())), preferred_element_type=F32)


def gather_ctx(rows):
    return lax.all_gather(rows, "ctx", axis=0, tiled=True)


def gather_plane(rows):
    return lax.all_gather(rows, PLANE, axis=0, tiled=True)


def scatter_ctx(partials):
    parts = lax.axis_size("ctx")
    pieces = lax.all_to_all(partials.astype(BF16), "ctx", 0, 0, tiled=True)
    pieces = pieces.reshape(parts, partials.shape[0] // parts, partials.shape[1])
    return jnp.sum(pieces.astype(F32), axis=0)


def scatter_weight(grad):
    seqs, ctxs, cores = lax.axis_size("seq"), lax.axis_size("ctx"), lax.axis_size("fsdp")
    rows = grad.shape[0] // (seqs * ctxs * cores)
    grad = grad.astype(BF16).reshape(seqs, ctxs, cores, rows, grad.shape[1])
    grad = jnp.transpose(grad, (0, 2, 1, 3, 4)).reshape(-1, grad.shape[-1])
    grad = lax.psum_scatter(grad, PLANE, scatter_dimension=0, tiled=True)
    grad = lax.all_to_all(grad, "ctx", 0, 0, tiled=True)
    return grad.reshape(ctxs, rows, grad.shape[-1])


def join_columns(pieces):
    parts, rows, width = pieces.shape
    return jnp.transpose(pieces, (1, 0, 2)).reshape(rows, parts * width).astype(F32)


def local(
    inputs,
    block_index,
    attention_gain,
    query_norm_gain,
    key_gain,
    feedforward_gain,
    attention_in,
    attention_out,
    gate_up,
    down_weight,
    grad_output,
):
    parts = lax.axis_size("ctx")
    me = lax.axis_index("ctx")
    tokens = inputs.shape[1]
    half_rows = tokens // 2
    length = tokens * parts
    query_heads = QUERY_HEADS // parts
    key_heads = max(1, KEY_VALUE_HEADS // parts)
    copies = key_heads * parts // KEY_VALUE_HEADS
    group = query_heads // key_heads
    query_width = query_heads * HEAD_SIZE
    key_width = key_heads * HEAD_SIZE
    all_query = QUERY_HEADS * HEAD_SIZE
    all_key = KEY_VALUE_HEADS * HEAD_SIZE
    hidden_width = FF // parts
    scale = HEAD_SIZE ** (-0.5)

    def columns(weight, start, width):
        return lax.dynamic_slice_in_dim(weight, start, width, axis=1)

    key_start = (me // copies) * key_width
    weight_in = gather_plane(
        jnp.concatenate(
            [
                columns(attention_in, me * query_width, query_width),
                columns(attention_in, all_query + key_start, key_width),
                columns(attention_in, all_query + all_key + key_start, key_width),
            ],
            axis=1,
        )
    )
    own_inputs = inputs[0]
    sequence_inputs = gather_ctx(own_inputs)
    blocks = lax.all_gather(block_index[0, 0], "ctx", axis=0, tiled=True)
    weight_out = gather_plane(attention_out)
    weight_gate_up = gather_plane(
        jnp.concatenate(
            [
                columns(gate_up, me * hidden_width, hidden_width),
                columns(gate_up, FF + me * hidden_width, hidden_width),
            ],
            axis=1,
        )
    )
    weight_down = gather_plane(columns(down_weight, me * hidden_width, hidden_width))
    own_grad = grad_output[0]
    sequence_grad = gather_ctx(own_grad)

    steps_along = jnp.arange(half_rows, dtype=jnp.int32)
    positions = (blocks[:, None] * half_rows + steps_along[None, :]).reshape(-1)
    cosine_table, sine_table = rope_tables(positions)

    rows = sequence_inputs.astype(F32)
    first_scale = rms_scale(rows)
    first_hat = rows * first_scale
    first_normed = (first_hat * attention_gain).astype(BF16)
    projected = rows_by(first_normed, weight_in)
    query = projected[:, :query_width].reshape(length, query_heads, HEAD_SIZE)
    key = projected[:, query_width : query_width + key_width].reshape(length, key_heads, HEAD_SIZE)
    value = projected[:, query_width + key_width :].astype(BF16)
    value = value.reshape(length, key_heads, HEAD_SIZE)
    query_scale = rms_scale(query)
    query_hat = query * query_scale
    key_scale = rms_scale(key)
    key_hat = key * key_scale
    rotary_query = (
        apply_rotation(query_hat * query_norm_gain, cosine_table, sine_table)
        .astype(BF16)
        .reshape(length, key_heads, group, HEAD_SIZE)
    )
    rotary_key = apply_rotation(key_hat * key_gain, cosine_table, sine_table).astype(BF16)

    scores = (
        jnp.einsum("qhgd,khd->hgqk", rotary_query, rotary_key, preferred_element_type=F32) * scale
    )
    allowed = positions[None, :] <= positions[:, None]
    scores = jnp.where(allowed, scores, MASK_FLOOR)
    peak = jnp.max(scores, axis=-1, keepdims=True)
    total = jnp.sum(jnp.where(allowed, jnp.exp(scores - peak), 0.0), axis=-1, keepdims=True)
    total_logarithm = peak + jnp.log(total)
    probs = jnp.where(allowed, jnp.exp(scores - total_logarithm), 0.0)
    weights = probs.astype(BF16)
    attended = jnp.einsum("hgqk,khd->qhgd", weights, value, preferred_element_type=F32)
    attended = attended.astype(BF16).reshape(length, query_width)

    own_attended = lax.all_to_all(attended, "ctx", 0, 1, tiled=True)
    own_rows = own_inputs.astype(F32)
    middle = own_rows + rows_by_t(own_attended, weight_out)
    second_scale = rms_scale(middle)
    second_hat = middle * second_scale
    second_normed = (second_hat * feedforward_gain).astype(BF16)
    sequence_second = gather_ctx(second_normed)

    grad_hidden = rows_by(sequence_grad, weight_down)
    gate_values = rows_by(sequence_second, weight_gate_up)
    gate = gate_values[:, :hidden_width]
    upward = gate_values[:, hidden_width:]
    sigmoid_gate = jax.nn.sigmoid(gate)
    silu_gate = gate * sigmoid_gate
    hidden = (silu_gate * upward).astype(BF16)
    grad_gate = grad_hidden * upward * sigmoid_gate * (1.0 + gate * (1.0 - sigmoid_gate))
    grad_upward = grad_hidden * silu_gate
    grad_gate_up = jnp.concatenate([grad_gate, grad_upward], axis=1).astype(BF16)
    grad_second = scatter_ctx(rows_by_t(grad_gate_up, weight_gate_up))

    down_pieces = scatter_weight(t_by_rows(sequence_grad, hidden))
    gate_up_pieces = scatter_weight(t_by_rows(sequence_second, grad_gate_up))
    output = middle + scatter_ctx(rows_by_t(hidden, weight_down))

    feedforward_part = jnp.sum(grad_second * second_hat, axis=0)
    grad_middle = own_grad.astype(F32) + rms_back(
        grad_second, second_hat, second_scale, feedforward_gain
    )
    grad_middle_short = grad_middle.astype(BF16)
    own_attended_grad = rows_by(grad_middle_short, weight_out).astype(BF16)
    attended_grad = lax.all_to_all(own_attended_grad, "ctx", 1, 0, tiled=True)
    sequence_middle_grad = gather_ctx(grad_middle_short)
    out_pieces = scatter_weight(t_by_rows(sequence_middle_grad, attended))

    delta = jnp.sum(
        (attended_grad.astype(F32) * attended.astype(F32)).reshape(
            length, key_heads, group, HEAD_SIZE
        ),
        axis=-1,
    )
    head_grads = attended_grad.reshape(length, key_heads, group, HEAD_SIZE)
    grad_probs = jnp.einsum("qhgd,khd->hgqk", head_grads, value, preferred_element_type=F32)
    grad_scores = (probs * (grad_probs - jnp.transpose(delta, (1, 2, 0))[..., None])).astype(BF16)
    grad_rotary_query = (
        jnp.einsum("hgqk,khd->qhgd", grad_scores, rotary_key, preferred_element_type=F32) * scale
    )
    grad_rotary_key = (
        jnp.einsum("hgqk,qhgd->khd", grad_scores, rotary_query, preferred_element_type=F32) * scale
    )
    value_grad = jnp.einsum("hgqk,qhgd->khd", weights, head_grads, preferred_element_type=F32)
    unrotated_query = rotate_back(
        grad_rotary_query.reshape(length, query_heads, HEAD_SIZE), cosine_table, sine_table
    )
    unrotated_key = rotate_back(grad_rotary_key, cosine_table, sine_table)
    query_part = jnp.sum(unrotated_query * query_hat, axis=(0, 1))
    key_part = jnp.sum(unrotated_key * key_hat, axis=(0, 1))
    grad_query = rms_back(unrotated_query, query_hat, query_scale, query_norm_gain)
    grad_key = rms_back(unrotated_key, key_hat, key_scale, key_gain)
    grad_projected = jnp.concatenate(
        [
            grad_query.reshape(length, query_width),
            grad_key.reshape(length, key_width),
            value_grad.reshape(length, key_width),
        ],
        axis=1,
    ).astype(BF16)
    partial_first = rows_by_t(grad_projected, weight_in)
    attention_part = jnp.sum(partial_first * first_hat, axis=0)
    grad_first = scatter_ctx(partial_first)
    in_pieces = scatter_weight(t_by_rows(first_normed, grad_projected))
    own_scale = rms_scale(own_rows)
    input_grad = grad_middle + rms_back(
        grad_first, own_rows * own_scale, own_scale, attention_gain
    )
    gain_sums = lax.psum(
        (attention_part, query_part, key_part, feedforward_part), ("seq", "ctx", "fsdp")
    )

    def merge_copies(pieces):
        shape = pieces.shape
        return jnp.sum(pieces.reshape(shape[0] // copies, copies, shape[1], shape[2]), axis=1)

    attention_in_grad = jnp.concatenate(
        [
            join_columns(in_pieces[:, :, :query_width]),
            join_columns(
                merge_copies(in_pieces[:, :, query_width : query_width + key_width].astype(F32))
            ),
            join_columns(merge_copies(in_pieces[:, :, query_width + key_width :].astype(F32))),
        ],
        axis=1,
    )
    gate_up_grad = jnp.concatenate(
        [
            join_columns(gate_up_pieces[:, :, :hidden_width]),
            join_columns(gate_up_pieces[:, :, hidden_width:]),
        ],
        axis=1,
    )
    return (
        output.astype(BF16)[None],
        input_grad.astype(BF16)[None],
        gain_sums[0],
        gain_sums[1],
        gain_sums[2],
        gain_sums[3],
        attention_in_grad,
        join_columns(out_pieces),
        gate_up_grad,
        join_columns(down_pieces),
    )


def solution(mesh):
    tokens = P(("seq", "fsdp"), "ctx", None)
    weight = P(("seq", "fsdp"), None)
    grad = P(("seq", "ctx", "fsdp"), None)
    in_specs = (tokens, tokens, P(), P(), P(), P(), weight, weight, weight, weight, tokens)
    out_specs = (tokens, tokens, P(), P(), P(), P(), grad, grad, grad, grad)
    return jax.shard_map(local, mesh=mesh, in_specs=in_specs, out_specs=out_specs, check_vma=False)
```

time: 2550 us -> 868 us (0.34)
  waiting for transfers between devices: 2020 us -> 419 us
  matrix products: 240 us -> 101 us
  blocking collectives: 48.9 us -> 176 us
  other arithmetic: 165 us -> 40.4 us
  local copies, waits for them, and re-layouts: 49.3 us -> 79.5 us
    reduce_scatter x3 -> x4, waiting for transfers between devices: 1530 us -> 0.06 us  [scatter_weight(): grad = lax.psum_scatter(grad, PLANE, scatter_dimension=0, tiled=True)]
    all_gather x6 -> x8, waiting for transfers between devices: 486 us -> 312 us  [the longest x4 159 us: gather_plane(): return lax.all_gather(rows, PLANE, axis=0, tiled=True)]
    dot_general x40 -> x18, matrix products: 240 us -> 101 us  [the longest x4 33.6 us: rows_by(): return jnp.dot(left, right, preferred_element_type=F32)]
    concatenate x1 -> x4, other arithmetic: 132 us -> 5.12 us  [the longest x1 1.87 us: local(): jnp.concatenate([join_columns(gate_up_pieces[:, :, :hidden_width]), join_...]
    all_to_all x0 -> x3, blocking collectives: none -> 125 us  [the longest x2 106 us: scatter_ctx(): pieces = lax.all_to_all(partials.astype(BF16), 'ctx', 0, 0, tiled=True)]
    all_to_all x0 -> x6, waiting for transfers between devices: none -> 106 us  [the longest x4 52.7 us: scatter_weight(): grad = lax.all_to_all(grad, 'ctx', 0, 0, tiled=True)]
  transfers between devices with their start and end apart: 9 -> 18, of which waited for: 8 -> 13; matrix products, arithmetic and copies ran while one was open for 6% -> 21% of each run, Pallas kernels for 0% -> 0%
where the time goes in v1:
time: 868 us; the launch traced here: 859 us
  waiting for transfers between devices  419 us (48%)
  blocking collectives  176 us (20%)
  matrix products  101 us (12%)
  local copies, waits for them, and re-layouts  79.5 us (9%)
  other arithmetic  40.4 us (5%)
  starting transfers between devices  25.7 us (3%)
  between operations  16.2 us (2%)
    all_gather x4, waiting for transfers between devices, gather_plane(): return lax.all_gather(rows, PLANE, axis=0, tiled=True)  159 us
    all_gather x4, waiting for transfers between devices, gather_ctx(): return lax.all_gather(rows, 'ctx', axis=0, tiled=True)  153 us
    all_to_all x2, blocking collectives, scatter_ctx(): pieces = lax.all_to_all(partials.astype(BF16), 'ctx', 0, 0, tiled=True)  106 us
    all_to_all x4, waiting for transfers between devices, scatter_weight(): grad = lax.all_to_all(grad, 'ctx', 0, 0, tiled=True)  52.7 us
    all_to_all x1, waiting for transfers between devices, scatter_ctx(): pieces = lax.all_to_all(partials.astype(BF16), 'ctx', 0, 0, tiled=True)  41.8 us
    psum x1, blocking collectives, local(): lax.psum((attention_part, query_part, key_part, feedforward_part), ('seq'...  41.1 us
    dot_general x4, matrix products, rows_by(): return jnp.dot(left, right, preferred_element_type=F32)  33.6 us
    dot_general x4, matrix products, rows_by_t(): lax.dot_general(left, right, (((1,), (1,)), ((), ())), preferred_element_...  28.5 us
  transfers between devices with their start and end apart: 18, of which 13 were waited for; matrix products, arithmetic and copies ran while one was open for 21% of the time, Pallas kernels for 0%

profile of v1, /device:TPU:0, one launch (start us, length us, event | category | flops | bytes accessed | tf_op | source)
XLA Modules:
  0.0 859.1 jit_solution(17743608366235928111)
XLA Ops:
  13.2 10.0 %all-reduce = s32[8]{0:T(128)S(1)} all-reduce(s32[8]{0:T(128)S(1)} %bitcast_dynamic-update-slice_fusion), channel_id=3, replica_groups=mesh['seq'=4,'ctx'=4,'fsdp'=2] {'ctx'}, use_global_device_ids=true, to_apply=%add | all-reduce | flops 8 | bytes 64
  25.5 32.6 %all-gather.24.cloned.1.call-done = bf16[1,512,2048]{2,1,0:T(8,128)(2,1)} async-done(((bf16[1,128,2048]{2,1,0:T(8,128)(2,1)}), bf16[1,512,2048]{2,1,0:T(8,128)(2,1)}) %all-gather.24.cloned.1.call-update) | async-done | bytes 2097168 | tf_op jit(solution)/shard_map/all_gather | solution.py:64
  60.1 35.7 %all-gather.12.cloned.1.call-done = bf16[2048,1024]{1,0:T(8,128)(2,1)} async-done(((bf16[256,1024]{1,0:T(8,128)(2,1)}), bf16[2048,1024]{1,0:T(8,128)(2,1)}) %all-gather.12.cloned.1.call-update) | async-done | bytes 4194320 | tf_op jit(solution)/shard_map/all_gather | solution.py:68
  128.9 19.9 %all_to_all.98 = bf16[4,128,512]{1,2,0:T(8,128)(2,1)} all-to-all(bf16[4,128,512]{1,2,0:T(8,128)(2,1)S(1)} %copy.204), channel_id=1, replica_groups=mesh['seq'=4,'ctx'=4,'fsdp'=2] {'ctx'}, dimensions={0} | all-to-all | bytes 1048576 | tf_op jit(solution)/shard_map/all_to_all | solution.py:190
  165.1 41.3 %all-gather.16.cloned.1.call-done = bf16[512,2048]{1,0:T(8,128)(2,1)} async-done(((bf16[128,2048]{1,0:T(8,128)(2,1)}), bf16[512,2048]{1,0:T(8,128)(2,1)}) %all-gather.16.cloned.1.call-update) | async-done | bytes 2097168 | tf_op jit(solution)/shard_map/all_gather | solution.py:64
  206.4 73.1 %all-gather.18.cloned.1.call-done = bf16[2048,3072]{1,0:T(8,128)(2,1)} async-done(((bf16[256,3072]{1,0:T(8,128)(2,1)}), bf16[2048,3072]{1,0:T(8,128)(2,1)}) %all-gather.18.cloned.1.call-update) | async-done | bytes 12582928 | tf_op jit(solution)/shard_map/all_gather | solution.py:68
  279.5 11.9 %fusion.50 = f32[512,3072]{1,0:T(8,128)} fusion(bf16[512,2048]{1,0:T(8,128)(2,1)} %all-gather.16.cloned.1.call-done, bf16[2048,3072]{1,0:T(8,128)(2,1)} %all-gather.18.cloned.1.call-done), kind=kOutput, calls=%fused_computation.145 | convolution fusion | flops 6442450944 | bytes 20971520 | tf_op jit(solution)/shard_map/dot_general | solution.py:52
  291.5 35.2 %all-gather.26.cloned.1.call-done = bf16[1,512,2048]{2,1,0:T(8,128)(2,1)} async-done(((bf16[1,128,2048]{2,1,0:T(8,128)(2,1)}), bf16[1,512,2048]{2,1,0:T(8,128)(2,1)}) %all-gather.26.cloned.1.call-update) | async-done | bytes 2097168 | tf_op jit(solution)/shard_map/all_gather | solution.py:64
  326.6 46.7 %all-gather.20.cloned.1.call-done = bf16[2048,1536]{1,0:T(8,128)(2,1)} async-done(((bf16[256,1536]{1,0:T(8,128)(2,1)}), bf16[2048,1536]{1,0:T(8,128)(2,1)}) %all-gather.20.cloned.1.call-update) | async-done | bytes 6291472 | tf_op jit(solution)/shard_map/all_gather | solution.py:68
  373.3 10.9 %multiply_convert_fusion.1 = (bf16[512,1536]{1,0:T(8,128)(2,1)S(1)}, bf16[512,1536]{1,0:T(8,128)(2,1)S(1)}, bf16[512,1536]{1,0:T(8,128)(2,1)}) fusion(f32[512,3072]{1,0:T(8,128)} %fusion.50, bf16[2048,1536]{1,0:T(8,128)(2,1)} %all-gather.20.cloned.1.call-done, bf16[1,512,2048]{2,1,0:T(8,128)(2,1)} %all-gather.26.cloned.1.call-done), kind=kOutput, calls=%fused_computation.24 | convolution fusion | flops 3233021952 | bytes 19398656 | tf_op jit(solution)/shard_map/dot_general | solution.py:52
  384.2 6.9 convolution_convert_fusion.3
  391.2 53.1 %all_to_all.99 = bf16[4,128,2048]{2,1,0:T(8,128)(2,1)S(1)} all-to-all(bf16[4,128,2048]{2,1,0:T(8,128)(2,1)S(1)} %bitcast.232), channel_id=1, replica_groups=mesh['seq'=4,'ctx'=4,'fsdp'=2] {'ctx'}, dimensions={0} | all-to-all | bytes 4194304 | tf_op jit(solution)/shard_map/all_to_all | solution.py:73
  446.8 43.7 %all-gather.22.cloned.1.call-done = bf16[512,2048]{1,0:T(8,128)(2,1)} async-done(((bf16[128,2048]{1,0:T(8,128)(2,1)}), bf16[512,2048]{1,0:T(8,128)(2,1)}) %all-gather.22.cloned.1.call-update) | async-done | bytes 2097168 | tf_op jit(solution)/shard_map/all_gather | solution.py:64
  495.0 8.2 fusion
  503.2 8.7 %copy.233 = bf16[2048,1536]{1,0:T(8,128)(2,1)} copy(bf16[2048,1536]{0,1:T(8,128)(2,1)} %fusion) | data formatting | bytes 12582912 | tf_op jit(solution)/shard_map/convert_element_type | solution.py:81
  534.2 11.3 %all-to-all-done.3 = bf16[128,4,512]{0,2,1:T(8,128)(2,1)} async-done(((bf16[128,4,512]{0,2,1:T(8,128)(2,1)}), bf16[128,4,512]{0,2,1:T(8,128)(2,1)}, u32[]{:S(2)}, u32[]{:S(2)}) %all-to-all-start.3) | async-done | bytes 524320 | tf_op jit(solution)/shard_map/all_to_all | solution.py:220
  592.3 9.3 %convolution_convert_fusion = bf16[2048,3072]{1,0:T(8,128)(2,1)S(1)} fusion(bf16[512,2048]{1,0:T(8,128)(2,1)} %all-gather.16.cloned.1.call-done, bf16[512,1536]{1,0:T(8,128)(2,1)} %copy-done.47, bf16[512,1536]{1,0:T(8,128)(2,1)} %copy-done.46), kind=kOutput, calls=%fused_computation | convolution fusion | flops 6455033856 | bytes 17825792 | tf_op jit(solution)/shard_map/dot_general | solution.py:60
  607.2 8.5 convolution_convert_fusion.5
  626.9 41.8 %all-to-all-done.1 = bf16[4,128,2048]{2,1,0:T(8,128)(2,1)} async-done(((bf16[4,128,2048]{2,1,0:T(8,128)(2,1)}), bf16[4,128,2048]{2,1,0:T(8,128)(2,1)}, u32[]{:S(2)}, u32[]{:S(2)}) %all-to-all-start.1) | async-done | bytes 2097184 | tf_op jit(solution)/shard_map/all_to_all | solution.py:73
  668.7 52.4 %all_to_all.100 = bf16[4,128,2048]{2,1,0:T(8,128)(2,1)} all-to-all(bf16[4,128,2048]{2,1,0:T(8,128)(2,1)} %bitcast.231), channel_id=1, replica_groups=mesh['seq'=4,'ctx'=4,'fsdp'=2] {'ctx'}, dimensions={0} | all-to-all | bytes 4194304 | tf_op jit(solution)/shard_map/all_to_all | solution.py:73
  724.5 8.0 all-to-all-done.6
  736.9 17.3 %all-to-all-done.8 = bf16[4,64,1536]{2,1,0:T(8,128)(2,1)} async-done(((bf16[4,64,1536]{2,1,0:T(8,128)(2,1)}), bf16[4,64,1536]{2,1,0:T(8,128)(2,1)}, u32[]{:S(2)}, u32[]{:S(2)}) %all-to-all-start.8) | async-done | bytes 786464 | tf_op jit(solution)/shard_map/all_to_all | solution.py:84
  761.4 41.1 %all-reduce.1 = (f32[2048]{0:T(1024)}, f32[128]{0:T(128)}, f32[128]{0:T(128)}, f32[2048]{0:T(1024)}) all-reduce(f32[2048]{0:T(1024)S(1)} %get-tuple-element.26, f32[128]{0:T(128)S(1)} %get-tuple-element.10, f32[128]{0:T(128)S(1)} %get-tuple-element.14, ...), channel_id=1, replica_groups=mesh['seq'=4,'ctx'=4,'fsdp'=2] {'seq','ctx','fsdp'}, use_global_device_ids=true, to_apply=%region_16.17 | all-reduce | flops 4352 | bytes 34816 | tf_op jit(solution)/shard_map/psum | solution.py:264
  819.8 27.4 %all-to-all-done.7 = bf16[4,64,3072]{2,1,0:T(8,128)(2,1)} async-done(((bf16[4,64,3072]{2,1,0:T(8,128)(2,1)}), bf16[4,64,3072]{2,1,0:T(8,128)(2,1)}, u32[]{:S(2)}, u32[]{:S(2)}) %all-to-all-start.7) | async-done | bytes 1572896 | tf_op jit(solution)/shard_map/all_to_all | solution.py:84
  (246 shorter events, 188.0 us)
Async XLA Ops:
  7.2 156.9 %copy-start = (bf16[256,6144]{1,0:T(8,128)(2,1)S(1)}, bf16[256,6144]{1,0:T(8,128)(2,1)}, u32[]{:S(2)}) copy-start(bf16[256,6144]{1,0:T(8,128)(2,1)} %param.20) | copy-start | bytes 9437188
  7.2 50.8 %all-gather.24.cloned.1.call-start = ((), (), s32[]{:S(2)}) async-start(), calls=%async_computation.23 | async-start | bytes 2621440 | tf_op jit(solution)/shard_map/all_gather | solution.py:64
  8.0 87.9 %all-gather.12.cloned.1.call-start = ((), (), s32[]{:S(2)}) async-start(), calls=%async_computation.13 | async-start | bytes 4718592 | tf_op jit(solution)/shard_map/all_gather | solution.py:68
  10.1 85.7 %copy-start.40 = (f32[2048]{0:T(1024)S(1)}, f32[2048]{0:T(1024)}, u32[]{:S(2)}) copy-start(f32[2048]{0:T(1024)} %param.13) | copy-start | bytes 24580
  11.0 141.0 %all-gather.14.cloned.1.call-start = ((), (), s32[]{:S(2)}) async-start(), calls=%async_computation.14 | async-start | bytes 9437184 | tf_op jit(solution)/shard_map/all_gather | solution.py:68
  11.8 194.6 %all-gather.16.cloned.1.call-start = ((), (), s32[]{:S(2)}) async-start(), calls=%async_computation.15 | async-start | bytes 2621440 | tf_op jit(solution)/shard_map/all_gather | solution.py:64
  160.5 119.0 %all-gather.18.cloned.1.call-start = ((), (), s32[]{:S(2)}) async-start(), calls=%async_computation.16 | async-start | bytes 14155776 | tf_op jit(solution)/shard_map/all_gather | solution.py:68
  163.4 163.2 %all-gather.26.cloned.1.call-start = ((), (), s32[]{:S(2)}) async-start(), calls=%async_computation.24 | async-start | bytes 2621440 | tf_op jit(solution)/shard_map/all_gather | solution.py:64
  164.0 209.3 %all-gather.20.cloned.1.call-start = ((), (), s32[]{:S(2)}) async-start(), calls=%async_computation.17 | async-start | bytes 7077888 | tf_op jit(solution)/shard_map/all_gather | solution.py:68
  165.0 325.4 %all-gather.22.cloned.1.call-start = ((), (), s32[]{:S(2)}) async-start(), calls=%async_computation.19 | async-start | bytes 2621440 | tf_op jit(solution)/shard_map/all_gather | solution.py:64
  391.2 53.6 %copy-start.5 = (f32[128,2048]{1,0:T(8,128)S(1)}, f32[128,2048]{1,0:T(8,128)}, u32[]{:S(2)}) copy-start(f32[128,2048]{1,0:T(8,128)} %copy-done.4) | copy-start | bytes 3145732
  444.7 45.7 %copy-start.29 = (bf16[2,128,2,512]{3,1,2,0:T(8,128)(2,1)S(1)}, bf16[2,128,2,512]{3,1,2,0:T(8,128)(2,1)}, u32[]{:S(2)}) copy-start(bf16[2,128,2,512]{3,1,2,0:T(8,128)(2,1)} %convolution_convert_fusion.7) | copy-start | bytes 1572868
  446.5 274.5 %reduce-scatter.7.cloned.1.call-start = ((), (), s32[]{:S(2)}) async-start(), calls=%async_computation.20 | async-start | bytes 2359296 | tf_op jit(solution)/shard_map/reduce_scatter | solution.py:83
  494.9 229.5 %reduce-scatter.11.cloned.1.call-start = ((), (), s32[]{:S(2)}) async-start(), calls=%async_computation.22 | async-start | bytes 7077888 | tf_op jit(solution)/shard_map/reduce_scatter | solution.py:83
  519.0 12.9 %copy-start.20 = (f32[512,128]{0,1:T(8,128)S(1)}, f32[512,128]{0,1:T(8,128)}, u32[]{:S(2)}) copy-start(f32[512,128]{0,1:T(8,128)} %get-tuple-element.47) | copy-start | bytes 786436
  526.7 18.8 %all-to-all-start.3 = ((bf16[128,4,512]{0,2,1:T(8,128)(2,1)}), bf16[128,4,512]{0,2,1:T(8,128)(2,1)}, u32[]{:S(2)}, u32[]{:S(2)}) async-start(bf16[128,4,512]{0,2,1:T(8,128)(2,1)} %bitcast.26), calls=%async_computation.3 | async-start | bytes 1048576 | tf_op jit(solution)/shard_map/all_to_all | solution.py:220
  530.8 206.1 %reduce-scatter.5.cloned.1.call-start = ((), (), s32[]{:S(2)}) async-start(), calls=%async_computation.18 | async-start | bytes 4718592 | tf_op jit(solution)/shard_map/reduce_scatter | solution.py:83
  592.3 213.6 %reduce-scatter.9.cloned.1.call-start = ((), (), s32[]{:S(2)}) async-start(), calls=%async_computation.21 | async-start | bytes 14155776 | tf_op jit(solution)/shard_map/reduce_scatter | solution.py:83
  615.7 53.0 %all-to-all-start.1 = ((bf16[4,128,2048]{2,1,0:T(8,128)(2,1)}), bf16[4,128,2048]{2,1,0:T(8,128)(2,1)}, u32[]{:S(2)}, u32[]{:S(2)}) async-start(bf16[4,128,2048]{2,1,0:T(8,128)(2,1)} %bitcast.230), calls=%async_computation.1 | async-start | bytes 4194304 | tf_op jit(solution)/shard_map/all_to_all | solution.py:73
  668.7 68.0 %copy-start.8 = (bf16[1,128,2048]{2,1,0:T(8,128)(2,1)S(1)}, bf16[1,128,2048]{2,1,0:T(8,128)(2,1)}, u32[]{:S(2)}) copy-start(bf16[1,128,2048]{2,1,0:T(8,128)(2,1)} %param.11) | copy-start | bytes 1572868
  721.0 11.5 %all-to-all-start.6 = ((bf16[4,64,512]{2,1,0:T(8,128)(2,1)}), bf16[4,64,512]{2,1,0:T(8,128)(2,1)S(1)}, u32[]{:S(2)}, u32[]{:S(2)}) async-start(bf16[4,64,512]{2,1,0:T(8,128)(2,1)} %bitcast.250), calls=%async_computation.8 | async-start | bytes 524288 | tf_op jit(solution)/shard_map/all_to_all | solution.py:84
  732.5 21.7 %all-to-all-start.8 = ((bf16[4,64,1536]{2,1,0:T(8,128)(2,1)}), bf16[4,64,1536]{2,1,0:T(8,128)(2,1)}, u32[]{:S(2)}, u32[]{:S(2)}) async-start(bf16[4,64,1536]{2,1,0:T(8,128)(2,1)} %bitcast.243), calls=%async_computation.12 | async-start | bytes 1572864 | tf_op jit(solution)/shard_map/all_to_all | solution.py:84
  754.2 51.7 %all-to-all-start.5 = ((bf16[4,64,1024]{2,1,0:T(8,128)(2,1)}), bf16[4,64,1024]{2,1,0:T(8,128)(2,1)}, u32[]{:S(2)}, u32[]{:S(2)}) async-start(bf16[4,64,1024]{2,1,0:T(8,128)(2,1)} %bitcast.246), calls=%async_computation.6 | async-start | bytes 1048576 | tf_op jit(solution)/shard_map/all_to_all | solution.py:84
  805.9 41.3 %all-to-all-start.7 = ((bf16[4,64,3072]{2,1,0:T(8,128)(2,1)}), bf16[4,64,3072]{2,1,0:T(8,128)(2,1)}, u32[]{:S(2)}, u32[]{:S(2)}) async-start(bf16[4,64,3072]{2,1,0:T(8,128)(2,1)} %bitcast.239), calls=%async_computation.10 | async-start | bytes 3145728 | tf_op jit(solution)/shard_map/all_to_all | solution.py:84
  (42 other events, 169.8 us)
Sparse Core Ops, SparseCore 0:
  9.6 48.4 all-gather.23
  60.5 35.2 all-gather.11
  97.7 54.2 all-gather.13
  160.6 45.6 all-gather.15
  208.7 70.7 all-gather.17
  281.0 45.6 all-gather.25
  329.1 44.1 all-gather.19
  446.7 43.7 all-gather.21
  495.1 39.9 reduce-scatter.6
  538.2 61.7 reduce-scatter.10
  603.4 51.1 reduce-scatter.4
  657.9 92.2 reduce-scatter.8

commit v2 on v1

v2 whole, which is shorter than its diff:
```python
import jax
import jax.numpy as jnp
from jax import lax
from jax.experimental import pallas as pl
from jax.experimental.pallas import tpu as pltpu
from jax.sharding import PartitionSpec as P


D = 2048
QUERY_HEADS = 16
KEY_VALUE_HEADS = 8
HEAD_SIZE = 128
FF = 6144

EPS = 1e-06
ROPE_BASE = 1000000.0
MASK_FLOOR = -1e30
PLANE = ("seq", "fsdp")
F32 = jnp.float32
BF16 = jnp.bfloat16


def rms_scale(values):
    return lax.rsqrt(jnp.mean(values * values, axis=-1, keepdims=True) + EPS)


def rms_back(grad_normed, normed_hat, scale, gain):
    grad_hat = grad_normed * gain
    inner = jnp.mean(grad_hat * normed_hat, axis=-1, keepdims=True)
    return scale * (grad_hat - normed_hat * inner)


def rope_tables(token_positions):
    half = HEAD_SIZE // 2
    rates = jnp.power(F32(ROPE_BASE), jnp.arange(half, dtype=F32) * (-2.0 / HEAD_SIZE))
    angles = token_positions.astype(F32)[:, None] * rates[None, :]
    cosine, sine = jnp.cos(angles), jnp.sin(angles)
    return (
        jnp.concatenate([cosine, cosine], axis=1),
        jnp.concatenate([-sine, sine], axis=1),
    )


def turn(values):
    return pltpu.roll(values, HEAD_SIZE // 2, 1)


def rows_by(left, right):
    return jnp.dot(left, right, preferred_element_type=F32)


def rows_by_t(left, right):
    return lax.dot_general(left, right, (((1,), (1,)), ((), ())), preferred_element_type=F32)


def t_by_rows(left, right):
    return lax.dot_general(left, right, (((0,), (0,)), ((), ())), preferred_element_type=F32)


def swap(values, axis, step):
    return lax.ppermute(values, axis, [(i, i ^ step) for i in range(lax.axis_size(axis))])


def gather_ctx(rows):
    parts = lax.axis_size("ctx")
    return jnp.concatenate([rows] + [swap(rows, "ctx", k) for k in range(1, parts)], axis=0)


def gather_plane(rows):
    return lax.all_gather(rows, PLANE, axis=0, tiled=True)


def pick_kernel(picks, starts, *refs):
    sources, out, sems = refs[:-2], refs[-2], refs[-1]
    copies, at = [], 0
    for n, (source, width) in enumerate(picks):
        start = pl.multiple_of(starts[n], HEAD_SIZE)
        copies.append(
            pltpu.make_async_copy(
                sources[source].at[:, pl.ds(start, width)],
                out.at[:, pl.ds(at, width)],
                sems.at[n],
            )
        )
        at += width
    for copy in copies:
        copy.start()
    for copy in copies:
        copy.wait()


def pick_columns(sources, picks):
    rows = sources[0].shape[0]
    starts = jnp.stack([jnp.asarray(start, jnp.int32) for _, start, _ in picks])
    anywhere = pl.BlockSpec(memory_space=pl.ANY)
    return pl.pallas_call(
        lambda *refs: pick_kernel([(source, width) for source, _, width in picks], *refs),
        out_shape=jax.ShapeDtypeStruct((rows, sum(width for _, _, width in picks)), BF16),
        in_specs=[pl.BlockSpec(memory_space=pltpu.SMEM)] + [anywhere] * len(sources),
        out_specs=pl.BlockSpec(memory_space=pltpu.VMEM),
        scratch_shapes=[pltpu.SemaphoreType.DMA((len(picks),))],
        name="pick_columns",
    )(starts, *sources)


def scatter_ctx(partials):
    parts = lax.axis_size("ctx")
    tokens = partials.shape[0] // parts
    pieces = [
        swap(partials[k * tokens : (k + 1) * tokens].astype(BF16), "ctx", k)
        for k in range(1, parts)
    ]
    total = partials[:tokens]
    for piece in pieces:
        total = total + piece.astype(F32)
    return total


def gather_heads(attended):
    parts = lax.axis_size("ctx")
    tokens = attended.shape[0] // parts
    pieces = [attended] + [swap(attended, "ctx", j) for j in range(1, parts)]
    whole = pl.BlockSpec(memory_space=pltpu.VMEM)
    return pl.pallas_call(
        lambda *refs: join_heads_kernel(tokens, *refs),
        out_shape=jax.ShapeDtypeStruct((parts * tokens, parts * attended.shape[1]), BF16),
        in_specs=[whole] * parts,
        out_specs=whole,
        name="join_heads",
    )(*pieces)


def join_heads_kernel(tokens, *refs):
    pieces, out = refs[:-1], refs[-1]
    width = pieces[0].shape[1]
    for j, piece in enumerate(pieces):
        for k in range(len(pieces)):
            at = (k ^ j) * tokens
            out[k * tokens : (k + 1) * tokens, j * width : (j + 1) * width] = piece[
                at : at + tokens, :
            ]


def tokens_to_heads(rows):
    parts = lax.axis_size("ctx")
    width = rows.shape[1] // parts
    pieces = [rows[:, :width]]
    for k in range(1, parts):
        pieces.append(swap(rows[:, k * width : (k + 1) * width], "ctx", k))
    return jnp.concatenate(pieces, axis=0)


def tokens_to_rows(rows):
    seqs, ctxs = lax.axis_size("seq"), lax.axis_size("ctx")
    me = lax.axis_index("ctx")
    width = rows.shape[1] // (seqs * ctxs)
    pieces = []
    for k in range(ctxs):
        blocks = [
            lax.dynamic_slice_in_dim(rows, (s * ctxs + (me ^ k)) * width, width, axis=1)
            for s in range(seqs)
        ]
        piece = jnp.concatenate(blocks, axis=1)
        pieces.append(piece if k == 0 else swap(piece, "ctx", k))
    return jnp.concatenate(pieces, axis=0)


def scatter_plane(grad):
    return lax.psum_scatter(grad, PLANE, scatter_dimension=0, tiled=True)


def scatter_plane_swaps(grad):
    seqs, cores = lax.axis_size("seq"), lax.axis_size("fsdp")
    seq, core = lax.axis_index("seq"), lax.axis_index("fsdp")
    rows = grad.shape[0] // (seqs * cores)
    grad = grad.reshape(seqs, cores, rows, grad.shape[1])

    def of_core(k):
        return lax.dynamic_slice_in_dim(grad, core ^ k, 1, axis=1)[:, 0]

    total = of_core(0).astype(F32)
    for k in range(1, cores):
        other = swap(of_core(k), "fsdp", k)
        total = total + other.astype(F32)
    out = lax.dynamic_slice_in_dim(total, seq, 1, axis=0)[0]
    short = total.astype(BF16)
    for k in range(1, seqs):
        piece = lax.dynamic_slice_in_dim(short, seq ^ k, 1, axis=0)[0]
        other = swap(piece, "seq", k)
        out = out + other.astype(F32)
    return out.astype(BF16)


def scatter_weight(grad, over_plane):
    ctxs, cores = lax.axis_size("ctx"), lax.axis_size("fsdp")
    ctx = lax.axis_index("ctx")
    grad = over_plane(grad)
    rows = grad.shape[0] // ctxs
    pieces = []
    for k in range(ctxs):
        piece = lax.dynamic_slice_in_dim(grad, (ctx ^ k) * rows, rows, axis=0)
        pairs = [
            (c * cores + f, f * ctxs + (c ^ k)) for c in range(ctxs) for f in range(cores)
        ]
        pieces.append(lax.ppermute(piece, ("ctx", "fsdp"), pairs))
    return pieces


def sum_everywhere(values):
    for axis in ("ctx", "seq", "fsdp"):
        size = lax.axis_size(axis)
        sums = [values] + [swap(values, axis, k) for k in range(1, size)]
        while len(sums) > 1:
            sums = [sums[i] + sums[i + 1] for i in range(0, len(sums), 2)]
        values = sums[0]
    return values


def join_kernel(segments, source_ref, *refs):
    pieces, outs = refs[: -len(segments)], refs[-len(segments) :]
    for out, group in zip(outs, segments):
        if any(copies > 1 for _, _, _, copies in group):
            out[...] = jnp.zeros_like(out)
    for k, piece in enumerate(pieces):
        owner = source_ref[0] ^ k
        for out, group in zip(outs, segments):
            for start, width, base, copies in group:
                at = pl.multiple_of(base + (owner // copies) * width, HEAD_SIZE)
                values = piece[:, start : start + width].astype(F32)
                if copies > 1:
                    values = values + out[:, pl.ds(at, width)]
                out[:, pl.ds(at, width)] = values


def join_pieces(source, pieces, segments):
    rows = pieces[0].shape[0]
    widths = [
        sum(width * len(pieces) // copies for _, width, _, copies in group) for group in segments
    ]
    whole = pl.BlockSpec(memory_space=pltpu.VMEM)
    return pl.pallas_call(
        lambda *refs: join_kernel(segments, *refs),
        out_shape=[jax.ShapeDtypeStruct((rows, width), F32) for width in widths],
        in_specs=[pl.BlockSpec(memory_space=pltpu.SMEM)] + [whole] * len(pieces),
        out_specs=[whole] * len(segments),
        name="join_pieces",
    )(source.astype(jnp.int32)[None], *pieces)


def head_columns(ref, head):
    return ref[:, head * HEAD_SIZE : (head + 1) * HEAD_SIZE]


def normalized(values):
    scale = lax.rsqrt(jnp.mean(values * values, axis=-1, keepdims=True) + EPS)
    return values * scale, scale


def rotated(normed, cosine, sine):
    return (normed * cosine + turn(normed) * sine).astype(BF16)


def row_blocks(length):
    step = min(length, 512)
    return [(at, step) for at in range(0, length, step)]


def forward_kernel(query_heads, key_heads, *refs):
    (projected, cosine_ref, sine_ref, column, row, query_gain, key_gain, attended, logs) = refs
    cosine, sine = cosine_ref[...], sine_ref[...]
    group = query_heads // key_heads
    scale = HEAD_SIZE ** (-0.5)
    length = projected.shape[0]
    for key_head in range(key_heads):
        key_hat, _ = normalized(head_columns(projected, query_heads + key_head))
        key = rotated(key_hat * key_gain[...], cosine, sine)
        value = head_columns(projected, query_heads + key_heads + key_head).astype(BF16)
        for head in range(key_head * group, (key_head + 1) * group):
            query_hat, _ = normalized(head_columns(projected, head))
            query = rotated(query_hat * query_gain[...], cosine, sine)
            for at, step in row_blocks(length):
                scores = rows_by_t(query[at : at + step], key) * scale
                allowed = row[...] <= column[at : at + step, :]
                scores = jnp.where(allowed, scores, MASK_FLOOR)
                peak = jnp.max(scores, axis=-1, keepdims=True)
                total = jnp.sum(jnp.exp(scores - peak), axis=-1, keepdims=True)
                log_total = peak + jnp.log(total)
                weights = jnp.exp(scores - log_total).astype(BF16)
                attended[at : at + step, head * HEAD_SIZE : (head + 1) * HEAD_SIZE] = rows_by(
                    weights, value
                ).astype(BF16)
                logs[at : at + step, head : head + 1] = log_total


def backward_kernel(query_heads, key_heads, *refs):
    (
        projected,
        cosine_ref,
        sine_ref,
        column,
        row,
        query_gain,
        key_gain,
        logs,
        attended,
        attended_grad,
        grad_projected,
        gain_parts,
    ) = refs
    cosine, sine = cosine_ref[...], sine_ref[...]
    group = query_heads // key_heads
    scale = HEAD_SIZE ** (-0.5)
    length = projected.shape[0]
    query_part = jnp.zeros((1, HEAD_SIZE), F32)
    key_part = jnp.zeros((1, HEAD_SIZE), F32)

    def finish(grad_rotary, hat, factor, gain):
        grad = grad_rotary * scale
        unrotated = grad * cosine - turn(grad) * sine
        part = jnp.sum(unrotated * hat, axis=0, keepdims=True)
        grad_hat = unrotated * gain
        inner = jnp.mean(grad_hat * hat, axis=-1, keepdims=True)
        return (factor * (grad_hat - hat * inner)).astype(BF16), part

    def store(head, values):
        grad_projected[:, head * HEAD_SIZE : (head + 1) * HEAD_SIZE] = values

    for key_head in range(key_heads):
        key_hat, key_scale = normalized(head_columns(projected, query_heads + key_head))
        key = rotated(key_hat * key_gain[...], cosine, sine)
        value = head_columns(projected, query_heads + key_heads + key_head).astype(BF16)
        key_acc = jnp.zeros((length, HEAD_SIZE), F32)
        value_acc = jnp.zeros((length, HEAD_SIZE), F32)
        for head in range(key_head * group, (key_head + 1) * group):
            query_hat, query_scale = normalized(head_columns(projected, head))
            query = rotated(query_hat * query_gain[...], cosine, sine)
            grad = head_columns(attended_grad, head)
            delta = jnp.sum(
                grad.astype(F32) * head_columns(attended, head).astype(F32), axis=-1, keepdims=True
            )
            query_accs = []
            for at, step in row_blocks(length):
                rows = slice(at, at + step)
                scores = rows_by_t(query[rows], key) * scale
                allowed = row[...] <= column[rows, :]
                scores = jnp.where(allowed, scores, MASK_FLOOR)
                probs = jnp.exp(scores - logs[rows, head : head + 1])
                grad_probs = rows_by_t(grad[rows], value)
                grad_scores = (probs * (grad_probs - delta[rows])).astype(BF16)
                query_accs.append(rows_by(grad_scores, key))
                key_acc = key_acc + t_by_rows(grad_scores, query[rows])
                value_acc = value_acc + t_by_rows(probs.astype(BF16), grad[rows])
            query_acc = jnp.concatenate(query_accs, axis=0)
            grads, part = finish(query_acc, query_hat, query_scale, query_gain[...])
            query_part = query_part + part
            store(head, grads)
        grads, part = finish(key_acc, key_hat, key_scale, key_gain[...])
        key_part = key_part + part
        store(query_heads + key_head, grads)
        store(query_heads + key_heads + key_head, value_acc.astype(BF16))
    gain_parts[0:1, :] = query_part
    gain_parts[1:2, :] = key_part


def attention_call(kernel, heads, operands, outs):
    whole = pl.BlockSpec(memory_space=pltpu.VMEM)
    return pl.pallas_call(
        lambda *refs: kernel(*heads, *refs),
        out_shape=outs,
        in_specs=[whole] * len(operands),
        out_specs=[whole] * len(outs),
    )(*operands)


def weight_grad_kernel(left, right, out, turned):
    @pl.when(pl.program_id(0) == 0)
    def _():
        turned[...] = left[...].T

    out[...] = rows_by(turned[...], right[...]).astype(BF16)


def weight_grad(left, right):
    length, depth = left.shape
    width = right.shape[1]
    tile = HEAD_SIZE * 4 if width % (HEAD_SIZE * 4) == 0 else HEAD_SIZE
    return pl.pallas_call(
        weight_grad_kernel,
        grid=(width // tile,),
        out_shape=jax.ShapeDtypeStruct((depth, width), BF16),
        in_specs=[
            pl.BlockSpec((length, depth), lambda j: (0, 0), pipeline_mode=pl.Buffered(1)),
            pl.BlockSpec((length, tile), lambda j: (0, j)),
        ],
        out_specs=pl.BlockSpec((depth, tile), lambda j: (0, j)),
        scratch_shapes=[pltpu.VMEM((depth, length), BF16)],
        name="weight_grad",
    )(left, right)


def local(
    inputs,
    block_index,
    attention_gain,
    query_norm_gain,
    key_gain,
    feedforward_gain,
    attention_in,
    attention_out,
    gate_up,
    down_weight,
    grad_output,
):
    parts = lax.axis_size("ctx")
    me = lax.axis_index("ctx")
    tokens = inputs.shape[1]
    half_rows = tokens // 2
    length = tokens * parts
    query_heads = QUERY_HEADS // parts
    key_heads = max(1, KEY_VALUE_HEADS // parts)
    copies = key_heads * parts // KEY_VALUE_HEADS
    query_width = query_heads * HEAD_SIZE
    key_width = key_heads * HEAD_SIZE
    all_query = QUERY_HEADS * HEAD_SIZE
    all_key = KEY_VALUE_HEADS * HEAD_SIZE
    hidden_width = FF // parts

    in_width = query_width + 2 * key_width
    own_key = (me // copies) * key_width
    picked_attention = pick_columns(
        [attention_in, attention_out],
        [
            (0, me * query_width, query_width),
            (0, all_query + own_key, key_width),
            (0, all_query + all_key + own_key, key_width),
        ]
        + [(1, (me ^ j) * query_width, query_width) for j in range(parts)],
    )
    weight_attention = gather_plane(picked_attention)
    weight_in = weight_attention[:, :in_width]
    weight_out = weight_attention[:, in_width:]
    own_inputs = inputs[0]
    sequence_inputs = gather_ctx(own_inputs)
    blocks = gather_ctx(block_index[0]).reshape(-1)
    picked_ff = pick_columns(
        [gate_up, down_weight],
        [
            (0, me * hidden_width, hidden_width),
            (0, FF + me * hidden_width, hidden_width),
            (1, me * hidden_width, hidden_width),
        ],
    )
    weight_ff = gather_plane(picked_ff)
    own_grad = grad_output[0]
    later_grad, _ = lax.optimization_barrier((own_grad, sequence_inputs))
    sequence_grad = gather_ctx(later_grad)

    steps_along = jnp.arange(half_rows, dtype=jnp.int32)
    positions = (blocks[:, None] * half_rows + steps_along[None, :]).reshape(-1)
    cosine_table, sine_table = rope_tables(positions)

    rows = sequence_inputs.astype(F32)
    first_scale = rms_scale(rows)
    first_hat = rows * first_scale
    first_normed = (first_hat * attention_gain).astype(BF16)
    projected = rows_by(first_normed, weight_in)
    heads = (query_heads, key_heads)
    shared = [
        projected,
        cosine_table,
        sine_table,
        positions[:, None],
        positions[None, :],
        query_norm_gain[None],
        key_gain[None],
    ]
    attended, logs = attention_call(
        forward_kernel,
        heads,
        shared,
        [
            jax.ShapeDtypeStruct((length, query_width), BF16),
            jax.ShapeDtypeStruct((length, query_heads), F32),
        ],
    )

    all_attended = gather_heads(attended)
    middle = rows + rows_by_t(all_attended, weight_out)
    second_scale = rms_scale(middle)
    second_hat = middle * second_scale
    second_normed = (second_hat * feedforward_gain).astype(BF16)
    own_middle, own_second_hat = middle[:tokens], second_hat[:tokens]
    own_second_scale = second_scale[:tokens]

    weight_gate_up = weight_ff[:, : 2 * hidden_width]
    weight_down = weight_ff[:, 2 * hidden_width :]
    grad_hidden = rows_by(sequence_grad, weight_down)
    gate_values = rows_by(second_normed, weight_gate_up)
    gate = gate_values[:, :hidden_width]
    upward = gate_values[:, hidden_width:]
    sigmoid_gate = jax.nn.sigmoid(gate)
    silu_gate = gate * sigmoid_gate
    hidden = (silu_gate * upward).astype(BF16)
    grad_gate = grad_hidden * upward * sigmoid_gate * (1.0 + gate * (1.0 - sigmoid_gate))
    grad_upward = grad_hidden * silu_gate
    grad_gate_up = jnp.concatenate([grad_gate, grad_upward], axis=1).astype(BF16)
    partial_second = rows_by_t(grad_gate_up, weight_gate_up)
    grad_second = scatter_ctx(partial_second)
    gate_up_weight_grad = weight_grad(second_normed, grad_gate_up)
    down_weight_grad = weight_grad(sequence_grad, hidden)
    gate_up_pieces = scatter_weight(gate_up_weight_grad, scatter_plane)
    down_pieces = scatter_weight(down_weight_grad, scatter_plane_swaps)
    partial_output = rows_by_t(hidden, weight_down)

    feedforward_part = jnp.sum(grad_second * own_second_hat, axis=0)
    grad_middle = own_grad.astype(F32) + rms_back(
        grad_second, own_second_hat, own_second_scale, feedforward_gain
    )
    grad_middle_short = grad_middle.astype(BF16)
    own_attended_grad = rows_by(grad_middle_short, weight_out).astype(BF16)
    attended_grad = tokens_to_heads(own_attended_grad)
    middle_grad_rows = tokens_to_rows(grad_middle_short)
    out_weight_grad = weight_grad(middle_grad_rows, all_attended)
    out_weight_sum = scatter_plane_swaps(out_weight_grad)
    output_sum = scatter_ctx(partial_output)
    output = (own_middle + output_sum).astype(BF16)[None]
    grad_projected, gain_parts = attention_call(
        backward_kernel,
        heads,
        shared + [logs, attended, attended_grad],
        [
            jax.ShapeDtypeStruct((length, in_width), BF16),
            jax.ShapeDtypeStruct((2, HEAD_SIZE), F32),
        ],
    )
    partial_first = rows_by_t(grad_projected, weight_in)
    attention_part = jnp.sum(partial_first * first_hat, axis=0)
    grad_first = scatter_ctx(partial_first)
    in_weight_grad = weight_grad(first_normed, grad_projected)
    in_pieces = scatter_weight(in_weight_grad, scatter_plane_swaps)
    cores = lax.axis_size("fsdp")
    source = (me * cores + lax.axis_index("fsdp")) % parts
    (attention_in_grad,) = join_pieces(
        source,
        in_pieces,
        [
            [
                (0, query_width, 0, 1),
                (query_width, key_width, all_query, copies),
                (query_width + key_width, key_width, all_query + all_key, copies),
            ]
        ],
    )
    out_pieces = [
        out_weight_sum[:, j * query_width : (j + 1) * query_width] for j in range(parts)
    ]
    (attention_out_grad,) = join_pieces(me, out_pieces, [[(0, query_width, 0, 1)]])
    (gate_up_grad,) = join_pieces(
        source, gate_up_pieces, [[(0, hidden_width, 0, 1), (hidden_width, hidden_width, FF, 1)]]
    )
    (down_grad,) = join_pieces(source, down_pieces, [[(0, hidden_width, 0, 1)]])
    input_grad = grad_middle + rms_back(
        grad_first, first_hat[:tokens], first_scale[:tokens], attention_gain
    )
    input_grad = input_grad.astype(BF16)[None]
    gains = sum_everywhere(
        jnp.concatenate([attention_part, gain_parts.reshape(-1), feedforward_part]),
    )
    marks = [D, D + HEAD_SIZE, D + 2 * HEAD_SIZE]
    gain_sums = jnp.split(gains, marks)

    return (
        output,
        input_grad,
        gain_sums[0],
        gain_sums[1],
        gain_sums[2],
        gain_sums[3],
        attention_in_grad,
        attention_out_grad,
        gate_up_grad,
        down_grad,
    )


def solution(mesh):
    tokens = P(("seq", "fsdp"), "ctx", None)
    weight = P(("seq", "fsdp"), None)
    grad = P(("seq", "ctx", "fsdp"), None)
    in_specs = (tokens, tokens, P(), P(), P(), P(), weight, weight, weight, weight, tokens)
    out_specs = (tokens, tokens, P(), P(), P(), P(), grad, grad, grad, grad)
    return jax.shard_map(local, mesh=mesh, in_specs=in_specs, out_specs=out_specs, check_vma=False)
```

time: 868 us -> 601 us (0.69)
  the two profiles are of different devices: /device:TPU:0 before, /device:TPU:1 now
where the time goes in v2:
time: 601 us; the launch traced here: 598 us
  waiting for transfers between devices  242 us (40%)
  starting transfers between devices  130 us (22%)
  Pallas kernels  70.9 us (12%)
  matrix products  66.6 us (11%)
  other arithmetic  38.1 us (6%)
  local copies, waits for them, and re-layouts  35.5 us (6%)
  between operations  14.8 us (2%)
    ppermute x46, waiting for transfers between devices, swap(): lax.ppermute(values, axis, [(i, i ^ step) for i in range(lax.axis_size(ax...  195 us
    ppermute x46, starting transfers between devices, swap(): lax.ppermute(values, axis, [(i, i ^ step) for i in range(lax.axis_size(ax...  99 us
    dot_general x4, matrix products, rows_by_t(): lax.dot_general(left, right, (((1,), (1,)), ((), ())), preferred_element_...  36.8 us
    pallas_call x4, Pallas kernels, weight_grad(): pl.pallas_call(weight_grad_kernel, grid=(width // tile,), out_shape=jax.S...  31.4 us
    ppermute x12, starting transfers between devices, scatter_weight(): pieces.append(lax.ppermute(piece, ('ctx', 'fsdp'), pairs))  31 us
    dot_general x4, matrix products, rows_by(): return jnp.dot(left, right, preferred_element_type=F32)  29.8 us
    ppermute x12, waiting for transfers between devices, scatter_weight(): pieces.append(lax.ppermute(piece, ('ctx', 'fsdp'), pairs))  24.8 us
    all_gather x2, waiting for transfers between devices, gather_plane(): return lax.all_gather(rows, PLANE, axis=0, tiled=True)  21.8 us
  transfers between devices with their start and end apart: 61, of which 18 were waited for; matrix products, arithmetic and copies ran while one was open for 18% of the time, Pallas kernels for 9%

profile of v2, /device:TPU:1, one launch (start us, length us, event | category | flops | bytes accessed | tf_op | source)
XLA Modules:
  0.0 597.6 jit_solution(15737407167946275634)
XLA Ops:
  23.5 30.3 %collective-permute-done.5 = s32[1,2]{1,0:T(1,128)S(1)} collective-permute-done((s32[1,2]{1,0:T(1,128)S(1)}, s32[1,2]{1,0:T(1,128)S(1)}, u32[]{:S(2)}, u32[]{:S(2)}) %collective-permute-start.5) | collective-permute-done | bytes 40 | tf_op jit(solution)/shard_map/ppermute | solution.py:61
  53.8 10.9 %collective-permute-start.3 = (s32[1,2]{1,0:T(1,128)S(1)}, s32[1,2]{1,0:T(1,128)S(1)}, u32[]{:S(2)}, u32[]{:S(2)}) collective-permute-start(s32[1,2]{1,0:T(1,128)S(1)} %bitcast.125), channel_id=1, source_target_pairs={{0,2},{2,0},{4,6},{6,4},{1,3},{3,1},{5,7},{7,5},{8,10},{10,8},{12,... | collective-permute-start | bytes 32 | tf_op jit(solution)/shard_map/ppermute | solution.py:61
  92.3 10.7 %shard_map.186 = (bf16[512,512]{1,0:T(8,128)(2,1)}, f32[512,4]{1,0:T(8,128)}) custom-call(f32[512,1024]{1,0:T(8,128)} %fusion.15.refs_0_, f32[512,128]{1,0:T(8,128)} %get-tuple-element.109.refs_1_, f32[512,128]{1,0:T(8,128)} %get-tuple-element.110.refs_2_, s32[512,1]{1,0:T(8,128)} %add.395.refs_3_, s32[1,512]{1,0:T(1,128)} %add.319.refs_4_, ...), custom_call_target="tpu_custom_call" | custom-call | tf_op jit(solution)/shard_map/pallas_call | solution.py:367
  111.1 14.8 %collective-permute-done.6.refs_1_ = bf16[512,512]{1,0:T(8,128)(2,1)} collective-permute-done((bf16[512,512]{1,0:T(8,128)(2,1)}, bf16[512,512]{1,0:T(8,128)(2,1)}, u32[]{:S(2)}, u32[]{:S(2)}) %collective-permute-start.6) | collective-permute-done | bytes 524320 | tf_op jit(solution)/shard_map/ppermute | solution.py:61
  125.9 28.8 %collective-permute-done.7.refs_2_ = bf16[512,512]{1,0:T(8,128)(2,1)} collective-permute-done((bf16[512,512]{1,0:T(8,128)(2,1)}, bf16[512,512]{1,0:T(8,128)(2,1)}, u32[]{:S(2)}, u32[]{:S(2)}) %collective-permute-start.7) | collective-permute-done | bytes 524320 | tf_op jit(solution)/shard_map/ppermute | solution.py:61
  157.7 8.1 %multiply_reduce_fusion.1 = (f32[512]{0:T(512)S(1)}, f32[512,2048]{1,0:T(8,128)S(1)}) fusion(bf16[512,2048]{1,0:T(8,128)(2,1)} %join_heads.1.right, bf16[2048,3072]{1,0:T(8,128)(2,1)} %all-gather.3.cloned.1.call-done, bf16[512,2048]{1,0:T(8,128)(2,1)S(1)} %get-tuple-element.32), kind=kOutput, calls=%fused_computation.20 | convolution fusion | flops 4299161088 | bytes 16779264 | tf_op jit(solution)/shard_map/dot_general | solution.py:53
  171.0 15.8 %all-gather.5.cloned.1.call-done = bf16[2048,4608]{1,0:T(8,128)(2,1)} async-done(((bf16[256,4608]{1,0:T(8,128)(2,1)}), bf16[2048,4608]{1,0:T(8,128)(2,1)}) %all-gather.5.cloned.1.call-update) | async-done | bytes 18874384 | tf_op jit(solution)/shard_map/all_gather | solution.py:70
  186.9 10.2 %fusion.2 = f32[512,3072]{1,0:T(8,128)S(1)} fusion(bf16[512,2048]{1,0:T(8,128)(2,1)} %get-tuple-element.29.left, bf16[2048,4608]{1,0:T(8,128)(2,1)} %all-gather.5.cloned.1.call-done), kind=kOutput, calls=%fused_computation.2 | convolution fusion | flops 6442450944 | bytes 20971520 | tf_op jit(solution)/shard_map/dot_general | solution.py:49
  197.1 8.3 %multiply_convert_fusion.3 = (bf16[512,1536]{1,0:T(8,128)(2,1)S(1)}, bf16[512,1536]{1,0:T(8,128)(2,1)S(1)}, bf16[512,1536]{1,0:T(8,128)(2,1)}) fusion(f32[512,3072]{1,0:T(8,128)S(1)} %fusion.2, bf16[512,2048]{1,0:T(8,128)(2,1)S(1)} %copy-done.7, bf16[2048,4608]{1,0:T(8,128)(2,1)} %all-gather.5.cloned.1.call-done), kind=kOutput, calls=%fused_computation.29 | convolution fusion | flops 3233021952 | bytes 19398656 | tf_op jit(solution)/shard_map/dot_general | solution.py:49
  209.2 11.9 %weight_grad.6 = bf16[2048,3072]{1,0:T(8,128)(2,1)} custom-call(bf16[512,2048]{1,0:T(8,128)(2,1)} %get-tuple-element.29.left, bf16[512,3072]{1,0:T(8,128)(2,1)} %pad_maximum_fusion.right), custom_call_target="tpu_custom_call" | custom-call | tf_op jit(solution)/shard_map/weight_grad/pallas_call | solution.py:387
  221.4 11.9 %fusion.58 = (bf16[512,2048]{1,0:T(8,128)(2,1)S(1)}, f32[512,2048]{1,0:T(8,128)}) fusion(bf16[2048,4608]{1,0:T(8,128)(2,1)} %all-gather.5.cloned.1.call-done, bf16[512,1536]{1,0:T(8,128)(2,1)} %copy-done.10, bf16[512,1536]{1,0:T(8,128)(2,1)} %copy-done.9), kind=kOutput, calls=%fused_computation.145 | convolution fusion | flops 6449790976 | bytes 22020096 | tf_op jit(solution)/shard_map/dot_general | solution.py:53
  238.1 8.5 %fusion.57 = (bf16[512,2048]{1,0:T(8,128)(2,1)S(1)}, f32[512,2048]{1,0:T(8,128)}) fusion(bf16[512,1536]{1,0:T(8,128)(2,1)S(1)} %copy-done.8, bf16[2048,4608]{1,0:T(8,128)(2,1)} %all-gather.5.cloned.1.call-done), kind=kOutput, calls=%fused_computation.144 | convolution fusion | flops 3222274048 | bytes 14155776 | tf_op jit(solution)/shard_map/dot_general | solution.py:53
  247.8 8.1 %weight_grad.7 = bf16[2048,1536]{1,0:T(8,128)(2,1)} custom-call(bf16[512,2048]{1,0:T(8,128)(2,1)} %constant_dynamic-update-slice_fusion.left, bf16[512,1536]{1,0:T(8,128)(2,1)} %get-tuple-element.35.right), custom_call_target="tpu_custom_call" | custom-call | tf_op jit(solution)/shard_map/weight_grad/pallas_call | solution.py:387
  263.0 8.7 %collective-permute-start.9 = (bf16[128,2048]{1,0:T(8,128)(2,1)S(1)}, bf16[128,2048]{1,0:T(8,128)(2,1)S(1)}, u32[]{:S(2)}, u32[]{:S(2)}) collective-permute-start(bf16[128,2048]{1,0:T(8,128)(2,1)S(1)} %copy-done.13), channel_id=1, source_target_pairs={{0,2},{2,0},{4,6},{6,4},{1,3},{3,1},{5,7},{7,5},{8,10},{10,8},{12,... | collective-permute-start | bytes 1572872 | tf_op jit(solution)/shard_map/ppermute | solution.py:61
  271.7 33.3 %collective-permute-done.16 = bf16[128,2048]{1,0:T(8,128)(2,1)S(1)} collective-permute-done((bf16[128,2048]{1,0:T(8,128)(2,1)}, bf16[128,2048]{1,0:T(8,128)(2,1)S(1)}, u32[]{:S(2)}, u32[]{:S(2)}) %collective-permute-start.16) | collective-permute-done | bytes 524320 | tf_op jit(solution)/shard_map/ppermute | solution.py:61
  317.5 15.6 %collective-permute-done.10 = bf16[128,2048]{1,0:T(8,128)(2,1)S(1)} collective-permute-done((bf16[128,2048]{1,0:T(8,128)(2,1)}, bf16[128,2048]{1,0:T(8,128)(2,1)S(1)}, u32[]{:S(2)}, u32[]{:S(2)}) %collective-permute-start.10) | collective-permute-done | bytes 524320 | tf_op jit(solution)/shard_map/ppermute | solution.py:61
  344.1 9.1 %shard_map.187 = (bf16[512,1024]{1,0:T(8,128)(2,1)}, f32[2,128]{1,0:T(2,128)}) custom-call(f32[512,1024]{1,0:T(8,128)} %fusion.15.refs_0_, f32[512,128]{1,0:T(8,128)} %get-tuple-element.109.refs_1_, f32[512,128]{1,0:T(8,128)} %get-tuple-element.110.refs_2_, s32[512,1]{1,0:T(8,128)} %add.395.refs_3_, s32[1,512]{1,0:T(1,128)} %add.319.refs_4_, ...), custom_call_target="tpu_custom_call" | custom-call | tf_op jit(solution)/shard_map/pallas_call | solution.py:367
  353.2 8.2 %multiply_reduce_fusion = (f32[2048]{0:T(1024)S(1)}, bf16[512,2048]{1,0:T(8,128)(2,1)S(1)}, f32[512,2048]{1,0:T(8,128)}, f32[512,2048]{1,0:T(8,128)}) fusion(f32[512]{0:T(512)} %copy-done.33, bf16[512,2048]{1,0:T(8,128)(2,1)S(1)} %get-tuple-element.32, bf16[512,1024]{1,0:T(8,128)(2,1)} %get-tuple-element.18.right, ...), kind=kOutput, calls=%fused_computation.18 | convolution fusion | flops 2152724480 | bytes 17836032 | tf_op jit(solution)/shard_map/dot_general | solution.py:53
  395.5 25.6 %collective-permute-start.21 = (bf16[128,2048]{1,0:T(8,128)(2,1)}, bf16[128,2048]{1,0:T(8,128)(2,1)S(1)}, u32[]{:S(2)}, u32[]{:S(2)}) collective-permute-start(bf16[128,2048]{1,0:T(8,128)(2,1)} %get-tuple-element.45), channel_id=1, source_target_pairs={{0,2},{2,0},{4,6},{6,4},{1,3},{3,1},{5,7},{7,5},{8,10},{10,8},{12,... | collective-permute-start | bytes 1572872 | tf_op jit(solution)/shard_map/ppermute | solution.py:61
  431.7 12.0 %collective-permute-done.21 = bf16[128,2048]{1,0:T(8,128)(2,1)S(1)} collective-permute-done((bf16[128,2048]{1,0:T(8,128)(2,1)}, bf16[128,2048]{1,0:T(8,128)(2,1)S(1)}, u32[]{:S(2)}, u32[]{:S(2)}) %collective-permute-start.21) | collective-permute-done | bytes 524320 | tf_op jit(solution)/shard_map/ppermute | solution.py:61
  469.5 9.7 %collective-permute-done.33 = bf16[256,1024]{1,0:T(8,128)(2,1)} collective-permute-done((bf16[256,1024]{1,0:T(8,128)(2,1)S(1)}, bf16[256,1024]{1,0:T(8,128)(2,1)}, u32[]{:S(2)}, u32[]{:S(2)}) %collective-permute-start.33) | collective-permute-done | bytes 524320 | tf_op jit(solution)/shard_map/ppermute | solution.py:61
  482.9 11.6 %collective-permute-done.53 = bf16[256,1536]{1,0:T(8,128)(2,1)S(1)} collective-permute-done((bf16[256,1536]{1,0:T(8,128)(2,1)S(1)}, bf16[256,1536]{1,0:T(8,128)(2,1)S(1)}, u32[]{:S(2)}, u32[]{:S(2)}) %collective-permute-start.53) | collective-permute-done | bytes 786464 | tf_op jit(solution)/shard_map/ppermute | solution.py:61
  495.7 17.0 %collective-permute-done.52 = bf16[256,1536]{1,0:T(8,128)(2,1)S(1)} collective-permute-done((bf16[256,1536]{1,0:T(8,128)(2,1)S(1)}, bf16[256,1536]{1,0:T(8,128)(2,1)S(1)}, u32[]{:S(2)}, u32[]{:S(2)}) %collective-permute-start.52) | collective-permute-done | bytes 786464 | tf_op jit(solution)/shard_map/ppermute | solution.py:61
  557.9 24.7 %collective-permute-done.57.refs_4_ = bf16[64,1536]{1,0:T(8,128)(2,1)S(1)} collective-permute-done((bf16[64,1536]{1,0:T(8,128)(2,1)}, bf16[64,1536]{1,0:T(8,128)(2,1)S(1)}, u32[]{:S(2)}, u32[]{:S(2)}) %collective-permute-start.57) | collective-permute-done | bytes 196640 | tf_op jit(solution)/shard_map/ppermute | solution.py:205
  (280 shorter events, 228.6 us)
Async XLA Ops:
  7.2 78.6 %all-gather.3.cloned.1.call-start = ((), (), s32[]{:S(2)}) async-start(), calls=%async_computation.1 | async-start | bytes 14155776 | tf_op jit(solution)/shard_map/all_gather | solution.py:70
  11.1 175.7 %all-gather.5.cloned.1.call-start = ((), (), s32[]{:S(2)}) async-start(), calls=%async_computation.2 | async-start | bytes 21233664 | tf_op jit(solution)/shard_map/all_gather | solution.py:70
  15.7 515.8 %reduce-scatter.2.cloned.1.call-start = ((), (), s32[]{:S(2)}) async-start(), calls=%async_computation.3 | async-start | bytes 14155776 | tf_op jit(solution)/shard_map/reduce_scatter | solution.py:169
  15.7 54.2 %collective-permute-start.2 = (bf16[128,2048]{1,0:T(8,128)(2,1)S(1)}, bf16[128,2048]{1,0:T(8,128)(2,1)S(1)}, u32[]{:S(2)}, u32[]{:S(2)}) collective-permute-start(bf16[128,2048]{1,0:T(8,128)(2,1)S(1)} %bitcast.113), channel_id=1, source_target_pairs={{0,6},{2,4},{4,2},{6,0},{1,7},{3,5},{5,3},{7,1},{8,14},{10,12},{12... | collective-permute-start | bytes 1572872 | tf_op jit(solution)/shard_map/ppermute | solution.py:61
  19.9 50.0 %collective-permute-start.1 = (bf16[128,2048]{1,0:T(8,128)(2,1)S(1)}, bf16[128,2048]{1,0:T(8,128)(2,1)S(1)}, u32[]{:S(2)}, u32[]{:S(2)}) collective-permute-start(bf16[128,2048]{1,0:T(8,128)(2,1)S(1)} %bitcast.114), channel_id=1, source_target_pairs={{0,4},{2,6},{4,0},{6,2},{1,5},{3,7},{5,1},{7,3},{8,12},{10,14},{12... | collective-permute-start | bytes 1572872 | tf_op jit(solution)/shard_map/ppermute | solution.py:61
  19.9 51.6 %collective-permute-start = (bf16[128,2048]{1,0:T(8,128)(2,1)S(1)}, bf16[128,2048]{1,0:T(8,128)(2,1)}, u32[]{:S(2)}, u32[]{:S(2)}) collective-permute-start(bf16[128,2048]{1,0:T(8,128)(2,1)S(1)} %bitcast.115), channel_id=1, source_target_pairs={{0,2},{2,0},{4,6},{6,4},{1,3},{3,1},{5,7},{7,5},{8,10},{10,8},{12,... | collective-permute-start | bytes 1572872 | tf_op jit(solution)/shard_map/ppermute | solution.py:61
  104.2 50.5 %collective-permute-start.7 = (bf16[512,512]{1,0:T(8,128)(2,1)}, bf16[512,512]{1,0:T(8,128)(2,1)}, u32[]{:S(2)}, u32[]{:S(2)}) collective-permute-start(bf16[512,512]{1,0:T(8,128)(2,1)} %get-tuple-element.15.refs_0_.refs_8_), channel_id=1, source_target_pairs={{0,4},{2,6},{4,0},{6,2},{1,5},{3,7},{5,1},{7,3},{8,12},{10,14},{12... | collective-permute-start | bytes 1572872 | tf_op jit(solution)/shard_map/ppermute | solution.py:61
  106.3 48.4 %collective-permute-start.8 = (bf16[512,512]{1,0:T(8,128)(2,1)}, bf16[512,512]{1,0:T(8,128)(2,1)}, u32[]{:S(2)}, u32[]{:S(2)}) collective-permute-start(bf16[512,512]{1,0:T(8,128)(2,1)} %get-tuple-element.15.refs_0_.refs_8_), channel_id=1, source_target_pairs={{0,6},{2,4},{4,2},{6,0},{1,7},{3,5},{5,3},{7,1},{8,14},{10,12},{12... | collective-permute-start | bytes 1572872 | tf_op jit(solution)/shard_map/ppermute | solution.py:61
  237.6 67.4 %collective-permute-start.16 = (bf16[128,2048]{1,0:T(8,128)(2,1)}, bf16[128,2048]{1,0:T(8,128)(2,1)S(1)}, u32[]{:S(2)}, u32[]{:S(2)}) collective-permute-start(bf16[128,2048]{1,0:T(8,128)(2,1)} %get-tuple-element.50), channel_id=1, source_target_pairs={{0,4},{2,6},{4,0},{6,2},{1,5},{3,7},{5,1},{7,3},{8,12},{10,14},{12... | collective-permute-start | bytes 1572872 | tf_op jit(solution)/shard_map/ppermute | solution.py:61
  237.6 69.4 %collective-permute-start.15 = (bf16[128,2048]{1,0:T(8,128)(2,1)}, bf16[128,2048]{1,0:T(8,128)(2,1)}, u32[]{:S(2)}, u32[]{:S(2)}) collective-permute-start(bf16[128,2048]{1,0:T(8,128)(2,1)} %get-tuple-element.48), channel_id=1, source_target_pairs={{0,2},{2,0},{4,6},{6,4},{1,3},{3,1},{5,7},{7,5},{8,10},{10,8},{12,... | collective-permute-start | bytes 1572872 | tf_op jit(solution)/shard_map/ppermute | solution.py:61
  255.9 61.3 %collective-permute-start.11 = (bf16[128,2048]{1,0:T(8,128)(2,1)}, bf16[128,2048]{1,0:T(8,128)(2,1)S(1)}, u32[]{:S(2)}, u32[]{:S(2)}) collective-permute-start(bf16[128,2048]{1,0:T(8,128)(2,1)} %get-tuple-element.52), channel_id=1, source_target_pairs={{0,6},{2,4},{4,2},{6,0},{1,7},{3,5},{5,3},{7,1},{8,14},{10,12},{12... | collective-permute-start | bytes 1572872 | tf_op jit(solution)/shard_map/ppermute | solution.py:61
  259.0 74.1 %collective-permute-start.10 = (bf16[128,2048]{1,0:T(8,128)(2,1)}, bf16[128,2048]{1,0:T(8,128)(2,1)S(1)}, u32[]{:S(2)}, u32[]{:S(2)}) collective-permute-start(bf16[128,2048]{1,0:T(8,128)(2,1)} %get-tuple-element.53), channel_id=1, source_target_pairs={{0,4},{2,6},{4,0},{6,2},{1,5},{3,7},{5,1},{7,3},{8,12},{10,14},{12... | collective-permute-start | bytes 1572872 | tf_op jit(solution)/shard_map/ppermute | solution.py:61
  263.0 70.1 %collective-permute-start.9 = (bf16[128,2048]{1,0:T(8,128)(2,1)S(1)}, bf16[128,2048]{1,0:T(8,128)(2,1)S(1)}, u32[]{:S(2)}, u32[]{:S(2)}) collective-permute-start(bf16[128,2048]{1,0:T(8,128)(2,1)S(1)} %copy-done.13), channel_id=1, source_target_pairs={{0,2},{2,0},{4,6},{6,4},{1,3},{3,1},{5,7},{7,5},{8,10},{10,8},{12,... | collective-permute-start | bytes 1572872 | tf_op jit(solution)/shard_map/ppermute | solution.py:61
  305.0 150.1 %collective-permute-start.50 = (bf16[4,256,1536]{2,1,0:T(8,128)(2,1)}, bf16[4,256,1536]{2,1,0:T(8,128)(2,1)}, u32[]{:S(2)}, u32[]{:S(2)}) collective-permute-start(bf16[4,256,1536]{2,1,0:T(8,128)(2,1)} %dynamic-slice_bitcast_fusion), channel_id=1, source_target_pairs={{0,1},{1,0},{2,3},{3,2},{4,5},{5,4},{6,7},{7,6},{8,9},{9,8},{10,11... | collective-permute-start | bytes 9437192 | tf_op jit(solution)/shard_map/ppermute | solution.py:61
  333.1 50.6 %collective-permute-start.41 = (bf16[128,512]{1,0:T(8,128)(2,1)S(1)}, bf16[128,512]{1,0:T(8,128)(2,1)}, u32[]{:S(2)}, u32[]{:S(2)}) collective-permute-start(bf16[128,512]{1,0:T(8,128)(2,1)S(1)} %pad_maximum_fusion.8), channel_id=1, source_target_pairs={{0,6},{2,4},{4,2},{6,0},{1,7},{3,5},{5,3},{7,1},{8,14},{10,12},{12... | collective-permute-start | bytes 393224 | tf_op jit(solution)/shard_map/ppermute | solution.py:61
  380.0 69.4 %collective-permute-start.31 = (bf16[4,256,1024]{2,1,0:T(8,128)(2,1)}, bf16[4,256,1024]{2,1,0:T(8,128)(2,1)}, u32[]{:S(2)}, u32[]{:S(2)}) collective-permute-start(bf16[4,256,1024]{2,1,0:T(8,128)(2,1)} %dynamic-slice_bitcast_fusion.1), channel_id=1, source_target_pairs={{0,1},{1,0},{2,3},{3,2},{4,5},{5,4},{6,7},{7,6},{8,9},{9,8},{10,11... | collective-permute-start | bytes 6291464 | tf_op jit(solution)/shard_map/ppermute | solution.py:61
  384.9 46.8 %collective-permute-start.22 = (bf16[128,2048]{1,0:T(8,128)(2,1)}, bf16[128,2048]{1,0:T(8,128)(2,1)S(1)}, u32[]{:S(2)}, u32[]{:S(2)}) collective-permute-start(bf16[128,2048]{1,0:T(8,128)(2,1)} %get-tuple-element.47), channel_id=1, source_target_pairs={{0,4},{2,6},{4,0},{6,2},{1,5},{3,7},{5,1},{7,3},{8,12},{10,14},{12... | collective-permute-start | bytes 1572872 | tf_op jit(solution)/shard_map/ppermute | solution.py:61
  395.5 48.2 %collective-permute-start.21 = (bf16[128,2048]{1,0:T(8,128)(2,1)}, bf16[128,2048]{1,0:T(8,128)(2,1)S(1)}, u32[]{:S(2)}, u32[]{:S(2)}) collective-permute-start(bf16[128,2048]{1,0:T(8,128)(2,1)} %get-tuple-element.45), channel_id=1, source_target_pairs={{0,2},{2,0},{4,6},{6,4},{1,3},{3,1},{5,7},{7,5},{8,10},{10,8},{12,... | collective-permute-start | bytes 1572872 | tf_op jit(solution)/shard_map/ppermute | solution.py:61
  459.7 53.1 %collective-permute-start.52 = (bf16[256,1536]{1,0:T(8,128)(2,1)S(1)}, bf16[256,1536]{1,0:T(8,128)(2,1)S(1)}, u32[]{:S(2)}, u32[]{:S(2)}) collective-permute-start(bf16[256,1536]{1,0:T(8,128)(2,1)S(1)} %get-tuple-element.40), channel_id=1, source_target_pairs={{0,16},{8,24},{16,0},{24,8},{1,17},{9,25},{17,1},{25,9},{2,18},{10... | collective-permute-start | bytes 2359304 | tf_op jit(solution)/shard_map/ppermute | solution.py:61
  466.5 48.5 %collective-permute-start.51 = (bf16[256,1536]{1,0:T(8,128)(2,1)S(1)}, bf16[256,1536]{1,0:T(8,128)(2,1)S(1)}, u32[]{:S(2)}, u32[]{:S(2)}) collective-permute-start(bf16[256,1536]{1,0:T(8,128)(2,1)S(1)} %get-tuple-element.38), channel_id=1, source_target_pairs={{0,8},{8,0},{16,24},{24,16},{1,9},{9,1},{17,25},{25,17},{2,10},{10... | collective-permute-start | bytes 2359304 | tf_op jit(solution)/shard_map/ppermute | solution.py:61
  535.5 50.3 %collective-permute-start.46 = (bf16[64,3072]{1,0:T(8,128)(2,1)}, bf16[64,3072]{1,0:T(8,128)(2,1)S(1)}, u32[]{:S(2)}, u32[]{:S(2)}) collective-permute-start(bf16[64,3072]{1,0:T(8,128)(2,1)} %get-tuple-element.57), channel_id=1, source_target_pairs={{0,0},{1,4},{2,1},{3,5},{4,2},{5,6},{6,3},{7,7},{8,8},{9,12},{10,9... | collective-permute-start | bytes 1179656 | tf_op jit(solution)/shard_map/ppermute | solution.py:205
  538.4 47.5 %collective-permute-start.47 = (bf16[64,3072]{1,0:T(8,128)(2,1)S(1)}, bf16[64,3072]{1,0:T(8,128)(2,1)S(1)}, u32[]{:S(2)}, u32[]{:S(2)}) collective-permute-start(bf16[64,3072]{1,0:T(8,128)(2,1)S(1)} %get-tuple-element.56), channel_id=1, source_target_pairs={{0,1},{1,5},{2,0},{3,4},{4,3},{5,7},{6,2},{7,6},{8,9},{9,13},{10,8... | collective-permute-start | bytes 1179656 | tf_op jit(solution)/shard_map/ppermute | solution.py:205
  540.7 45.1 %collective-permute-start.48 = (bf16[64,3072]{1,0:T(8,128)(2,1)S(1)}, bf16[64,3072]{1,0:T(8,128)(2,1)S(1)}, u32[]{:S(2)}, u32[]{:S(2)}) collective-permute-start(bf16[64,3072]{1,0:T(8,128)(2,1)S(1)} %get-tuple-element.55), channel_id=1, source_target_pairs={{0,2},{1,6},{2,3},{3,7},{4,0},{5,4},{6,1},{7,5},{8,10},{9,14},{10,... | collective-permute-start | bytes 1179656 | tf_op jit(solution)/shard_map/ppermute | solution.py:205
  542.9 43.0 %collective-permute-start.49 = (bf16[64,3072]{1,0:T(8,128)(2,1)S(1)}, bf16[64,3072]{1,0:T(8,128)(2,1)S(1)}, u32[]{:S(2)}, u32[]{:S(2)}) collective-permute-start(bf16[64,3072]{1,0:T(8,128)(2,1)S(1)} %get-tuple-element.54), channel_id=1, source_target_pairs={{0,3},{1,7},{2,2},{3,6},{4,1},{5,5},{6,0},{7,4},{8,11},{9,15},{10,... | collective-permute-start | bytes 1179656 | tf_op jit(solution)/shard_map/ppermute | solution.py:205
  (85 other events, 1572.4 us)
Sparse Core Ops, SparseCore 0:
  11.3 74.4 all-gather.2
  88.2 98.5 all-gather.4
  221.3 91.6 reduce-scatter.1

commit v3 on v2

--- a/solution.py
+++ b/solution.py
@@ -15,7 +15,6 @@
 EPS = 1e-06
 ROPE_BASE = 1000000.0
 MASK_FLOOR = -1e30
-PLANE = ("seq", "fsdp")
 F32 = jnp.float32
 BF16 = jnp.bfloat16
 
@@ -61,27 +60,48 @@
     return lax.ppermute(values, axis, [(i, i ^ step) for i in range(lax.axis_size(axis))])
 
 
+def slots(parts):
+    order = [0]
+    while len(order) < parts:
+        order = [2 * k for k in order] + [2 * k + 1 for k in order]
+    return order
+
+
 def gather_ctx(rows):
-    parts = lax.axis_size("ctx")
-    return jnp.concatenate([rows] + [swap(rows, "ctx", k) for k in range(1, parts)], axis=0)
-
-
-def gather_plane(rows):
-    return lax.all_gather(rows, PLANE, axis=0, tiled=True)
+    blocks = [rows if k == 0 else swap(rows, "ctx", k) for k in slots(lax.axis_size("ctx"))]
+    return jnp.concatenate(blocks, axis=0)
+
+
+def to_relative(rows):
+    seqs, cores = lax.axis_size("seq"), lax.axis_size("fsdp")
+    core = lax.axis_index("fsdp")
+    blocks = rows.reshape(rows.shape[0], seqs, cores, -1)
+    parts = [lax.dynamic_slice_in_dim(blocks, core ^ j, 1, axis=2)[:, :, 0] for j in range(cores)]
+    return jnp.concatenate(parts, axis=1).reshape(rows.shape)
+
+
+def from_relative(rows):
+    seqs, cores = lax.axis_size("seq"), lax.axis_size("fsdp")
+    core = lax.axis_index("fsdp")
+    blocks = rows.reshape(rows.shape[0], cores, seqs, -1)
+    parts = [lax.dynamic_slice_in_dim(blocks, core ^ j, 1, axis=1)[:, 0] for j in range(cores)]
+    return jnp.stack(parts, axis=2).reshape(rows.shape)
 
 
 def pick_kernel(picks, starts, *refs):
-    sources, out, sems = refs[:-2], refs[-2], refs[-1]
+    sources, upper, lower, sems = refs[:-3], refs[-3], refs[-2], refs[-1]
+    half = upper.shape[0]
     copies, at = [], 0
     for n, (source, width) in enumerate(picks):
         start = pl.multiple_of(starts[n], HEAD_SIZE)
-        copies.append(
-            pltpu.make_async_copy(
-                sources[source].at[:, pl.ds(start, width)],
-                out.at[:, pl.ds(at, width)],
-                sems.at[n],
+        for m, out in enumerate((upper, lower)):
+            copies.append(
+                pltpu.make_async_copy(
+                    sources[source].at[pl.ds(m * half, half), pl.ds(start, width)],
+                    out.at[:, pl.ds(at, width)],
+                    sems.at[2 * n + m],
+                )
             )
-        )
         at += width
     for copy in copies:
         copy.start()
@@ -90,26 +110,114 @@
 
 
 def pick_columns(sources, picks):
-    rows = sources[0].shape[0]
+    half = sources[0].shape[0] // 2
     starts = jnp.stack([jnp.asarray(start, jnp.int32) for _, start, _ in picks])
     anywhere = pl.BlockSpec(memory_space=pl.ANY)
+    shape = jax.ShapeDtypeStruct((half, sum(width for _, _, width in picks)), BF16)
     return pl.pallas_call(
         lambda *refs: pick_kernel([(source, width) for source, _, width in picks], *refs),
-        out_shape=jax.ShapeDtypeStruct((rows, sum(width for _, _, width in picks)), BF16),
+        out_shape=[shape, shape],
         in_specs=[pl.BlockSpec(memory_space=pltpu.SMEM)] + [anywhere] * len(sources),
-        out_specs=pl.BlockSpec(memory_space=pltpu.VMEM),
-        scratch_shapes=[pltpu.SemaphoreType.DMA((len(picks),))],
+        out_specs=[pl.BlockSpec(memory_space=pltpu.VMEM)] * 2,
+        scratch_shapes=[pltpu.SemaphoreType.DMA((2 * len(picks),))],
         name="pick_columns",
     )(starts, *sources)
 
 
+def assemble_kernel(widths, seq, *refs):
+    count = (len(refs) - 3 - len(widths)) // 2
+    uppers, lowers = refs[:count], refs[count : 2 * count]
+    outs, (held, in_sems, out_sems) = refs[2 * count : -3], refs[-3:]
+    half = uppers[0].shape[0]
+    loads = []
+    for k in range(count):
+        for m, pieces in enumerate((uppers, lowers)):
+            load = pltpu.make_async_copy(
+                pieces[k], held.at[k, pl.ds(m * half, half)], in_sems.at[2 * k + m]
+            )
+            load.start()
+            loads.append(load)
+    stores = []
+    for k in range(count):
+        loads[2 * k].wait()
+        loads[2 * k + 1].wait()
+        at = pl.multiple_of((seq[0] ^ k) * 2 * half, 2 * half)
+        column = 0
+        for n, (out, width) in enumerate(zip(outs, widths)):
+            store = pltpu.make_async_copy(
+                held.at[k, :, pl.ds(column, width)],
+                out.at[pl.ds(at, 2 * half)],
+                out_sems.at[len(widths) * k + n],
+            )
+            store.start()
+            stores.append(store)
+            column += width
+    for store in stores:
+        store.wait()
+
+
+def assemble(uppers, lowers, widths):
+    count = len(uppers)
+    half, width = uppers[0].shape
+    anywhere = pl.BlockSpec(memory_space=pl.ANY)
+    return pl.pallas_call(
+        lambda *refs: assemble_kernel(widths, *refs),
+        out_shape=[jax.ShapeDtypeStruct((2 * half * count, w), BF16) for w in widths],
+        in_specs=[pl.BlockSpec(memory_space=pltpu.SMEM)] + [anywhere] * (2 * count),
+        out_specs=[anywhere] * len(widths),
+        scratch_shapes=[
+            pltpu.VMEM((count, 2 * half, width), BF16),
+            pltpu.SemaphoreType.DMA((2 * count,)),
+            pltpu.SemaphoreType.DMA((len(widths) * count,)),
+        ],
+        name="asm",
+    )(lax.axis_index("seq").astype(jnp.int32)[None], *uppers, *lowers)
+
+
+def gather_plane(upper, lower, widths):
+    seqs, cores = lax.axis_size("seq"), lax.axis_size("fsdp")
+    bits = [1 << n for n in range(seqs.bit_length() - 1)]
+    gathered = []
+    for piece, order in ((upper, bits), (lower, bits[::-1])):
+        have = {0: piece}
+        for bit in order:
+            have.update({k ^ bit: swap(have[k], "seq", bit) for k in list(have)})
+        gathered.append([have[k] for k in range(seqs)])
+    wholes = assemble(*gathered, widths)
+    return [
+        [whole] + [swap(whole, "fsdp", j) for j in range(1, cores)] for whole in wholes
+    ]
+
+
+def times(rows, weights):
+    depth = weights[0].shape[0]
+    return sum(
+        rows_by(rows[:, j * depth : (j + 1) * depth], weight) for j, weight in enumerate(weights)
+    )
+
+
+def times_t(rows, weights):
+    return [rows_by_t(rows, weight) for weight in weights]
+
+
 def scatter_ctx(partials):
+    step = 1
+    while step < lax.axis_size("ctx"):
+        half = partials[0].shape[0] // 2
+        sent = jnp.concatenate([part[half:].astype(BF16) for part in partials], axis=1)
+        other = swap(sent, "ctx", step)
+        partials = [jnp.concatenate([part[:half] for part in partials], axis=1) + other.astype(F32)]
+        step *= 2
+    return partials[0]
+
+
+def scatter_ctx_direct(partials):
     parts = lax.axis_size("ctx")
     tokens = partials.shape[0] // parts
-    pieces = [
-        swap(partials[k * tokens : (k + 1) * tokens].astype(BF16), "ctx", k)
-        for k in range(1, parts)
-    ]
+    pieces = []
+    for at, slot in enumerate(slots(parts)[1:], 1):
+        piece = partials[at * tokens : (at + 1) * tokens].astype(BF16)
+        pieces.append(swap(piece, "ctx", slot))
     total = partials[:tokens]
     for piece in pieces:
         total = total + piece.astype(F32)
@@ -126,47 +234,47 @@
         out_shape=jax.ShapeDtypeStruct((parts * tokens, parts * attended.shape[1]), BF16),
         in_specs=[whole] * parts,
         out_specs=whole,
-        name="join_heads",
+        name="jh",
     )(*pieces)
 
 
 def join_heads_kernel(tokens, *refs):
     pieces, out = refs[:-1], refs[-1]
     width = pieces[0].shape[1]
+    order = slots(len(pieces))
     for j, piece in enumerate(pieces):
-        for k in range(len(pieces)):
-            at = (k ^ j) * tokens
-            out[k * tokens : (k + 1) * tokens, j * width : (j + 1) * width] = piece[
-                at : at + tokens, :
+        for at, slot in enumerate(order):
+            there = order.index(slot ^ j) * tokens
+            out[at * tokens : (at + 1) * tokens, j * width : (j + 1) * width] = piece[
+                there : there + tokens, :
             ]
 
 
 def tokens_to_heads(rows):
     parts = lax.axis_size("ctx")
     width = rows.shape[1] // parts
-    pieces = [rows[:, :width]]
-    for k in range(1, parts):
-        pieces.append(swap(rows[:, k * width : (k + 1) * width], "ctx", k))
+    pieces = []
+    for k in slots(parts):
+        piece = rows[:, k * width : (k + 1) * width]
+        pieces.append(piece if k == 0 else swap(piece, "ctx", k))
     return jnp.concatenate(pieces, axis=0)
 
 
 def tokens_to_rows(rows):
-    seqs, ctxs = lax.axis_size("seq"), lax.axis_size("ctx")
-    me = lax.axis_index("ctx")
-    width = rows.shape[1] // (seqs * ctxs)
+    seqs, ctxs, cores = lax.axis_size("seq"), lax.axis_size("ctx"), lax.axis_size("fsdp")
+    me, core = lax.axis_index("ctx"), lax.axis_index("fsdp")
+    depth = rows.shape[1]
+    width, block = depth // (seqs * ctxs), depth // (seqs * cores)
     pieces = []
-    for k in range(ctxs):
+    for k in slots(ctxs):
+        first = (me ^ k) * width
+        start = ((first // block) ^ core) * (depth // cores) + first % block
         blocks = [
-            lax.dynamic_slice_in_dim(rows, (s * ctxs + (me ^ k)) * width, width, axis=1)
-            for s in range(seqs)
+            lax.dynamic_slice_in_dim(rows, start + s * block, width, axis=1) for s in range(seqs)
         ]
         piece = jnp.concatenate(blocks, axis=1)
         pieces.append(piece if k == 0 else swap(piece, "ctx", k))
     return jnp.concatenate(pieces, axis=0)
-
-
-def scatter_plane(grad):
-    return lax.psum_scatter(grad, PLANE, scatter_dimension=0, tiled=True)
 
 
 def scatter_plane_swaps(grad):
@@ -178,23 +286,63 @@
     def of_core(k):
         return lax.dynamic_slice_in_dim(grad, core ^ k, 1, axis=1)[:, 0]
 
+    others = []
+    for k in range(1, cores):
+        others.append(swap(of_core(k), "fsdp", k))
     total = of_core(0).astype(F32)
-    for k in range(1, cores):
-        other = swap(of_core(k), "fsdp", k)
+    for other in others:
         total = total + other.astype(F32)
-    out = lax.dynamic_slice_in_dim(total, seq, 1, axis=0)[0]
     short = total.astype(BF16)
+    others = []
     for k in range(1, seqs):
         piece = lax.dynamic_slice_in_dim(short, seq ^ k, 1, axis=0)[0]
-        other = swap(piece, "seq", k)
+        others.append(swap(piece, "seq", k))
+    out = lax.dynamic_slice_in_dim(total, seq, 1, axis=0)[0]
+    for other in others:
         out = out + other.astype(F32)
     return out.astype(BF16)
 
 
-def scatter_weight(grad, over_plane):
+def scatter_halves(halves):
+    seqs = lax.axis_size("seq")
+    seq = lax.axis_index("seq")
+    others = [swap(half, "fsdp", j) for j, half in enumerate(halves[1:], 1)]
+    total = halves[0].astype(F32)
+    for other in others:
+        total = total + other.astype(F32)
+    total = total.astype(BF16)
+    rows = total.shape[0] // seqs
+    bits = [1 << n for n in range(seqs.bit_length() - 1)]
+    states = []
+    for m in range(2):
+        at = [(seq ^ k) * rows + m * (rows // 2) for k in range(seqs)]
+        states.append(
+            {k: lax.dynamic_slice_in_dim(total, at[k], rows // 2, axis=0) for k in range(seqs)}
+        )
+    for phase in range(len(bits)):
+        for m, order in enumerate((bits, bits[::-1])):
+            state, bit = states[m], order[phase]
+            sent = [k for k in sorted(state) if k & bit]
+            piece = jnp.concatenate([state[k].astype(BF16) for k in sent], axis=0)
+            piece = swap(piece, "seq", bit)
+            last = phase + 1 == len(bits)
+            states[m] = {
+                k ^ bit: state[k ^ bit].astype(F32)
+                + piece[n * (rows // 2) : (n + 1) * (rows // 2)].astype(F32)
+                for n, k in enumerate(sent)
+            }
+            if not last:
+                states[m] = lax.optimization_barrier(states[m])
+    return jnp.concatenate([state[0].astype(BF16) for state in states], axis=0)
+
+
+def scatter_plane(grad):
+    return lax.psum_scatter(grad, ("fsdp", "seq"), scatter_dimension=0, tiled=True)
+
+
+def exchange(grad):
     ctxs, cores = lax.axis_size("ctx"), lax.axis_size("fsdp")
     ctx = lax.axis_index("ctx")
-    grad = over_plane(grad)
     rows = grad.shape[0] // ctxs
     pieces = []
     for k in range(ctxs):
@@ -204,6 +352,10 @@
         ]
         pieces.append(lax.ppermute(piece, ("ctx", "fsdp"), pairs))
     return pieces
+
+
+def scatter_weight(grad, over_plane):
+    return exchange(over_plane(grad))
 
 
 def sum_everywhere(values):
@@ -372,30 +524,66 @@
     )(*operands)
 
 
-def weight_grad_kernel(left, right, out, turned):
+def weight_grad_kernel(left, right, *refs):
+    outs, turned = refs[:-1], refs[-1]
+
     @pl.when(pl.program_id(0) == 0)
     def _():
         turned[...] = left[...].T
 
-    out[...] = rows_by(turned[...], right[...]).astype(BF16)
-
-
-def weight_grad(left, right):
+    rows = outs[0].shape[0]
+    for j, out in enumerate(outs):
+        out[...] = rows_by(turned[j * rows : (j + 1) * rows], right[...]).astype(BF16)
+
+
+def weight_grad(left, right, count=1):
     length, depth = left.shape
     width = right.shape[1]
     tile = HEAD_SIZE * 4 if width % (HEAD_SIZE * 4) == 0 else HEAD_SIZE
     return pl.pallas_call(
         weight_grad_kernel,
         grid=(width // tile,),
-        out_shape=jax.ShapeDtypeStruct((depth, width), BF16),
+        out_shape=[jax.ShapeDtypeStruct((depth // count, width), BF16)] * count,
         in_specs=[
             pl.BlockSpec((length, depth), lambda j: (0, 0), pipeline_mode=pl.Buffered(1)),
             pl.BlockSpec((length, tile), lambda j: (0, j)),
         ],
-        out_specs=pl.BlockSpec((depth, tile), lambda j: (0, j)),
+        out_specs=[pl.BlockSpec((depth // count, tile), lambda j: (0, j))] * count,
         scratch_shapes=[pltpu.VMEM((depth, length), BF16)],
         name="weight_grad",
     )(left, right)
+
+
+def weight_grad_sorted_kernel(cores, core, left, right, out, turned):
+    rows = turned.shape[0] // cores
+
+    @pl.when(pl.program_id(0) == 0)
+    def _():
+        for j in range(cores):
+            at = pl.multiple_of((core[0] ^ j) * rows, rows)
+            turned[pl.ds(at, rows)] = left[:, j * rows : (j + 1) * rows].T
+
+    out[...] = rows_by(turned[...], right[...]).astype(BF16)
+
+
+def weight_grad_sorted(left, right):
+    cores = lax.axis_size("fsdp")
+    length, depth = left.shape
+    width = right.shape[1]
+    tile = HEAD_SIZE * 4 if width % (HEAD_SIZE * 4) == 0 else HEAD_SIZE
+    return pl.pallas_call(
+        lambda *refs: weight_grad_sorted_kernel(cores, *refs),
+        grid=(width // tile,),
+        out_shape=jax.ShapeDtypeStruct((depth, width), BF16),
+        in_specs=[
+            pl.BlockSpec(memory_space=pltpu.SMEM),
+            pl.BlockSpec((length, depth), lambda t: (0, 0), pipeline_mode=pl.Buffered(1)),
+            pl.BlockSpec((length, tile), lambda t: (0, t)),
+        ],
+        out_specs=pl.BlockSpec((depth, tile), lambda t: (0, t)),
+        scratch_shapes=[pltpu.VMEM((depth, length), BF16)],
+        name="weight_grad",
+    )(lax.axis_index("fsdp").astype(jnp.int32)[None], left, right)
 
 
 def local(
@@ -411,7 +599,7 @@
     down_weight,
     grad_output,
 ):
-    parts = lax.axis_size("ctx")
+    parts, cores = lax.axis_size("ctx"), lax.axis_size("fsdp")
     me = lax.axis_index("ctx")
     tokens = inputs.shape[1]
     half_rows = tokens // 2
@@ -427,21 +615,28 @@
 
     in_width = query_width + 2 * key_width
     own_key = (me // copies) * key_width
-    picked_attention = pick_columns(
-        [attention_in, attention_out],
+    own_inputs = to_relative(inputs[0])
+    sequence_inputs = gather_ctx(own_inputs)
+    blocks = gather_ctx(block_index[0]).reshape(-1)
+    own_grad = to_relative(grad_output[0])
+    sequence_grad = gather_ctx(own_grad)
+    first_gain, second_gain = (
+        to_relative(gain[None])[0] for gain in (attention_gain, feedforward_gain)
+    )
+
+    picked_in = pick_columns(
+        [attention_in],
         [
             (0, me * query_width, query_width),
             (0, all_query + own_key, key_width),
             (0, all_query + all_key + own_key, key_width),
-        ]
-        + [(1, (me ^ j) * query_width, query_width) for j in range(parts)],
-    )
-    weight_attention = gather_plane(picked_attention)
-    weight_in = weight_attention[:, :in_width]
-    weight_out = weight_attention[:, in_width:]
-    own_inputs = inputs[0]
-    sequence_inputs = gather_ctx(own_inputs)
-    blocks = gather_ctx(block_index[0]).reshape(-1)
+        ],
+    )
+    (weight_in,) = gather_plane(*picked_in, [in_width])
+    picked_out = pick_columns(
+        [attention_out], [(0, (me ^ j) * query_width, query_width) for j in range(parts)]
+    )
+    (weight_out,) = gather_plane(*picked_out, [all_query])
     picked_ff = pick_columns(
         [gate_up, down_weight],
         [
@@ -450,10 +645,7 @@
             (1, me * hidden_width, hidden_width),
         ],
     )
-    weight_ff = gather_plane(picked_ff)
-    own_grad = grad_output[0]
-    later_grad, _ = lax.optimization_barrier((own_grad, sequence_inputs))
-    sequence_grad = gather_ctx(later_grad)
+    weight_gate_up, weight_down = gather_plane(*picked_ff, [2 * hidden_width, hidden_width])
 
     steps_along = jnp.arange(half_rows, dtype=jnp.int32)
     positions = (blocks[:, None] * half_rows + steps_along[None, :]).reshape(-1)
@@ -462,8 +654,8 @@
     rows = sequence_inputs.astype(F32)
     first_scale = rms_scale(rows)
     first_hat = rows * first_scale
-    first_normed = (first_hat * attention_gain).astype(BF16)
-    projected = rows_by(first_normed, weight_in)
+    first_normed = (first_hat * first_gain).astype(BF16)
+    projected = times(first_normed, weight_in)
     heads = (query_heads, key_heads)
     shared = [
         projected,
@@ -485,17 +677,15 @@
     )
 
     all_attended = gather_heads(attended)
-    middle = rows + rows_by_t(all_attended, weight_out)
+    middle = rows + jnp.concatenate(times_t(all_attended, weight_out), axis=1)
     second_scale = rms_scale(middle)
     second_hat = middle * second_scale
-    second_normed = (second_hat * feedforward_gain).astype(BF16)
+    second_normed = (second_hat * second_gain).astype(BF16)
     own_middle, own_second_hat = middle[:tokens], second_hat[:tokens]
     own_second_scale = second_scale[:tokens]
 
-    weight_gate_up = weight_ff[:, : 2 * hidden_width]
-    weight_down = weight_ff[:, 2 * hidden_width :]
-    grad_hidden = rows_by(sequence_grad, weight_down)
-    gate_values = rows_by(second_normed, weight_gate_up)
+    grad_hidden = times(sequence_grad, weight_down)
+    gate_values = times(second_normed, weight_gate_up)
     gate = gate_values[:, :hidden_width]
     upward = gate_values[:, hidden_width:]
     sigmoid_gate = jax.nn.sigmoid(gate)
@@ -504,26 +694,31 @@
     grad_gate = grad_hidden * upward * sigmoid_gate * (1.0 + gate * (1.0 - sigmoid_gate))
     grad_upward = grad_hidden * silu_gate
     grad_gate_up = jnp.concatenate([grad_gate, grad_upward], axis=1).astype(BF16)
-    partial_second = rows_by_t(grad_gate_up, weight_gate_up)
-    grad_second = scatter_ctx(partial_second)
-    gate_up_weight_grad = weight_grad(second_normed, grad_gate_up)
-    down_weight_grad = weight_grad(sequence_grad, hidden)
+    grad_second = jnp.concatenate(
+        [
+            scatter_ctx_direct(lax.optimization_barrier(rows_by_t(grad_gate_up, weight)))
+            for weight in weight_gate_up
+        ],
+        axis=1,
+    )
+    gate_up_weight_grad = weight_grad_sorted(second_normed, grad_gate_up)
+    down_weight_grad = weight_grad(sequence_grad, hidden, cores)
     gate_up_pieces = scatter_weight(gate_up_weight_grad, scatter_plane)
-    down_pieces = scatter_weight(down_weight_grad, scatter_plane_swaps)
-    partial_output = rows_by_t(hidden, weight_down)
+    down_pieces = scatter_weight(down_weight_grad, scatter_halves)
+    partial_output = times_t(hidden, weight_down)
 
     feedforward_part = jnp.sum(grad_second * own_second_hat, axis=0)
     grad_middle = own_grad.astype(F32) + rms_back(
-        grad_second, own_second_hat, own_second_scale, feedforward_gain
+        grad_second, own_second_hat, own_second_scale, second_gain
     )
     grad_middle_short = grad_middle.astype(BF16)
-    own_attended_grad = rows_by(grad_middle_short, weight_out).astype(BF16)
+    own_attended_grad = times(grad_middle_short, weight_out).astype(BF16)
     attended_grad = tokens_to_heads(own_attended_grad)
     middle_grad_rows = tokens_to_rows(grad_middle_short)
-    out_weight_grad = weight_grad(middle_grad_rows, all_attended)
+    (out_weight_grad,) = weight_grad(middle_grad_rows, all_attended)
     out_weight_sum = scatter_plane_swaps(out_weight_grad)
     output_sum = scatter_ctx(partial_output)
-    output = (own_middle + output_sum).astype(BF16)[None]
+    output = from_relative((own_middle + output_sum).astype(BF16))[None]
     grad_projected, gain_parts = attention_call(
         backward_kernel,
         heads,
@@ -533,12 +728,17 @@
             jax.ShapeDtypeStruct((2, HEAD_SIZE), F32),
         ],
     )
-    partial_first = rows_by_t(grad_projected, weight_in)
-    attention_part = jnp.sum(partial_first * first_hat, axis=0)
+    partial_first = times_t(grad_projected, weight_in)
+    depth = D // cores
+    attention_part = jnp.concatenate(
+        [
+            jnp.sum(part * first_hat[:, j * depth : (j + 1) * depth], axis=0)
+            for j, part in enumerate(partial_first)
+        ]
+    )
     grad_first = scatter_ctx(partial_first)
-    in_weight_grad = weight_grad(first_normed, grad_projected)
-    in_pieces = scatter_weight(in_weight_grad, scatter_plane_swaps)
-    cores = lax.axis_size("fsdp")
+    in_weight_grad = weight_grad(first_normed, grad_projected, cores)
+    in_pieces = scatter_weight(in_weight_grad, scatter_halves)
     source = (me * cores + lax.axis_index("fsdp")) % parts
     (attention_in_grad,) = join_pieces(
         source,
@@ -554,17 +754,26 @@
     out_pieces = [
         out_weight_sum[:, j * query_width : (j + 1) * query_width] for j in range(parts)
     ]
-    (attention_out_grad,) = join_pieces(me, out_pieces, [[(0, query_width, 0, 1)]])
+    (attention_out_grad,) = join_pieces(
+        me, out_pieces, [[(0, query_width, 0, 1)]])
     (gate_up_grad,) = join_pieces(
-        source, gate_up_pieces, [[(0, hidden_width, 0, 1), (hidden_width, hidden_width, FF, 1)]]
-    )
-    (down_grad,) = join_pieces(source, down_pieces, [[(0, hidden_width, 0, 1)]])
+        source,
+        gate_up_pieces, [[(0, hidden_width, 0, 1), (hidden_width, hidden_width, FF, 1)]]
+    )
+    (down_grad,) = join_pieces(
+        source, down_pieces, [[(0, hidden_width, 0, 1)]])
     input_grad = grad_middle + rms_back(
-        grad_first, first_hat[:tokens], first_scale[:tokens], attention_gain
-    )
-    input_grad = input_grad.astype(BF16)[None]
+        grad_first, first_hat[:tokens], first_scale[:tokens], first_gain
+    )
+    input_grad = from_relative(input_grad.astype(BF16))[None]
     gains = sum_everywhere(
-        jnp.concatenate([attention_part, gain_parts.reshape(-1), feedforward_part]),
+        jnp.concatenate(
+            [
+                from_relative(attention_part[None])[0],
+                gain_parts.reshape(-1),
+                from_relative(feedforward_part[None])[0],
+            ]
+        ),
     )
     marks = [D, D + HEAD_SIZE, D + 2 * HEAD_SIZE]
     gain_sums = jnp.split(gains, marks)

time: 601 us -> 672 us (1.12)
  waiting for transfers between devices: 242 us -> 309 us
  Pallas kernels: 70.9 us -> 86 us
  starting transfers between devices: 130 us -> 118 us
  other arithmetic: 38.1 us -> 47.7 us
  local copies, waits for them, and re-layouts: 35.5 us -> 28.2 us
  matrix products: 66.6 us -> 59.8 us
    ppermute x46 -> x71, waiting for transfers between devices: 195 us -> 283 us  [swap(): lax.ppermute(values, axis, [(i, i ^ step) for i in range(lax.axis_size(ax...]
    all_gather x2 -> x0, waiting for transfers between devices: 21.8 us -> none  [gather_plane(): return lax.all_gather(rows, PLANE, axis=0, tiled=True)]
    pallas_call x4 -> x7, Pallas kernels: 31.4 us -> 44.2 us  [the longest x3 18.7 us: weight_grad(): pl.pallas_call(weight_grad_kernel, grid=(width // tile,), out_shape=[jax....]
    ppermute x46 -> x71, starting transfers between devices: 99 us -> 89.8 us  [swap(): lax.ppermute(values, axis, [(i, i ^ step) for i in range(lax.axis_size(ax...]
    convert_element_type x2 -> x9, other arithmetic: 4.99 us -> 12.9 us  [the longest x2 5.91 us: scatter_halves(): total = total.astype(BF16)]
    squeeze x3 -> x1, local copies, waits for them, and re-layouts: 8.28 us -> 1.45 us  [of_core(): return lax.dynamic_slice_in_dim(grad, core ^ k, 1, axis=1)[:, 0]]
    dot_general x4 -> x8, matrix products: 36.8 us -> 32 us  [rows_by_t(): lax.dot_general(left, right, (((1,), (1,)), ((), ())), preferred_element_...]
    dot_general x4 -> x8, matrix products: 29.8 us -> 27.8 us  [rows_by(): return jnp.dot(left, right, preferred_element_type=F32)]
  transfers between devices with their start and end apart: 61 -> 84, of which waited for: 18 -> 32; matrix products, arithmetic and copies ran while one was open for 18% -> 17% of each run, Pallas kernels for 9% -> 10%
where the time goes in v3:
time: 672 us; the launch traced here: 664 us
  waiting for transfers between devices  309 us (46%)
  starting transfers between devices  118 us (18%)
  Pallas kernels  86 us (13%)
  matrix products  59.8 us (9%)
  other arithmetic  47.7 us (7%)
  local copies, waits for them, and re-layouts  28.2 us (4%)
  between operations  15.9 us (2%)
    ppermute x71, waiting for transfers between devices, swap(): lax.ppermute(values, axis, [(i, i ^ step) for i in range(lax.axis_size(ax...  283 us
    ppermute x71, starting transfers between devices, swap(): lax.ppermute(values, axis, [(i, i ^ step) for i in range(lax.axis_size(ax...  89.8 us
    dot_general x8, matrix products, rows_by_t(): lax.dot_general(left, right, (((1,), (1,)), ((), ())), preferred_element_...  32 us
    ppermute x12, starting transfers between devices, exchange(): pieces.append(lax.ppermute(piece, ('ctx', 'fsdp'), pairs))  27.9 us
    dot_general x8, matrix products, rows_by(): return jnp.dot(left, right, preferred_element_type=F32)  27.8 us
    ppermute x12, waiting for transfers between devices, exchange(): pieces.append(lax.ppermute(piece, ('ctx', 'fsdp'), pairs))  26.1 us
    pallas_call x2, Pallas kernels, attention_call(): pl.pallas_call(lambda *refs: kernel(*heads, *refs), out_shape=outs, in_sp...  19.8 us
    pallas_call x3, Pallas kernels, weight_grad(): pl.pallas_call(weight_grad_kernel, grid=(width // tile,), out_shape=[jax....  18.7 us
  transfers between devices with their start and end apart: 84, of which 32 were waited for; matrix products, arithmetic and copies ran while one was open for 17% of the time, Pallas kernels for 10%

profile of v3, /device:TPU:1, one launch (start us, length us, event | category | flops | bytes accessed | tf_op | source)
XLA Modules:
  0.0 664.0 jit_solution(8547244878957339699)
XLA Ops:
  35.4 22.5 %collective-permute-done.5.refs_4_ = bf16[128,1024]{1,0:T(8,128)(2,1)S(1)} collective-permute-done((bf16[128,1024]{1,0:T(8,128)(2,1)S(1)}, bf16[128,1024]{1,0:T(8,128)(2,1)S(1)}, u32[]{:S(2)}, u32[]{:S(2)}) %collective-permute-start.5) | collective-permute-done | bytes 262176 | tf_op jit(solution)/shard_map/ppermute | solution.py:60
  59.4 8.7 %collective-permute-done.16.refs_2_ = bf16[128,2048]{1,0:T(8,128)(2,1)S(1)} collective-permute-done((bf16[128,2048]{1,0:T(8,128)(2,1)}, bf16[128,2048]{1,0:T(8,128)(2,1)S(1)}, u32[]{:S(2)}, u32[]{:S(2)}) %collective-permute-start.16) | collective-permute-done | bytes 524320 | tf_op jit(solution)/shard_map/ppermute | solution.py:60
  69.6 9.8 %collective-permute-done.19.refs_6_ = bf16[128,2048]{1,0:T(8,128)(2,1)S(1)} collective-permute-done((bf16[128,2048]{1,0:T(8,128)(2,1)}, bf16[128,2048]{1,0:T(8,128)(2,1)S(1)}, u32[]{:S(2)}, u32[]{:S(2)}) %collective-permute-start.19) | collective-permute-done | bytes 524320 | tf_op jit(solution)/shard_map/ppermute | solution.py:60
  82.3 32.3 %collective-permute-done.18.refs_4_ = bf16[128,2048]{1,0:T(8,128)(2,1)S(1)} collective-permute-done((bf16[128,2048]{1,0:T(8,128)(2,1)S(1)}, bf16[128,2048]{1,0:T(8,128)(2,1)S(1)}, u32[]{:S(2)}, u32[]{:S(2)}) %collective-permute-start.18) | collective-permute-done | bytes 524320 | tf_op jit(solution)/shard_map/ppermute | solution.py:60
  119.5 14.1 %collective-permute-done.21.refs_8_ = bf16[128,2048]{1,0:T(8,128)(2,1)} collective-permute-done((bf16[128,2048]{1,0:T(8,128)(2,1)}, bf16[128,2048]{1,0:T(8,128)(2,1)}, u32[]{:S(2)}, u32[]{:S(2)}) %collective-permute-start.21) | collective-permute-done | bytes 524320 | tf_op jit(solution)/shard_map/ppermute | solution.py:60
  133.6 12.6 %collective-permute-start.9 = (bf16[1024,1024]{1,0:T(8,128)(2,1)}, bf16[1024,1024]{1,0:T(8,128)(2,1)}, u32[]{:S(2)}, u32[]{:S(2)}) collective-permute-start(bf16[1024,1024]{1,0:T(8,128)(2,1)} %asm.3), channel_id=1, source_target_pairs={{0,1},{1,0},{2,3},{3,2},{4,5},{5,4},{6,7},{7,6},{8,9},{9,8},{10,11... | collective-permute-start | bytes 6291464 | tf_op jit(solution)/shard_map/ppermute | solution.py:60
  154.3 7.7 %asm.5 = (bf16[1024,3072]{1,0:T(8,128)(2,1)}, bf16[1024,1536]{1,0:T(8,128)(2,1)}) custom-call(s32[1]{0:T(128)} %bitcast.6.refs_0_, bf16[128,4608]{1,0:T(8,128)(2,1)} %get-tuple-element.39.refs_1_, bf16[128,4608]{1,0:T(8,128)(2,1)} %collective-permute-done.23.refs_2_, bf16[128,4608]{1,0:T(8,128)(2,1)} %collective-permute-done.24.refs_3_, ...), custom_call_target="tpu_custom_call" | custom-call | tf_op jit(solution)/shard_map/asm/pallas_call | solution.py:163
  166.5 9.0 %collective-permute-done.1 = bf16[128,2048]{1,0:T(8,128)(2,1)S(1)} collective-permute-done((bf16[128,2048]{1,0:T(8,128)(2,1)S(1)}, bf16[128,2048]{1,0:T(8,128)(2,1)S(1)}, u32[]{:S(2)}, u32[]{:S(2)}) %collective-permute-start.1) | collective-permute-done | bytes 524320 | tf_op jit(solution)/shard_map/ppermute | solution.py:60
  175.9 28.6 %collective-permute-done = bf16[128,2048]{1,0:T(8,128)(2,1)S(1)} collective-permute-done((bf16[128,2048]{1,0:T(8,128)(2,1)S(1)}, bf16[128,2048]{1,0:T(8,128)(2,1)S(1)}, u32[]{:S(2)}, u32[]{:S(2)}) %collective-permute-start) | collective-permute-done | bytes 524320 | tf_op jit(solution)/shard_map/ppermute | solution.py:60
  216.9 10.7 %shard_map.186 = (bf16[512,512]{1,0:T(8,128)(2,1)}, f32[512,4]{1,0:T(8,128)}) custom-call(f32[512,1024]{1,0:T(8,128)} %convolution_add_fusion.3.refs_0_, f32[512,128]{1,0:T(8,128)} %get-tuple-element.178.refs_1_, f32[512,128]{1,0:T(8,128)} %get-tuple-element.179.refs_2_, s32[512,1]{1,0:T(8,128)} %add.571.refs_3_, s32[1,512]{1,0:T(1,128)} %add.467.refs_4_, ...), custom_call_target="tpu_custom_call" | custom-call | tf_op jit(solution)/shard_map/pallas_call | solution.py:519
  229.3 9.3 %collective-permute-done.34 = bf16[128,2048]{1,0:T(8,128)(2,1)} collective-permute-done((bf16[128,2048]{1,0:T(8,128)(2,1)S(1)}, bf16[128,2048]{1,0:T(8,128)(2,1)}, u32[]{:S(2)}, u32[]{:S(2)}) %collective-permute-start.34) | collective-permute-done | bytes 524320 | tf_op jit(solution)/shard_map/ppermute | solution.py:60
  239.2 11.1 %collective-permute-done.13.refs_1_ = bf16[512,512]{1,0:T(8,128)(2,1)S(1)} collective-permute-done((bf16[512,512]{1,0:T(8,128)(2,1)}, bf16[512,512]{1,0:T(8,128)(2,1)S(1)}, u32[]{:S(2)}, u32[]{:S(2)}) %collective-permute-start.13) | collective-permute-done | bytes 524320 | tf_op jit(solution)/shard_map/ppermute | solution.py:60
  254.9 21.0 %collective-permute-done.14.refs_2_ = bf16[512,512]{1,0:T(8,128)(2,1)S(1)} collective-permute-done((bf16[512,512]{1,0:T(8,128)(2,1)}, bf16[512,512]{1,0:T(8,128)(2,1)S(1)}, u32[]{:S(2)}, u32[]{:S(2)}) %collective-permute-start.14) | collective-permute-done | bytes 524320 | tf_op jit(solution)/shard_map/ppermute | solution.py:60
  316.5 12.0 %weight_grad.6 = bf16[2048,3072]{1,0:T(8,128)(2,1)} custom-call(s32[1]{0:T(128)} %bitcast.46.refs_0_, bf16[512,2048]{1,0:T(8,128)(2,1)} %copy-done.4, bf16[512,3072]{1,0:T(8,128)(2,1)} %pad_maximum_fusion.refs_2_), custom_call_target="tpu_custom_call" | custom-call | tf_op jit(solution)/shard_map/weight_grad/pallas_call | solution.py:574
  335.1 6.6 fusion.45
  344.2 10.8 %collective-permute-start.40 = (bf16[128,1024]{1,0:T(8,128)(2,1)}, bf16[128,1024]{1,0:T(8,128)(2,1)}, u32[]{:S(2)}, u32[]{:S(2)}) collective-permute-start(bf16[128,1024]{1,0:T(8,128)(2,1)} %get-tuple-element.113), channel_id=1, source_target_pairs={{0,2},{2,0},{4,6},{6,4},{1,3},{3,1},{5,7},{7,5},{8,10},{10,8},{12,... | collective-permute-start | bytes 786440 | tf_op jit(solution)/shard_map/ppermute | solution.py:60
  362.1 7.8 %weight_grad.7 = (bf16[1024,1536]{1,0:T(8,128)(2,1)}, bf16[1024,1536]{1,0:T(8,128)(2,1)}) custom-call(bf16[512,2048]{1,0:T(8,128)(2,1)} %constant_dynamic-update-slice_fusion.left, bf16[512,1536]{1,0:T(8,128)(2,1)} %copy-done.26), custom_call_target="tpu_custom_call" | custom-call | tf_op jit(solution)/shard_map/weight_grad/pallas_call | solution.py:543
  381.0 18.6 %collective-permute-done.38 = bf16[128,1024]{1,0:T(8,128)(2,1)S(1)} collective-permute-done((bf16[128,1024]{1,0:T(8,128)(2,1)S(1)}, bf16[128,1024]{1,0:T(8,128)(2,1)S(1)}, u32[]{:S(2)}, u32[]{:S(2)}) %collective-permute-start.38) | collective-permute-done | bytes 262176 | tf_op jit(solution)/shard_map/ppermute | solution.py:60
  399.6 14.0 %collective-permute-done.37 = bf16[128,1024]{1,0:T(8,128)(2,1)S(1)} collective-permute-done((bf16[128,1024]{1,0:T(8,128)(2,1)S(1)}, bf16[128,1024]{1,0:T(8,128)(2,1)S(1)}, u32[]{:S(2)}, u32[]{:S(2)}) %collective-permute-start.37) | collective-permute-done | bytes 262176 | tf_op jit(solution)/shard_map/ppermute | solution.py:60
  432.8 9.1 %shard_map.187 = (bf16[512,1024]{1,0:T(8,128)(2,1)}, f32[2,128]{1,0:T(2,128)}) custom-call(f32[512,1024]{1,0:T(8,128)} %convolution_add_fusion.3.refs_0_, f32[512,128]{1,0:T(8,128)} %get-tuple-element.178.refs_1_, f32[512,128]{1,0:T(8,128)} %get-tuple-element.179.refs_2_, s32[512,1]{1,0:T(8,128)} %add.571.refs_3_, s32[1,512]{1,0:T(1,128)} %add.467.refs_4_, ...), custom_call_target="tpu_custom_call" | custom-call | tf_op jit(solution)/shard_map/pallas_call | solution.py:519
  489.9 20.0 %collective-permute-done.45 = bf16[256,2048]{1,0:T(8,128)(2,1)S(1)} collective-permute-done((bf16[256,2048]{1,0:T(8,128)(2,1)S(1)}, bf16[256,2048]{1,0:T(8,128)(2,1)S(1)}, u32[]{:S(2)}, u32[]{:S(2)}) %collective-permute-start.45) | collective-permute-done | bytes 1048608 | tf_op jit(solution)/shard_map/ppermute | solution.py:60
  549.6 14.0 %collective-permute-done.77 = bf16[256,1536]{1,0:T(8,128)(2,1)S(1)} collective-permute-done((bf16[256,1536]{1,0:T(8,128)(2,1)S(1)}, bf16[256,1536]{1,0:T(8,128)(2,1)S(1)}, u32[]{:S(2)}, u32[]{:S(2)}) %collective-permute-start.77) | collective-permute-done | bytes 786464 | tf_op jit(solution)/shard_map/ppermute | solution.py:60
  582.6 10.7 %collective-permute-done.78 = bf16[128,1536]{1,0:T(8,128)(2,1)S(1)} collective-permute-done((bf16[128,1536]{1,0:T(8,128)(2,1)S(1)}, bf16[128,1536]{1,0:T(8,128)(2,1)S(1)}, u32[]{:S(2)}, u32[]{:S(2)}) %collective-permute-start.78) | collective-permute-done | bytes 393248 | tf_op jit(solution)/shard_map/ppermute | solution.py:60
  623.8 26.0 %collective-permute-done.82.refs_4_ = bf16[64,1536]{1,0:T(8,128)(2,1)S(1)} collective-permute-done((bf16[64,1536]{1,0:T(8,128)(2,1)}, bf16[64,1536]{1,0:T(8,128)(2,1)S(1)}, u32[]{:S(2)}, u32[]{:S(2)}) %collective-permute-start.82) | collective-permute-done | bytes 196640 | tf_op jit(solution)/shard_map/ppermute | solution.py:353
  (434 shorter events, 301.2 us)
Async XLA Ops:
  7.2 592.1 %reduce-scatter.2.cloned.1.call-start = ((), (), s32[]{:S(2)}) async-start(), calls=%async_computation.1 | async-start | bytes 14155776 | tf_op jit(solution)/shard_map/reduce_scatter | solution.py:340
  27.6 54.2 %collective-permute-start.23 = (bf16[128,4608]{1,0:T(8,128)(2,1)}, bf16[128,4608]{1,0:T(8,128)(2,1)}, u32[]{:S(2)}, u32[]{:S(2)}) collective-permute-start(bf16[128,4608]{1,0:T(8,128)(2,1)} %get-tuple-element.39.refs_1_), channel_id=1, source_target_pairs={{0,8},{8,0},{16,24},{24,16},{1,9},{9,1},{17,25},{25,17},{2,10},{10... | collective-permute-start | bytes 3538952 | tf_op jit(solution)/shard_map/ppermute | solution.py:60
  28.8 53.2 %collective-permute-start.27 = (bf16[128,4608]{1,0:T(8,128)(2,1)}, bf16[128,4608]{1,0:T(8,128)(2,1)}, u32[]{:S(2)}, u32[]{:S(2)}) collective-permute-start(bf16[128,4608]{1,0:T(8,128)(2,1)} %get-tuple-element.40.refs_5_), channel_id=1, source_target_pairs={{0,16},{8,24},{16,0},{24,8},{1,17},{9,25},{17,1},{25,9},{2,18},{10... | collective-permute-start | bytes 3538952 | tf_op jit(solution)/shard_map/ppermute | solution.py:60
  69.3 76.8 %collective-permute-start.24 = (bf16[128,4608]{1,0:T(8,128)(2,1)}, bf16[128,4608]{1,0:T(8,128)(2,1)}, u32[]{:S(2)}, u32[]{:S(2)}) collective-permute-start(bf16[128,4608]{1,0:T(8,128)(2,1)} %get-tuple-element.39.refs_1_), channel_id=1, source_target_pairs={{0,16},{8,24},{16,0},{24,8},{1,17},{9,25},{17,1},{25,9},{2,18},{10... | collective-permute-start | bytes 3538952 | tf_op jit(solution)/shard_map/ppermute | solution.py:60
  79.3 35.3 %collective-permute-start.18 = (bf16[128,2048]{1,0:T(8,128)(2,1)S(1)}, bf16[128,2048]{1,0:T(8,128)(2,1)S(1)}, u32[]{:S(2)}, u32[]{:S(2)}) collective-permute-start(bf16[128,2048]{1,0:T(8,128)(2,1)S(1)} %collective-permute-done.16.refs_2_), channel_id=1, source_target_pairs={{0,16},{8,24},{16,0},{24,8},{1,17},{9,25},{17,1},{25,9},{2,18},{10... | collective-permute-start | bytes 1572872 | tf_op jit(solution)/shard_map/ppermute | solution.py:60
  80.6 69.4 %collective-permute-start.26 = (bf16[128,4608]{1,0:T(8,128)(2,1)}, bf16[128,4608]{1,0:T(8,128)(2,1)}, u32[]{:S(2)}, u32[]{:S(2)}) collective-permute-start(bf16[128,4608]{1,0:T(8,128)(2,1)} %get-tuple-element.40.refs_5_), channel_id=1, source_target_pairs={{0,8},{8,0},{16,24},{24,16},{1,9},{9,1},{17,25},{25,17},{2,10},{10... | collective-permute-start | bytes 3538952 | tf_op jit(solution)/shard_map/ppermute | solution.py:60
  81.8 68.3 %collective-permute-start.25 = (bf16[128,4608]{1,0:T(8,128)(2,1)}, bf16[128,4608]{1,0:T(8,128)(2,1)}, u32[]{:S(2)}, u32[]{:S(2)}) collective-permute-start(bf16[128,4608]{1,0:T(8,128)(2,1)} %collective-permute-done.23.refs_2_), channel_id=1, source_target_pairs={{0,16},{8,24},{16,0},{24,8},{1,17},{9,25},{17,1},{25,9},{2,18},{10... | collective-permute-start | bytes 3538952 | tf_op jit(solution)/shard_map/ppermute | solution.py:60
  82.0 71.3 %collective-permute-start.28 = (bf16[128,4608]{1,0:T(8,128)(2,1)}, bf16[128,4608]{1,0:T(8,128)(2,1)}, u32[]{:S(2)}, u32[]{:S(2)}) collective-permute-start(bf16[128,4608]{1,0:T(8,128)(2,1)} %collective-permute-done.27.refs_7_), channel_id=1, source_target_pairs={{0,8},{8,0},{16,24},{24,16},{1,9},{9,1},{17,25},{25,17},{2,10},{10... | collective-permute-start | bytes 3538952 | tf_op jit(solution)/shard_map/ppermute | solution.py:60
  133.6 76.5 %collective-permute-start.9 = (bf16[1024,1024]{1,0:T(8,128)(2,1)}, bf16[1024,1024]{1,0:T(8,128)(2,1)}, u32[]{:S(2)}, u32[]{:S(2)}) collective-permute-start(bf16[1024,1024]{1,0:T(8,128)(2,1)} %asm.3), channel_id=1, source_target_pairs={{0,1},{1,0},{2,3},{3,2},{4,5},{5,4},{6,7},{7,6},{8,9},{9,8},{10,11... | collective-permute-start | bytes 6291464 | tf_op jit(solution)/shard_map/ppermute | solution.py:60
  150.1 54.4 %collective-permute-start = (bf16[128,2048]{1,0:T(8,128)(2,1)S(1)}, bf16[128,2048]{1,0:T(8,128)(2,1)S(1)}, u32[]{:S(2)}, u32[]{:S(2)}) collective-permute-start(bf16[128,2048]{1,0:T(8,128)(2,1)S(1)} %bitcast.117), channel_id=1, source_target_pairs={{0,4},{2,6},{4,0},{6,2},{1,5},{3,7},{5,1},{7,3},{8,12},{10,14},{12... | collective-permute-start | bytes 1572872 | tf_op jit(solution)/shard_map/ppermute | solution.py:60
  153.3 131.8 %collective-permute-start.22 = (bf16[1024,2048]{1,0:T(8,128)(2,1)}, bf16[1024,2048]{1,0:T(8,128)(2,1)}, u32[]{:S(2)}, u32[]{:S(2)}) collective-permute-start(bf16[1024,2048]{1,0:T(8,128)(2,1)} %asm.4), channel_id=1, source_target_pairs={{0,1},{1,0},{2,3},{3,2},{4,5},{5,4},{6,7},{7,6},{8,9},{9,8},{10,11... | collective-permute-start | bytes 12582920 | tf_op jit(solution)/shard_map/ppermute | solution.py:60
  162.0 138.3 %collective-permute-start.29 = (bf16[1024,3072]{1,0:T(8,128)(2,1)}, bf16[1024,3072]{1,0:T(8,128)(2,1)}, u32[]{:S(2)}, u32[]{:S(2)}) collective-permute-start(bf16[1024,3072]{1,0:T(8,128)(2,1)} %get-tuple-element.41), channel_id=1, source_target_pairs={{0,1},{1,0},{2,3},{3,2},{4,5},{5,4},{6,7},{7,6},{8,9},{9,8},{10,11... | collective-permute-start | bytes 18874376 | tf_op jit(solution)/shard_map/ppermute | solution.py:60
  175.5 52.1 %collective-permute-start.33 = (bf16[128,2048]{1,0:T(8,128)(2,1)S(1)}, bf16[128,2048]{1,0:T(8,128)(2,1)S(1)}, u32[]{:S(2)}, u32[]{:S(2)}) collective-permute-start(bf16[128,2048]{1,0:T(8,128)(2,1)S(1)} %bitcast.121), channel_id=1, source_target_pairs={{0,4},{2,6},{4,0},{6,2},{1,5},{3,7},{5,1},{7,3},{8,12},{10,14},{12... | collective-permute-start | bytes 1572872 | tf_op jit(solution)/shard_map/ppermute | solution.py:60
  238.6 56.9 %collective-permute-start.30 = (bf16[1024,1536]{1,0:T(8,128)(2,1)}, bf16[1024,1536]{1,0:T(8,128)(2,1)}, u32[]{:S(2)}, u32[]{:S(2)}) collective-permute-start(bf16[1024,1536]{1,0:T(8,128)(2,1)} %get-tuple-element.42), channel_id=1, source_target_pairs={{0,1},{1,0},{2,3},{3,2},{4,5},{5,4},{6,7},{7,6},{8,9},{9,8},{10,11... | collective-permute-start | bytes 9437192 | tf_op jit(solution)/shard_map/ppermute | solution.py:60
  239.2 36.8 %collective-permute-start.14 = (bf16[512,512]{1,0:T(8,128)(2,1)}, bf16[512,512]{1,0:T(8,128)(2,1)S(1)}, u32[]{:S(2)}, u32[]{:S(2)}) collective-permute-start(bf16[512,512]{1,0:T(8,128)(2,1)} %get-tuple-element.36.refs_0_.refs_8_), channel_id=1, source_target_pairs={{0,4},{2,6},{4,0},{6,2},{1,5},{3,7},{5,1},{7,3},{8,12},{10,14},{12... | collective-permute-start | bytes 1572872 | tf_op jit(solution)/shard_map/ppermute | solution.py:60
  369.9 116.9 %collective-permute-start.31 = (bf16[256,2048]{1,0:T(8,128)(2,1)}, bf16[256,2048]{1,0:T(8,128)(2,1)}, u32[]{:S(2)}, u32[]{:S(2)}) collective-permute-start(bf16[256,2048]{1,0:T(8,128)(2,1)} %pad_maximum_fusion.2), channel_id=1, source_target_pairs={{0,2},{2,0},{4,6},{6,4},{1,3},{3,1},{5,7},{7,5},{8,10},{10,8},{12,... | collective-permute-start | bytes 3145736 | tf_op jit(solution)/shard_map/ppermute | solution.py:60
  374.2 39.4 %collective-permute-start.37 = (bf16[128,1024]{1,0:T(8,128)(2,1)S(1)}, bf16[128,1024]{1,0:T(8,128)(2,1)S(1)}, u32[]{:S(2)}, u32[]{:S(2)}) collective-permute-start(bf16[128,1024]{1,0:T(8,128)(2,1)S(1)} %get-tuple-element.110), channel_id=1, source_target_pairs={{0,2},{2,0},{4,6},{6,4},{1,3},{3,1},{5,7},{7,5},{8,10},{10,8},{12,... | collective-permute-start | bytes 786440 | tf_op jit(solution)/shard_map/ppermute | solution.py:60
  374.2 39.4 %collective-permute-start.36 = (bf16[128,1024]{1,0:T(8,128)(2,1)S(1)}, bf16[128,1024]{1,0:T(8,128)(2,1)S(1)}, u32[]{:S(2)}, u32[]{:S(2)}) collective-permute-start(bf16[128,1024]{1,0:T(8,128)(2,1)S(1)} %get-tuple-element.108), channel_id=1, source_target_pairs={{0,4},{2,6},{4,0},{6,2},{1,5},{3,7},{5,1},{7,3},{8,12},{10,14},{12... | collective-permute-start | bytes 786440 | tf_op jit(solution)/shard_map/ppermute | solution.py:60
  376.9 160.3 %collective-permute-start.74 = (bf16[1024,1536]{1,0:T(8,128)(2,1)}, bf16[1024,1536]{1,0:T(8,128)(2,1)}, u32[]{:S(2)}, u32[]{:S(2)}) collective-permute-start(bf16[1024,1536]{1,0:T(8,128)(2,1)} %get-tuple-element.53), channel_id=1, source_target_pairs={{0,1},{1,0},{2,3},{3,2},{4,5},{5,4},{6,7},{7,6},{8,9},{9,8},{10,11... | collective-permute-start | bytes 9437192 | tf_op jit(solution)/shard_map/ppermute | solution.py:60
  477.7 53.8 %collective-permute-start.54 = (bf16[1024,1024]{1,0:T(8,128)(2,1)}, bf16[1024,1024]{1,0:T(8,128)(2,1)}, u32[]{:S(2)}, u32[]{:S(2)}) collective-permute-start(bf16[1024,1024]{1,0:T(8,128)(2,1)} %get-tuple-element.47), channel_id=1, source_target_pairs={{0,1},{1,0},{2,3},{3,2},{4,5},{5,4},{6,7},{7,6},{8,9},{9,8},{10,11... | collective-permute-start | bytes 6291464 | tf_op jit(solution)/shard_map/ppermute | solution.py:60
  604.4 48.6 %collective-permute-start.70 = (bf16[64,3072]{1,0:T(8,128)(2,1)}, bf16[64,3072]{1,0:T(8,128)(2,1)S(1)}, u32[]{:S(2)}, u32[]{:S(2)}) collective-permute-start(bf16[64,3072]{1,0:T(8,128)(2,1)} %get-tuple-element.104), channel_id=1, source_target_pairs={{0,0},{1,4},{2,1},{3,5},{4,2},{5,6},{6,3},{7,7},{8,8},{9,12},{10,9... | collective-permute-start | bytes 1179656 | tf_op jit(solution)/shard_map/ppermute | solution.py:353
  606.5 46.5 %collective-permute-start.71 = (bf16[64,3072]{1,0:T(8,128)(2,1)}, bf16[64,3072]{1,0:T(8,128)(2,1)}, u32[]{:S(2)}, u32[]{:S(2)}) collective-permute-start(bf16[64,3072]{1,0:T(8,128)(2,1)} %get-tuple-element.103), channel_id=1, source_target_pairs={{0,1},{1,5},{2,0},{3,4},{4,3},{5,7},{6,2},{7,6},{8,9},{9,13},{10,8... | collective-permute-start | bytes 1179656 | tf_op jit(solution)/shard_map/ppermute | solution.py:353
  608.4 44.5 %collective-permute-start.72 = (bf16[64,3072]{1,0:T(8,128)(2,1)}, bf16[64,3072]{1,0:T(8,128)(2,1)}, u32[]{:S(2)}, u32[]{:S(2)}) collective-permute-start(bf16[64,3072]{1,0:T(8,128)(2,1)} %get-tuple-element.102), channel_id=1, source_target_pairs={{0,2},{1,6},{2,3},{3,7},{4,0},{5,4},{6,1},{7,5},{8,10},{9,14},{10,... | collective-permute-start | bytes 1179656 | tf_op jit(solution)/shard_map/ppermute | solution.py:353
  610.5 42.5 %collective-permute-start.73 = (bf16[64,3072]{1,0:T(8,128)(2,1)}, bf16[64,3072]{1,0:T(8,128)(2,1)}, u32[]{:S(2)}, u32[]{:S(2)}) collective-permute-start(bf16[64,3072]{1,0:T(8,128)(2,1)} %get-tuple-element.101), channel_id=1, source_target_pairs={{0,3},{1,7},{2,2},{3,6},{4,1},{5,5},{6,0},{7,4},{8,11},{9,15},{10,... | collective-permute-start | bytes 1179656 | tf_op jit(solution)/shard_map/ppermute | solution.py:353
  (127 other events, 2632.4 us)
Sparse Core Ops, SparseCore 0:
  328.6 101.1 reduce-scatter.1

commit v4 on v3

--- a/solution.py
+++ b/solution.py
@@ -124,30 +124,25 @@
     )(starts, *sources)
 
 
-def assemble_kernel(widths, seq, *refs):
-    count = (len(refs) - 3 - len(widths)) // 2
-    uppers, lowers = refs[:count], refs[count : 2 * count]
-    outs, (held, in_sems, out_sems) = refs[2 * count : -3], refs[-3:]
-    half = uppers[0].shape[0]
+def assemble_kernel(places, widths, seq, *refs):
+    outs, (held, in_sems, out_sems) = refs[-3 - len(widths) : -3], refs[-3:]
+    pieces = refs[-3 - len(widths) - len(places) : -3 - len(widths)]
+    half = pieces[0].shape[0]
     loads = []
-    for k in range(count):
-        for m, pieces in enumerate((uppers, lowers)):
-            load = pltpu.make_async_copy(
-                pieces[k], held.at[k, pl.ds(m * half, half)], in_sems.at[2 * k + m]
-            )
-            load.start()
-            loads.append(load)
+    for n, piece in enumerate(pieces):
+        load = pltpu.make_async_copy(piece, held.at[n], in_sems.at[n])
+        load.start()
+        loads.append(load)
     stores = []
-    for k in range(count):
-        loads[2 * k].wait()
-        loads[2 * k + 1].wait()
-        at = pl.multiple_of((seq[0] ^ k) * 2 * half, 2 * half)
+    for n, (slot, m) in enumerate(places):
+        loads[n].wait()
+        at = pl.multiple_of((seq[0] ^ slot) * 2 * half + m * half, half)
         column = 0
-        for n, (out, width) in enumerate(zip(outs, widths)):
+        for w, (out, width) in enumerate(zip(outs, widths)):
             store = pltpu.make_async_copy(
-                held.at[k, :, pl.ds(column, width)],
-                out.at[pl.ds(at, 2 * half)],
-                out_sems.at[len(widths) * k + n],
+                held.at[n, :, pl.ds(column, width)],
+                out.at[pl.ds(at, half)],
+                out_sems.at[len(widths) * n + w],
             )
             store.start()
             stores.append(store)
@@ -156,44 +151,54 @@
         store.wait()
 
 
-def assemble(uppers, lowers, widths):
-    count = len(uppers)
-    half, width = uppers[0].shape
+def assemble(pieces, rows, widths, base=()):
+    places = list(pieces)
+    arrays = [pieces[place] for place in places]
     anywhere = pl.BlockSpec(memory_space=pl.ANY)
     return pl.pallas_call(
-        lambda *refs: assemble_kernel(widths, *refs),
-        out_shape=[jax.ShapeDtypeStruct((2 * half * count, w), BF16) for w in widths],
-        in_specs=[pl.BlockSpec(memory_space=pltpu.SMEM)] + [anywhere] * (2 * count),
+        lambda *refs: assemble_kernel(places, widths, *refs),
+        out_shape=[jax.ShapeDtypeStruct((rows, w), BF16) for w in widths],
+        in_specs=[pl.BlockSpec(memory_space=pltpu.SMEM)]
+        + [anywhere] * (len(base) + len(arrays)),
         out_specs=[anywhere] * len(widths),
         scratch_shapes=[
-            pltpu.VMEM((count, 2 * half, width), BF16),
-            pltpu.SemaphoreType.DMA((2 * count,)),
-            pltpu.SemaphoreType.DMA((len(widths) * count,)),
+            pltpu.VMEM((len(arrays),) + arrays[0].shape, BF16),
+            pltpu.SemaphoreType.DMA((len(arrays),)),
+            pltpu.SemaphoreType.DMA((len(widths) * len(arrays),)),
         ],
+        input_output_aliases={1 + n: n for n in range(len(base))},
         name="asm",
-    )(lax.axis_index("seq").astype(jnp.int32)[None], *uppers, *lowers)
-
-
-def gather_plane(upper, lower, widths):
+    )(lax.axis_index("seq").astype(jnp.int32)[None], *base, *arrays)
+
+
+def gather_plane(upper, lower, widths, early=False):
     seqs, cores = lax.axis_size("seq"), lax.axis_size("fsdp")
     bits = [1 << n for n in range(seqs.bit_length() - 1)]
-    gathered = []
-    for piece, order in ((upper, bits), (lower, bits[::-1])):
-        have = {0: piece}
-        for bit in order:
-            have.update({k ^ bit: swap(have[k], "seq", bit) for k in list(have)})
-        gathered.append([have[k] for k in range(seqs)])
-    wholes = assemble(*gathered, widths)
+    have = {(0, 0): upper, (0, 1): lower}
+    wholes, done = (), set()
+    rows = 2 * seqs * upper.shape[0]
+    for phase in range(len(bits)):
+        if early and phase == len(bits) - 1:
+            wholes = assemble(have, rows, widths)
+            done = set(have)
+        for k, m in list(have):
+            bit = bits[phase] if m == 0 else bits[-1 - phase]
+            have[k ^ bit, m] = swap(have[k, m], "seq", bit)
+    rest = {place: piece for place, piece in have.items() if place not in done}
+    wholes = assemble(rest, rows, widths, wholes)
     return [
         [whole] + [swap(whole, "fsdp", j) for j in range(1, cores)] for whole in wholes
     ]
 
 
-def times(rows, weights):
+def times(rows, weights, apart=False):
     depth = weights[0].shape[0]
-    return sum(
-        rows_by(rows[:, j * depth : (j + 1) * depth], weight) for j, weight in enumerate(weights)
-    )
+    total = rows_by(rows[:, :depth], weights[0])
+    if apart:
+        total = lax.optimization_barrier(total)
+    for j, weight in enumerate(weights[1:], 1):
+        total = total + rows_by(rows[:, j * depth : (j + 1) * depth], weight)
+    return total
 
 
 def times_t(rows, weights):
@@ -645,7 +650,7 @@
             (1, me * hidden_width, hidden_width),
         ],
     )
-    weight_gate_up, weight_down = gather_plane(*picked_ff, [2 * hidden_width, hidden_width])
+    weight_gate_up, weight_down = gather_plane(*picked_ff, [2 * hidden_width, hidden_width], True)
 
     steps_along = jnp.arange(half_rows, dtype=jnp.int32)
     positions = (blocks[:, None] * half_rows + steps_along[None, :]).reshape(-1)
@@ -684,7 +689,7 @@
     own_middle, own_second_hat = middle[:tokens], second_hat[:tokens]
     own_second_scale = second_scale[:tokens]
 
-    grad_hidden = times(sequence_grad, weight_down)
+    grad_hidden = times(sequence_grad, weight_down, True)
     gate_values = times(second_normed, weight_gate_up)
     gate = gate_values[:, :hidden_width]
     upward = gate_values[:, hidden_width:]

time: 672 us -> 663 us (0.987)
  waiting for transfers between devices: 309 us -> 280 us
  local copies, waits for them, and re-layouts: 28.2 us -> 37.4 us
  starting transfers between devices: 118 us -> 126 us
    ppermute x71, waiting for transfers between devices: 283 us -> 253 us  [swap(): lax.ppermute(values, axis, [(i, i ^ step) for i in range(lax.axis_size(ax...]
    unnamed x137 -> x135, local copies, waits for them, and re-layouts: 12.6 us -> 16.9 us
    pallas_call x3 -> x4, Pallas kernels: 13.5 us -> 13.7 us  [assemble(): pl.pallas_call(lambda *refs: assemble_kernel(places, widths, *refs), out_...]
  transfers between devices with their start and end apart: 84 -> 84, of which waited for: 32 -> 28; matrix products, arithmetic and copies ran while one was open for 17% -> 19% of each run, Pallas kernels for 10% -> 10%
where the time goes in v4:
time: 663 us; the launch traced here: 655 us
  waiting for transfers between devices  280 us (42%)
  starting transfers between devices  126 us (19%)
  Pallas kernels  86.3 us (13%)
  matrix products  60.1 us (9%)
  other arithmetic  48.7 us (7%)
  local copies, waits for them, and re-layouts  37.4 us (6%)
  between operations  16.4 us (2%)
    ppermute x71, waiting for transfers between devices, swap(): lax.ppermute(values, axis, [(i, i ^ step) for i in range(lax.axis_size(ax...  253 us
    ppermute x71, starting transfers between devices, swap(): lax.ppermute(values, axis, [(i, i ^ step) for i in range(lax.axis_size(ax...  95.9 us
    dot_general x8, matrix products, rows_by_t(): lax.dot_general(left, right, (((1,), (1,)), ((), ())), preferred_element_...  32.2 us
    ppermute x12, starting transfers between devices, exchange(): pieces.append(lax.ppermute(piece, ('ctx', 'fsdp'), pairs))  30.1 us
    dot_general x8, matrix products, rows_by(): return jnp.dot(left, right, preferred_element_type=F32)  27.9 us
    ppermute x12, waiting for transfers between devices, exchange(): pieces.append(lax.ppermute(piece, ('ctx', 'fsdp'), pairs))  27.1 us
    pallas_call x2, Pallas kernels, attention_call(): pl.pallas_call(lambda *refs: kernel(*heads, *refs), out_shape=outs, in_sp...  19.8 us
    pallas_call x3, Pallas kernels, weight_grad(): pl.pallas_call(weight_grad_kernel, grid=(width // tile,), out_shape=[jax....  18.7 us
  transfers between devices with their start and end apart: 84, of which 28 were waited for; matrix products, arithmetic and copies ran while one was open for 19% of the time, Pallas kernels for 10%

profile of v4, /device:TPU:1, one launch (start us, length us, event | category | flops | bytes accessed | tf_op | source)
XLA Modules:
  0.0 655.1 jit_solution(13403752252202303440)
XLA Ops:
  35.4 22.5 %collective-permute-done.7.refs_7_ = bf16[128,1024]{1,0:T(8,128)(2,1)S(1)} collective-permute-done((bf16[128,1024]{1,0:T(8,128)(2,1)S(1)}, bf16[128,1024]{1,0:T(8,128)(2,1)S(1)}, u32[]{:S(2)}, u32[]{:S(2)}) %collective-permute-start.7) | collective-permute-done | bytes 262176 | tf_op jit(solution)/shard_map/ppermute | solution.py:60
  58.5 9.5 %collective-permute-done.8.refs_8_ = bf16[128,1024]{1,0:T(8,128)(2,1)S(1)} collective-permute-done((bf16[128,1024]{1,0:T(8,128)(2,1)S(1)}, bf16[128,1024]{1,0:T(8,128)(2,1)S(1)}, u32[]{:S(2)}, u32[]{:S(2)}) %collective-permute-start.8) | collective-permute-done | bytes 262176 | tf_op jit(solution)/shard_map/ppermute | solution.py:60
  71.2 8.5 %collective-permute-done.18.refs_5_ = bf16[128,2048]{1,0:T(8,128)(2,1)S(1)} collective-permute-done((bf16[128,2048]{1,0:T(8,128)(2,1)}, bf16[128,2048]{1,0:T(8,128)(2,1)S(1)}, u32[]{:S(2)}, u32[]{:S(2)}) %collective-permute-start.18) | collective-permute-done | bytes 524320 | tf_op jit(solution)/shard_map/ppermute | solution.py:60
  84.0 7.0 %collective-permute-done.20.refs_7_ = bf16[128,2048]{1,0:T(8,128)(2,1)} collective-permute-done((bf16[128,2048]{1,0:T(8,128)(2,1)S(1)}, bf16[128,2048]{1,0:T(8,128)(2,1)}, u32[]{:S(2)}, u32[]{:S(2)}) %collective-permute-start.20) | collective-permute-done | bytes 524320 | tf_op jit(solution)/shard_map/ppermute | solution.py:60
  96.2 17.9 %collective-permute-done.21.refs_8_ = bf16[128,2048]{1,0:T(8,128)(2,1)} collective-permute-done((bf16[128,2048]{1,0:T(8,128)(2,1)S(1)}, bf16[128,2048]{1,0:T(8,128)(2,1)}, u32[]{:S(2)}, u32[]{:S(2)}) %collective-permute-start.21) | collective-permute-done | bytes 524320 | tf_op jit(solution)/shard_map/ppermute | solution.py:60
  114.1 19.1 %collective-permute-start.9 = (bf16[1024,1024]{1,0:T(8,128)(2,1)}, bf16[1024,1024]{1,0:T(8,128)(2,1)}, u32[]{:S(2)}, u32[]{:S(2)}) collective-permute-start(bf16[1024,1024]{1,0:T(8,128)(2,1)} %asm.4), channel_id=1, source_target_pairs={{0,1},{1,0},{2,3},{3,2},{4,5},{5,4},{6,7},{7,6},{8,9},{9,8},{10,11... | collective-permute-start | bytes 6291464 | tf_op jit(solution)/shard_map/ppermute | solution.py:60
  165.0 26.4 %collective-permute-done = bf16[128,2048]{1,0:T(8,128)(2,1)S(1)} collective-permute-done((bf16[128,2048]{1,0:T(8,128)(2,1)S(1)}, bf16[128,2048]{1,0:T(8,128)(2,1)S(1)}, u32[]{:S(2)}, u32[]{:S(2)}) %collective-permute-start) | collective-permute-done | bytes 524320 | tf_op jit(solution)/shard_map/ppermute | solution.py:60
  203.6 10.7 %shard_map.186 = (bf16[512,512]{1,0:T(8,128)(2,1)}, f32[512,4]{1,0:T(8,128)}) custom-call(f32[512,1024]{1,0:T(8,128)} %convolution_add_fusion.2.refs_0_, f32[512,128]{1,0:T(8,128)} %get-tuple-element.182.refs_1_, f32[512,128]{1,0:T(8,128)} %get-tuple-element.183.refs_2_, s32[512,1]{1,0:T(8,128)} %add.571.refs_3_, s32[1,512]{1,0:T(1,128)} %add.467.refs_4_, ...), custom_call_target="tpu_custom_call" | custom-call | tf_op jit(solution)/shard_map/pallas_call | solution.py:524
  216.3 9.2 %collective-permute-done.34 = bf16[128,2048]{1,0:T(8,128)(2,1)} collective-permute-done((bf16[128,2048]{1,0:T(8,128)(2,1)S(1)}, bf16[128,2048]{1,0:T(8,128)(2,1)}, u32[]{:S(2)}, u32[]{:S(2)}) %collective-permute-start.34) | collective-permute-done | bytes 524320 | tf_op jit(solution)/shard_map/ppermute | solution.py:60
  228.0 8.8 %collective-permute-done.13.refs_1_ = bf16[512,512]{1,0:T(8,128)(2,1)S(1)} collective-permute-done((bf16[512,512]{1,0:T(8,128)(2,1)}, bf16[512,512]{1,0:T(8,128)(2,1)S(1)}, u32[]{:S(2)}, u32[]{:S(2)}) %collective-permute-start.13) | collective-permute-done | bytes 524320 | tf_op jit(solution)/shard_map/ppermute | solution.py:60
  243.5 20.8 %collective-permute-done.14.refs_2_ = bf16[512,512]{1,0:T(8,128)(2,1)S(1)} collective-permute-done((bf16[512,512]{1,0:T(8,128)(2,1)}, bf16[512,512]{1,0:T(8,128)(2,1)S(1)}, u32[]{:S(2)}, u32[]{:S(2)}) %collective-permute-start.14) | collective-permute-done | bytes 524320 | tf_op jit(solution)/shard_map/ppermute | solution.py:60
  303.8 12.1 %weight_grad.6 = bf16[2048,3072]{1,0:T(8,128)(2,1)} custom-call(s32[1]{0:T(128)} %bitcast.46.refs_0_, bf16[512,2048]{1,0:T(8,128)(2,1)} %copy-done.4, bf16[512,3072]{1,0:T(8,128)(2,1)} %pad_maximum_fusion.refs_2_), custom_call_target="tpu_custom_call" | custom-call | tf_op jit(solution)/shard_map/weight_grad/pallas_call | solution.py:579
  322.0 6.6 %fusion.46 = f32[512,1024]{1,0:T(8,128)S(1)} fusion(bf16[1024,3072]{1,0:T(8,128)(2,1)} %collective-permute-done.29, bf16[512,1536]{1,0:T(8,128)(2,1)S(1)} %copy-done.15, bf16[512,1536]{1,0:T(8,128)(2,1)S(1)} %get-tuple-element.84), kind=kOutput, calls=%fused_computation.207 | convolution fusion | flops 3227516928 | bytes 11534336 | tf_op jit(solution)/shard_map/dot_general | solution.py:52
  332.3 11.5 %collective-permute-start.40 = (bf16[128,1024]{1,0:T(8,128)(2,1)}, bf16[128,1024]{1,0:T(8,128)(2,1)}, u32[]{:S(2)}, u32[]{:S(2)}) collective-permute-start(bf16[128,1024]{1,0:T(8,128)(2,1)} %get-tuple-element.117), channel_id=1, source_target_pairs={{0,2},{2,0},{4,6},{6,4},{1,3},{3,1},{5,7},{7,5},{8,10},{10,8},{12,... | collective-permute-start | bytes 786440 | tf_op jit(solution)/shard_map/ppermute | solution.py:60
  349.6 7.7 %weight_grad.7 = (bf16[1024,1536]{1,0:T(8,128)(2,1)}, bf16[1024,1536]{1,0:T(8,128)(2,1)}) custom-call(bf16[512,2048]{1,0:T(8,128)(2,1)} %constant_dynamic-update-slice_fusion.left, bf16[512,1536]{1,0:T(8,128)(2,1)} %copy-done.13), custom_call_target="tpu_custom_call" | custom-call | tf_op jit(solution)/shard_map/weight_grad/pallas_call | solution.py:548
  366.4 22.5 %collective-permute-done.38 = bf16[128,1024]{1,0:T(8,128)(2,1)S(1)} collective-permute-done((bf16[128,1024]{1,0:T(8,128)(2,1)S(1)}, bf16[128,1024]{1,0:T(8,128)(2,1)S(1)}, u32[]{:S(2)}, u32[]{:S(2)}) %collective-permute-start.38) | collective-permute-done | bytes 262176 | tf_op jit(solution)/shard_map/ppermute | solution.py:60
  388.9 12.6 %collective-permute-done.37 = bf16[128,1024]{1,0:T(8,128)(2,1)S(1)} collective-permute-done((bf16[128,1024]{1,0:T(8,128)(2,1)S(1)}, bf16[128,1024]{1,0:T(8,128)(2,1)S(1)}, u32[]{:S(2)}, u32[]{:S(2)}) %collective-permute-start.37) | collective-permute-done | bytes 262176 | tf_op jit(solution)/shard_map/ppermute | solution.py:60
  419.7 9.1 %shard_map.187 = (bf16[512,1024]{1,0:T(8,128)(2,1)}, f32[2,128]{1,0:T(2,128)}) custom-call(f32[512,1024]{1,0:T(8,128)} %convolution_add_fusion.2.refs_0_, f32[512,128]{1,0:T(8,128)} %get-tuple-element.182.refs_1_, f32[512,128]{1,0:T(8,128)} %get-tuple-element.183.refs_2_, s32[512,1]{1,0:T(8,128)} %add.571.refs_3_, s32[1,512]{1,0:T(1,128)} %add.467.refs_4_, ...), custom_call_target="tpu_custom_call" | custom-call | tf_op jit(solution)/shard_map/pallas_call | solution.py:524
  476.1 22.5 %collective-permute-done.45 = bf16[256,2048]{1,0:T(8,128)(2,1)S(1)} collective-permute-done((bf16[256,2048]{1,0:T(8,128)(2,1)}, bf16[256,2048]{1,0:T(8,128)(2,1)S(1)}, u32[]{:S(2)}, u32[]{:S(2)}) %collective-permute-start.45) | collective-permute-done | bytes 1048608 | tf_op jit(solution)/shard_map/ppermute | solution.py:60
  530.5 10.9 %collective-permute-done.46 = bf16[128,2048]{1,0:T(8,128)(2,1)} collective-permute-done((bf16[128,2048]{1,0:T(8,128)(2,1)}, bf16[128,2048]{1,0:T(8,128)(2,1)}, u32[]{:S(2)}, u32[]{:S(2)}) %collective-permute-start.46) | collective-permute-done | bytes 524320 | tf_op jit(solution)/shard_map/ppermute | solution.py:60
  545.1 7.5 %collective-permute-done.77 = bf16[256,1536]{1,0:T(8,128)(2,1)S(1)} collective-permute-done((bf16[256,1536]{1,0:T(8,128)(2,1)S(1)}, bf16[256,1536]{1,0:T(8,128)(2,1)S(1)}, u32[]{:S(2)}, u32[]{:S(2)}) %collective-permute-start.77) | collective-permute-done | bytes 786464 | tf_op jit(solution)/shard_map/ppermute | solution.py:60
  559.7 9.7 %collective-permute-start.59 = (bf16[64,1024]{1,0:T(8,128)(2,1)S(1)}, bf16[64,1024]{1,0:T(8,128)(2,1)}, u32[]{:S(2)}, u32[]{:S(2)}) collective-permute-start(bf16[64,1024]{1,0:T(8,128)(2,1)S(1)} %get-tuple-element.139), channel_id=1, source_target_pairs={{0,0},{1,4},{2,1},{3,5},{4,2},{5,6},{6,3},{7,7},{8,8},{9,12},{10,9... | collective-permute-start | bytes 393224 | tf_op jit(solution)/shard_map/ppermute | solution.py:358
  575.2 9.5 %collective-permute-done.78 = bf16[128,1536]{1,0:T(8,128)(2,1)S(1)} collective-permute-done((bf16[128,1536]{1,0:T(8,128)(2,1)S(1)}, bf16[128,1536]{1,0:T(8,128)(2,1)S(1)}, u32[]{:S(2)}, u32[]{:S(2)}) %collective-permute-start.78) | collective-permute-done | bytes 393248 | tf_op jit(solution)/shard_map/ppermute | solution.py:60
  613.6 27.0 %collective-permute-done.82.refs_4_ = bf16[64,1536]{1,0:T(8,128)(2,1)S(1)} collective-permute-done((bf16[64,1536]{1,0:T(8,128)(2,1)}, bf16[64,1536]{1,0:T(8,128)(2,1)S(1)}, u32[]{:S(2)}, u32[]{:S(2)}) %collective-permute-start.82) | collective-permute-done | bytes 196640 | tf_op jit(solution)/shard_map/ppermute | solution.py:358
  (434 shorter events, 309.1 us)
Async XLA Ops:
  7.2 583.7 %reduce-scatter.2.cloned.1.call-start = ((), (), s32[]{:S(2)}) async-start(), calls=%async_computation.1 | async-start | bytes 14155776 | tf_op jit(solution)/shard_map/reduce_scatter | solution.py:345
  27.5 54.2 %collective-permute-start.23 = (bf16[128,4608]{1,0:T(8,128)(2,1)}, bf16[128,4608]{1,0:T(8,128)(2,1)}, u32[]{:S(2)}, u32[]{:S(2)}) collective-permute-start(bf16[128,4608]{1,0:T(8,128)(2,1)} %get-tuple-element.41.refs_1_), channel_id=1, source_target_pairs={{0,8},{8,0},{16,24},{24,16},{1,9},{9,1},{17,25},{25,17},{2,10},{10... | collective-permute-start | bytes 3538952 | tf_op jit(solution)/shard_map/ppermute | solution.py:60
  28.7 63.5 %collective-permute-start.24 = (bf16[128,4608]{1,0:T(8,128)(2,1)}, bf16[128,4608]{1,0:T(8,128)(2,1)}, u32[]{:S(2)}, u32[]{:S(2)}) collective-permute-start(bf16[128,4608]{1,0:T(8,128)(2,1)} %get-tuple-element.42.refs_2_), channel_id=1, source_target_pairs={{0,16},{8,24},{16,0},{24,8},{1,17},{9,25},{17,1},{25,9},{2,18},{10... | collective-permute-start | bytes 3538952 | tf_op jit(solution)/shard_map/ppermute | solution.py:60
  34.1 36.4 %collective-permute-start.17 = (bf16[128,2048]{1,0:T(8,128)(2,1)}, bf16[128,2048]{1,0:T(8,128)(2,1)S(1)}, u32[]{:S(2)}, u32[]{:S(2)}) collective-permute-start(bf16[128,2048]{1,0:T(8,128)(2,1)} %get-tuple-element.40.refs_2_), channel_id=1, source_target_pairs={{0,16},{8,24},{16,0},{24,8},{1,17},{9,25},{17,1},{25,9},{2,18},{10... | collective-permute-start | bytes 1572872 | tf_op jit(solution)/shard_map/ppermute | solution.py:60
  79.7 54.3 %collective-permute-start.25 = (bf16[128,4608]{1,0:T(8,128)(2,1)}, bf16[128,4608]{1,0:T(8,128)(2,1)}, u32[]{:S(2)}, u32[]{:S(2)}) collective-permute-start(bf16[128,4608]{1,0:T(8,128)(2,1)} %get-tuple-element.41.refs_1_), channel_id=1, source_target_pairs={{0,16},{8,24},{16,0},{24,8},{1,17},{9,25},{17,1},{25,9},{2,18},{10... | collective-permute-start | bytes 3538952 | tf_op jit(solution)/shard_map/ppermute | solution.py:60
  80.4 55.6 %collective-permute-start.26 = (bf16[128,4608]{1,0:T(8,128)(2,1)}, bf16[128,4608]{1,0:T(8,128)(2,1)}, u32[]{:S(2)}, u32[]{:S(2)}) collective-permute-start(bf16[128,4608]{1,0:T(8,128)(2,1)} %get-tuple-element.42.refs_2_), channel_id=1, source_target_pairs={{0,8},{8,0},{16,24},{24,16},{1,9},{9,1},{17,25},{25,17},{2,10},{10... | collective-permute-start | bytes 3538952 | tf_op jit(solution)/shard_map/ppermute | solution.py:60
  81.7 59.9 %collective-permute-start.27 = (bf16[128,4608]{1,0:T(8,128)(2,1)}, bf16[128,4608]{1,0:T(8,128)(2,1)}, u32[]{:S(2)}, u32[]{:S(2)}) collective-permute-start(bf16[128,4608]{1,0:T(8,128)(2,1)} %collective-permute-done.23.refs_3_), channel_id=1, source_target_pairs={{0,16},{8,24},{16,0},{24,8},{1,17},{9,25},{17,1},{25,9},{2,18},{10... | collective-permute-start | bytes 3538952 | tf_op jit(solution)/shard_map/ppermute | solution.py:60
  92.3 53.9 %collective-permute-start.28 = (bf16[128,4608]{1,0:T(8,128)(2,1)}, bf16[128,4608]{1,0:T(8,128)(2,1)}, u32[]{:S(2)}, u32[]{:S(2)}) collective-permute-start(bf16[128,4608]{1,0:T(8,128)(2,1)} %collective-permute-done.24.refs_4_), channel_id=1, source_target_pairs={{0,8},{8,0},{16,24},{24,16},{1,9},{9,1},{17,25},{25,17},{2,10},{10... | collective-permute-start | bytes 3538952 | tf_op jit(solution)/shard_map/ppermute | solution.py:60
  114.1 82.5 %collective-permute-start.9 = (bf16[1024,1024]{1,0:T(8,128)(2,1)}, bf16[1024,1024]{1,0:T(8,128)(2,1)}, u32[]{:S(2)}, u32[]{:S(2)}) collective-permute-start(bf16[1024,1024]{1,0:T(8,128)(2,1)} %asm.4), channel_id=1, source_target_pairs={{0,1},{1,0},{2,3},{3,2},{4,5},{5,4},{6,7},{7,6},{8,9},{9,8},{10,11... | collective-permute-start | bytes 6291464 | tf_op jit(solution)/shard_map/ppermute | solution.py:60
  141.6 49.7 %collective-permute-start = (bf16[128,2048]{1,0:T(8,128)(2,1)S(1)}, bf16[128,2048]{1,0:T(8,128)(2,1)S(1)}, u32[]{:S(2)}, u32[]{:S(2)}) collective-permute-start(bf16[128,2048]{1,0:T(8,128)(2,1)S(1)} %bitcast.117), channel_id=1, source_target_pairs={{0,4},{2,6},{4,0},{6,2},{1,5},{3,7},{5,1},{7,3},{8,12},{10,14},{12... | collective-permute-start | bytes 1572872 | tf_op jit(solution)/shard_map/ppermute | solution.py:60
  146.2 128.1 %collective-permute-start.22 = (bf16[1024,2048]{1,0:T(8,128)(2,1)}, bf16[1024,2048]{1,0:T(8,128)(2,1)}, u32[]{:S(2)}, u32[]{:S(2)}) collective-permute-start(bf16[1024,2048]{1,0:T(8,128)(2,1)} %asm.5), channel_id=1, source_target_pairs={{0,1},{1,0},{2,3},{3,2},{4,5},{5,4},{6,7},{7,6},{8,9},{9,8},{10,11... | collective-permute-start | bytes 12582920 | tf_op jit(solution)/shard_map/ppermute | solution.py:60
  160.0 129.6 %collective-permute-start.29 = (bf16[1024,3072]{1,0:T(8,128)(2,1)}, bf16[1024,3072]{1,0:T(8,128)(2,1)}, u32[]{:S(2)}, u32[]{:S(2)}) collective-permute-start(bf16[1024,3072]{1,0:T(8,128)(2,1)} %get-tuple-element.45), channel_id=1, source_target_pairs={{0,1},{1,0},{2,3},{3,2},{4,5},{5,4},{6,7},{7,6},{8,9},{9,8},{10,11... | collective-permute-start | bytes 18874376 | tf_op jit(solution)/shard_map/ppermute | solution.py:60
  164.1 50.2 %collective-permute-start.33 = (bf16[128,2048]{1,0:T(8,128)(2,1)S(1)}, bf16[128,2048]{1,0:T(8,128)(2,1)S(1)}, u32[]{:S(2)}, u32[]{:S(2)}) collective-permute-start(bf16[128,2048]{1,0:T(8,128)(2,1)S(1)} %bitcast.126), channel_id=1, source_target_pairs={{0,4},{2,6},{4,0},{6,2},{1,5},{3,7},{5,1},{7,3},{8,12},{10,14},{12... | collective-permute-start | bytes 1572872 | tf_op jit(solution)/shard_map/ppermute | solution.py:60
  227.4 57.7 %collective-permute-start.30 = (bf16[1024,1536]{1,0:T(8,128)(2,1)}, bf16[1024,1536]{1,0:T(8,128)(2,1)}, u32[]{:S(2)}, u32[]{:S(2)}) collective-permute-start(bf16[1024,1536]{1,0:T(8,128)(2,1)} %get-tuple-element.46), channel_id=1, source_target_pairs={{0,1},{1,0},{2,3},{3,2},{4,5},{5,4},{6,7},{7,6},{8,9},{9,8},{10,11... | collective-permute-start | bytes 9437192 | tf_op jit(solution)/shard_map/ppermute | solution.py:60
  228.0 36.4 %collective-permute-start.14 = (bf16[512,512]{1,0:T(8,128)(2,1)}, bf16[512,512]{1,0:T(8,128)(2,1)S(1)}, u32[]{:S(2)}, u32[]{:S(2)}) collective-permute-start(bf16[512,512]{1,0:T(8,128)(2,1)} %get-tuple-element.38.refs_0_.refs_8_), channel_id=1, source_target_pairs={{0,4},{2,6},{4,0},{6,2},{1,5},{3,7},{5,1},{7,3},{8,12},{10,14},{12... | collective-permute-start | bytes 1572872 | tf_op jit(solution)/shard_map/ppermute | solution.py:60
  357.4 116.2 %collective-permute-start.31 = (bf16[256,2048]{1,0:T(8,128)(2,1)}, bf16[256,2048]{1,0:T(8,128)(2,1)}, u32[]{:S(2)}, u32[]{:S(2)}) collective-permute-start(bf16[256,2048]{1,0:T(8,128)(2,1)} %pad_maximum_fusion.2), channel_id=1, source_target_pairs={{0,2},{2,0},{4,6},{6,4},{1,3},{3,1},{5,7},{7,5},{8,10},{10,8},{12,... | collective-permute-start | bytes 3145736 | tf_op jit(solution)/shard_map/ppermute | solution.py:60
  361.3 40.1 %collective-permute-start.37 = (bf16[128,1024]{1,0:T(8,128)(2,1)S(1)}, bf16[128,1024]{1,0:T(8,128)(2,1)S(1)}, u32[]{:S(2)}, u32[]{:S(2)}) collective-permute-start(bf16[128,1024]{1,0:T(8,128)(2,1)S(1)} %get-tuple-element.114), channel_id=1, source_target_pairs={{0,2},{2,0},{4,6},{6,4},{1,3},{3,1},{5,7},{7,5},{8,10},{10,8},{12,... | collective-permute-start | bytes 786440 | tf_op jit(solution)/shard_map/ppermute | solution.py:60
  361.3 40.1 %collective-permute-start.36 = (bf16[128,1024]{1,0:T(8,128)(2,1)S(1)}, bf16[128,1024]{1,0:T(8,128)(2,1)S(1)}, u32[]{:S(2)}, u32[]{:S(2)}) collective-permute-start(bf16[128,1024]{1,0:T(8,128)(2,1)S(1)} %get-tuple-element.112), channel_id=1, source_target_pairs={{0,4},{2,6},{4,0},{6,2},{1,5},{3,7},{5,1},{7,3},{8,12},{10,14},{12... | collective-permute-start | bytes 786440 | tf_op jit(solution)/shard_map/ppermute | solution.py:60
  362.7 162.0 %collective-permute-start.74 = (bf16[1024,1536]{1,0:T(8,128)(2,1)}, bf16[1024,1536]{1,0:T(8,128)(2,1)}, u32[]{:S(2)}, u32[]{:S(2)}) collective-permute-start(bf16[1024,1536]{1,0:T(8,128)(2,1)} %get-tuple-element.57), channel_id=1, source_target_pairs={{0,1},{1,0},{2,3},{3,2},{4,5},{5,4},{6,7},{7,6},{8,9},{9,8},{10,11... | collective-permute-start | bytes 9437192 | tf_op jit(solution)/shard_map/ppermute | solution.py:60
  464.3 56.7 %collective-permute-start.54 = (bf16[1024,1024]{1,0:T(8,128)(2,1)}, bf16[1024,1024]{1,0:T(8,128)(2,1)}, u32[]{:S(2)}, u32[]{:S(2)}) collective-permute-start(bf16[1024,1024]{1,0:T(8,128)(2,1)} %get-tuple-element.51), channel_id=1, source_target_pairs={{0,1},{1,0},{2,3},{3,2},{4,5},{5,4},{6,7},{7,6},{8,9},{9,8},{10,11... | collective-permute-start | bytes 6291464 | tf_op jit(solution)/shard_map/ppermute | solution.py:60
  595.9 47.9 %collective-permute-start.70 = (bf16[64,3072]{1,0:T(8,128)(2,1)}, bf16[64,3072]{1,0:T(8,128)(2,1)S(1)}, u32[]{:S(2)}, u32[]{:S(2)}) collective-permute-start(bf16[64,3072]{1,0:T(8,128)(2,1)} %get-tuple-element.108), channel_id=1, source_target_pairs={{0,0},{1,4},{2,1},{3,5},{4,2},{5,6},{6,3},{7,7},{8,8},{9,12},{10,9... | collective-permute-start | bytes 1179656 | tf_op jit(solution)/shard_map/ppermute | solution.py:358
  597.8 46.0 %collective-permute-start.71 = (bf16[64,3072]{1,0:T(8,128)(2,1)}, bf16[64,3072]{1,0:T(8,128)(2,1)}, u32[]{:S(2)}, u32[]{:S(2)}) collective-permute-start(bf16[64,3072]{1,0:T(8,128)(2,1)} %get-tuple-element.107), channel_id=1, source_target_pairs={{0,1},{1,5},{2,0},{3,4},{4,3},{5,7},{6,2},{7,6},{8,9},{9,13},{10,8... | collective-permute-start | bytes 1179656 | tf_op jit(solution)/shard_map/ppermute | solution.py:358
  600.3 43.5 %collective-permute-start.72 = (bf16[64,3072]{1,0:T(8,128)(2,1)}, bf16[64,3072]{1,0:T(8,128)(2,1)}, u32[]{:S(2)}, u32[]{:S(2)}) collective-permute-start(bf16[64,3072]{1,0:T(8,128)(2,1)} %get-tuple-element.106), channel_id=1, source_target_pairs={{0,2},{1,6},{2,3},{3,7},{4,0},{5,4},{6,1},{7,5},{8,10},{9,14},{10,... | collective-permute-start | bytes 1179656 | tf_op jit(solution)/shard_map/ppermute | solution.py:358
  602.0 41.8 %collective-permute-start.73 = (bf16[64,3072]{1,0:T(8,128)(2,1)}, bf16[64,3072]{1,0:T(8,128)(2,1)}, u32[]{:S(2)}, u32[]{:S(2)}) collective-permute-start(bf16[64,3072]{1,0:T(8,128)(2,1)} %get-tuple-element.105), channel_id=1, source_target_pairs={{0,3},{1,7},{2,2},{3,6},{4,1},{5,5},{6,0},{7,4},{8,11},{9,15},{10,... | collective-permute-start | bytes 1179656 | tf_op jit(solution)/shard_map/ppermute | solution.py:358
  (126 other events, 2147.0 us)
Sparse Core Ops, SparseCore 0:
  316.1 99.4 reduce-scatter.1
